TPU v7x, 512 devices: a whole 4x8x8 slice. The times are simulated.
512 devices in a mesh: dp: 4 (over x), shard: 128 (over z, y, core).
Axes of the slice: x: 4, y: 8, z: 8, core: 2. Of those that a mesh axis runs over, the one named last changes fastest.
Arguments:
- stats_partial: float32 [4, 128, 2, 512, 512], P('dp', None, None, 'shard'), may hold values from -800 to 800, as said below
- gradient: bfloat16 [128, 512, 512], P(None, 'shard'), may hold values from -240 to 240
- owner_of: int32 [128], replicated, may hold values from 0 to 127, as said below
- layer_count: int32 [4], replicated, may hold values from 1 to 64, 128 in all
Outputs:
- preconditioned: bfloat16 [128, 2, 512, 512], P('shard', None, 'dp')
Inputs may be any that keep to these rules, and one draw needn't show every extreme that they name: `owner_of`: each owner holds 0 to 2 blocks, and in every draw some owner holds exactly 2. `layer_count`: the counts sum to 128. `stats_partial`: each [512, 512] slice is symmetric positive definite.
All inputs are finite; a program needn't handle non-finite values.
Results may differ from a plain program's by a relative error of at most 0.0062.
The roundings to bfloat16 on the way count: a program that leaves them out, or rounds other values in their place, can miss the bound.
Values may be sent and summed in bfloat16 or wider, within the bound.
No kernel may reach another device: no remote copies, remote signals or barrier semaphores. Data moves between devices by JAX's collectives and lax.ppermute only.
A program may use at most 64 MiB of HBM per device.

v0:
```python
import functools

import jax
import jax.numpy as jnp
from jax import lax
from jax.sharding import Mesh
from jax.sharding import PartitionSpec as P

B = 512
ITERS = 3
OCAP = 2
LAYERS = 4
SHARD = ("shard_0", "shard_1", "shard_2")
DP_SHARD = ("dp", "shard_0", "shard_1", "shard_2")


highest = lax.Precision.HIGHEST


def in_blocks(x, dim, peers):
    before, after = (x.shape[:dim], x.shape[dim + 1 :])
    return jnp.moveaxis(x.reshape(*before, peers, -1, *after), dim, 0)


def sent_and_summed(x, axis, dim):
    peers = lax.axis_size(axis)
    tiles = lax.all_to_all(in_blocks(x, dim, peers), axis, 0, 0, tiled=True)
    return jnp.sum(tiles, axis=0)


def copy_for_each(x, axis):
    peers = lax.axis_size(axis)
    return lax.all_to_all(jnp.broadcast_to(x[None], (peers, *x.shape)), axis, 0, 0, tiled=True)


def joined_along(tiles, dim):
    shape = list(tiles.shape[1:])
    shape[dim] *= tiles.shape[0]
    return jnp.moveaxis(tiles, 0, dim).reshape(shape)


def gather_directly(x, axis, dim):
    tiles = copy_for_each(x, axis)
    return joined_along(tiles, dim)


def over_axes(x, axes):
    return functools.reduce(lax.psum, axes, x)


def product(left_side, right_side):
    return jnp.dot(left_side, right_side, precision=highest, preferred_element_type=jnp.float32)


def inverse_root(statistic):
    identity = jnp.eye(B, dtype=jnp.float32)
    magnitude = B * jnp.sqrt(jnp.mean(statistic * statistic) + 1e-06)
    matrix = statistic / magnitude
    factor = identity * magnitude ** (-0.25)
    for number in range(ITERS):
        update = (5.0 * identity - matrix) * 0.25
        factor = product(factor, update)
        if number + 1 < ITERS:
            square = product(update, update)
            fourth = product(square, square)
            matrix = product(fourth, matrix)
    return factor.astype(jnp.bfloat16)


def precondition(left_all, right_all, grad_full, member, quarter):
    left_rows = lax.dynamic_slice_in_dim(left_all, member * quarter, quarter, 1)
    middle = jnp.einsum(
        "kqb,kbc->kqc", left_rows, grad_full, preferred_element_type=jnp.float32
    ).astype(jnp.bfloat16)
    result = jnp.einsum("kqc,kcd->kqd", middle, right_all, preferred_element_type=jnp.float32)
    grad_rows = lax.dynamic_slice_in_dim(grad_full, member * quarter, quarter, 1).astype(
        jnp.float32
    )
    return (
        result,
        jnp.sum(grad_rows * grad_rows, axis=(1, 2)),
        jnp.sum(result * result, axis=(1, 2)),
    )


def on_device(stats_partial, gradient, owner_of, layer_count):
    shards = lax.axis_size(SHARD)
    groups = lax.axis_size("dp")
    my_shard = lax.axis_index(SHARD)
    member = lax.axis_index("dp")
    blocks = owner_of.shape[0]
    quarter = B // groups
    block_ids = jnp.arange(blocks, dtype=jnp.int32)
    same_owner = (owner_of[:, None] == owner_of[None, :]) & (
        block_ids[None, :] < block_ids[:, None]
    )
    earlier = jnp.sum(same_owner.astype(jnp.int32), axis=1)
    target = owner_of * OCAP + earlier
    places = jnp.arange(shards * OCAP, dtype=jnp.int32)
    matches = target[:, None] == places[None, :]
    filled = jnp.any(matches, axis=0)
    chosen = jnp.sum(jnp.where(matches, block_ids[:, None], 0), axis=0)
    all_places = (
        jnp.arange(OCAP, dtype=jnp.int32)[:, None]
        + OCAP * jnp.arange(shards, dtype=jnp.int32)[None, :]
    )
    grad_pick = jnp.take(chosen, all_places)
    grad_live = jnp.take(filled, all_places)
    layer_ends = jnp.cumsum(layer_count)
    layer_of = jnp.sum((block_ids[:, None] >= layer_ends[None, :]).astype(jnp.int32), axis=1)
    local = stats_partial[0]
    local_rows = local.shape[2]
    slot_index = member // 2
    members = jnp.arange(groups, dtype=jnp.int32)
    place_all = jnp.arange(shards, dtype=jnp.int32)[None, :] * OCAP + (members // 2)[:, None]
    pick_all = jnp.take(chosen, place_all)
    live_all = jnp.take(filled, place_all)
    flat_local = local.reshape(blocks * 2, local_rows, B)
    laid = jnp.where(
        live_all[:, :, None, None],
        jnp.take(flat_local, pick_all * 2 + (members % 2)[:, None], axis=0),
        0.0,
    )
    outgoing = sent_and_summed(laid, "dp", 0)[0]
    incoming = lax.all_to_all(outgoing, SHARD, split_axis=0, concat_axis=0, tiled=True)
    statistic = incoming.reshape(B, B)
    my_blocks = jnp.take(chosen, my_shard * OCAP + jnp.arange(OCAP, dtype=jnp.int32))
    mine_live = jnp.take(filled, my_shard * OCAP + slot_index)
    statistic = jnp.where(mine_live, statistic, jnp.eye(B, dtype=jnp.float32))
    factor = inverse_root(statistic)
    factors = gather_directly(factor[None], "dp", 0).reshape(OCAP, 2, B, B)
    grad_send = jnp.where(
        grad_live[:, :, None, None],
        jnp.take(gradient, grad_pick, axis=0),
        jnp.zeros((), jnp.bfloat16),
    )
    grad_full = lax.all_to_all(grad_send, SHARD, split_axis=1, concat_axis=1, tiled=True).reshape(
        OCAP, B, B
    )
    result, grad_terms, result_terms = precondition(
        factors[:, 0], factors[:, 1], grad_full, member, quarter
    )
    layer_hot = (
        jnp.take(layer_of, my_blocks)[:, None] == jnp.arange(LAYERS, dtype=jnp.int32)[None, :]
    ).astype(jnp.float32)
    grad_total, result_total = (
        over_axes(jnp.sum(layer_hot * grad_terms[:, None], axis=0), DP_SHARD),
        over_axes(jnp.sum(layer_hot * result_terms[:, None], axis=0), DP_SHARD),
    )
    graft_ratio = jnp.sqrt((grad_total + 1e-06) / (result_total + 1e-06))
    scaled = (result * jnp.sum(layer_hot * graft_ratio[None, :], axis=1)[:, None, None]).astype(
        jnp.bfloat16
    )
    return scaled[None]


def solution(mesh):
    torus = Mesh(
        mesh.devices.reshape(mesh.shape["dp"], 8, 8, 2), ("dp", "shard_0", "shard_1", "shard_2")
    )
    placed = (P("dp", None, None, SHARD, None), P(None, SHARD, None), P(), P())
    return jax.shard_map(
        on_device,
        mesh=torus,
        in_specs=placed,
        out_specs=P(SHARD, None, "dp", None),
        check_vma=False,
    )
```

profile of v0, /device:TPU:1, one launch (start us, length us, event | category | flops | bytes accessed | tf_op | source)
XLA Modules:
  0.0 246.9 jit_solution(17074807883259065991)
XLA Ops:
  2.0 3.5 %gather_fusion.1 = s32[512]{0:T(512)S(1)} fusion(s32[256]{0:T(256)S(1)} %select_reduce_fusion, s32[1024]{0:T(1024)S(1)} %pad_clamp_fusion.5), kind=kCustom, calls=%fused_computation.1 | custom fusion | bytes 6144 | tf_op jit(solution)/shard_map/jit(_take)/gather | solution.py:116
  5.6 3.4 %gather_fusion = pred[512]{0:T(512)(128)(4,1)S(1)} fusion(pred[256]{0:T(512)(128)(4,1)S(1)} %fusion.28, s32[1024]{0:T(1024)S(1)} %pad_clamp_fusion.5), kind=kCustom, calls=%fused_computation | custom fusion | bytes 3072 | tf_op jit(solution)/shard_map/jit(_take)/gather | solution.py:117
  9.0 4.6 %gather_fusion.2 = f32[512,4,512]{2,1,0:T(4,128)} fusion(f32[256,4,512]{2,1,0:T(4,128)S(1)} %bitcast.82, s32[1024]{0:T(1024)S(1)} %pad_clamp_fusion.4), kind=kCustom, calls=%fused_computation.2 | custom fusion | bytes 8390656 | tf_op jit(solution)/shard_map/jit(_take)/gather | solution.py:121
  13.6 4.5 %select_select_fusion = f32[4,1,128,4,512]{4,3,2,1,0:T(4,128)S(1)} fusion(f32[4,1,128,4,512]{4,3,2,1,0:T(4,128)} %bitcast.83, pred[4,128]{1,0:T(4,128)(4,1)S(1)} %get-tuple-element.27, pred[4,128]{1,0:T(4,128)(4,1)S(1)} %get-tuple-element.26), kind=kLoop, calls=%fused_computation.8 | loop fusion | flops 2097152 | bytes 8389632 | tf_op jit(solution)/shard_map/jit(_where)/select_n | solution.py:119
  18.1 47.8 %all_to_all.20 = f32[4,1,128,4,512]{4,3,2,1,0:T(4,128)} all-to-all(f32[4,1,128,4,512]{4,3,2,1,0:T(4,128)S(1)} %select_select_fusion), channel_id=1, replica_groups=mesh['dp'=4,'shard_0'=8,'shard_1'=8,'shard_2'=2] {'dp'}, dimensions={0} | all-to-all | bytes 8388608 | tf_op jit(solution)/shard_map/all_to_all | solution.py:27
  66.0 4.2 %reduce_sum.92 = f32[128,4,512]{2,1,0:T(4,128)} reduce(f32[4,1,128,4,512]{4,3,2,1,0:T(4,128)} %all_to_all.20, f32[]{:T(128)} %constant.200.clone.1), dimensions={0,1}, to_apply=%region_3.4 | reduce | flops 786432 | bytes 5242884 | tf_op jit(solution)/shard_map/reduce_sum | solution.py:28
  70.2 23.6 %all-to-all-start.1 = ((f32[128,4,512]{2,1,0:T(4,128)}), f32[128,4,512]{2,1,0:T(4,128)S(1)}, u32[]{:S(2)}, u32[]{:S(2)}) async-start(f32[128,4,512]{2,1,0:T(4,128)} %reduce_sum.92), calls=%async_computation.1 | async-start | bytes 2097152 | tf_op jit(solution)/shard_map/all_to_all | solution.py:125
  98.4 3.5 %gather_fusion.5 = bf16[256,4,512]{2,1,0:T(4,128)(2,1)} fusion(bf16[128,4,512]{2,1,0:T(4,128)(2,1)} %param.5, s32[1024]{0:T(1024)S(1)} %pad_clamp_fusion.2), kind=kCustom, calls=%fused_computation.5 | custom fusion | bytes 2098176 | tf_op jit(solution)/shard_map/jit(_take)/gather | solution.py:134
  106.0 18.7 %all-to-all-done.1 = f32[128,4,512]{2,1,0:T(4,128)S(1)} async-done(((f32[128,4,512]{2,1,0:T(4,128)}), f32[128,4,512]{2,1,0:T(4,128)S(1)}, u32[]{:S(2)}, u32[]{:S(2)}) %all-to-all-start.1) | async-done | bytes 1048608 | tf_op jit(solution)/shard_map/all_to_all | solution.py:125
  124.7 7.1 %all-to-all-start.3 = ((bf16[2,128,4,512]{3,2,0,1:T(4,128)(2,1)}), bf16[2,128,4,512]{3,2,0,1:T(4,128)(2,1)}, u32[]{:S(2)}, u32[]{:S(2)}) async-start(bf16[2,128,4,512]{3,2,0,1:T(4,128)(2,1)} %copy.16), calls=%async_computation.3 | async-start | bytes 2097152 | tf_op jit(solution)/shard_map/all_to_all | solution.py:137
  135.7 2.6 %mul.157 = f32[512,512]{1,0:T(8,128)} reshape(f32[128,4,512]{2,1,0:T(4,128)} %fusion.7) | data formatting | bytes 2097152 | tf_op jit(solution)/shard_map/mul | solution.py:61
  138.3 3.4 %fusion.60 = f32[512,512]{1,0:T(8,128)S(1)} fusion(f32[512,512]{1,0:T(8,128)} %mul.157), kind=kOutput, calls=%fused_computation.126 | convolution fusion | flops 1610612736 | bytes 2097152 | tf_op jit(solution)/shard_map/dot_general | solution.py:52
  141.7 2.8 %fusion.61 = f32[512,512]{1,0:T(8,128)} fusion(f32[512,512]{1,0:T(8,128)S(1)} %fusion.60), kind=kOutput, calls=%fused_computation.127 | convolution fusion | flops 1610612736 | bytes 2097152 | tf_op jit(solution)/shard_map/dot_general | solution.py:52
  145.9 3.5 %fusion.22 = f32[512,512]{1,0:T(8,128)S(1)} fusion(f32[512,512]{1,0:T(8,128)} %fusion.61, f32[512,512]{1,0:T(8,128)} %reshape.507, f32[]{:T(128)S(6)} %mul_shard_map.3, pred[]{:T(512)} %bitcast.1), kind=kOutput, calls=%fused_computation.44 | convolution fusion | flops 1611661312 | bytes 3145733 | tf_op jit(solution)/shard_map/dot_general | solution.py:52
  153.4 2.1 fusion.10
  163.7 4.4 %all-to-all-start.2 = ((bf16[4,1,512,512]{3,2,1,0:T(8,128)(2,1)}), bf16[4,1,512,512]{3,2,1,0:T(8,128)(2,1)}, u32[]{:S(2)}, u32[]{:S(2)}) async-start(bf16[4,1,512,512]{3,2,1,0:T(8,128)(2,1)} %broadcast_in_dim.132), calls=%async_computation.2 | async-start | bytes 4194304 | tf_op jit(solution)/shard_map/all_to_all | solution.py:33
  169.7 2.6 %copy.17 = bf16[2,128,4,512]{3,2,1,0:T(4,128)(2,1)} copy(bf16[2,128,4,512]{3,2,0,1:T(4,128)(2,1)} %all-to-all-done.3) | data formatting | bytes 2097152 | tf_op jit(solution)/shard_map/all_to_all | solution.py:137
  173.9 20.6 %all-to-all-done.2 = bf16[4,1,512,512]{3,2,1,0:T(8,128)(2,1)} async-done(((bf16[4,1,512,512]{3,2,1,0:T(8,128)(2,1)}), bf16[4,1,512,512]{3,2,1,0:T(8,128)(2,1)}, u32[]{:S(2)}, u32[]{:S(2)}) %all-to-all-start.2) | async-done | bytes 2097184 | tf_op jit(solution)/shard_map/all_to_all | solution.py:33
  194.5 2.3 slice.29
  196.8 2.6 %multiply_reduce_fusion.1 = (f32[2]{0:T(128)S(1)}, f32[2,128,512]{2,1,0:T(8,128)}) fusion(bf16[2,2,512,512]{3,2,1,0:T(8,128)(2,1)} %bitcast.9, bf16[2,512,512]{2,1,0:T(8,128)(2,1)S(1)} %reshape.508, bf16[2,1,512,512]{3,2,1,0:T(8,128)(2,1)} %slice.29, s32[]{:T(128)S(6)} %select_n.327), kind=kOutput, calls=%fused_computation.32 | convolution fusion | flops 268828672 | bytes 2883596 | tf_op jit(solution)/shard_map/kqc,kcd->kqd/dot_general | solution.py:75
  199.4 6.9 %all-reduce.2 = (f32[4]{0:T(128)S(1)}, f32[4]{0:T(128)S(1)}) all-reduce(f32[4]{0:T(128)S(1)} %get-tuple-element.17, f32[4]{0:T(128)S(1)} %get-tuple-element.16), channel_id=1, replica_groups=mesh['dp'=4,'shard_0'=8,'shard_1'=8,'shard_2'=2] {'dp'}, use_global_device_ids=true, to_apply=%region_15.16 | all-reduce | flops 8 | bytes 64 | tf_op jit(solution)/shard_map/psum | solution.py:48
  206.3 12.7 %all-reduce.1 = (f32[4]{0:T(128)S(1)}, f32[4]{0:T(128)S(1)}) all-reduce(f32[4]{0:T(128)S(1)} %get-tuple-element.22, f32[4]{0:T(128)S(1)} %get-tuple-element.23), channel_id=1, replica_groups=mesh['dp'=4,'shard_0'=8,'shard_1'=8,'shard_2'=2] {'shard_0'}, use_global_device_ids=true, to_apply=%region_16.17 | all-reduce | flops 8 | bytes 64 | tf_op jit(solution)/shard_map/psum | solution.py:48
  219.0 13.1 %all-reduce = (f32[4]{0:T(128)S(1)}, f32[4]{0:T(128)S(1)}) all-reduce(f32[4]{0:T(128)S(1)} %get-tuple-element.20, f32[4]{0:T(128)S(1)} %get-tuple-element.21), channel_id=1, replica_groups=mesh['dp'=4,'shard_0'=8,'shard_1'=8,'shard_2'=2] {'shard_1'}, use_global_device_ids=true, to_apply=%region_17.18 | all-reduce | flops 8 | bytes 64 | tf_op jit(solution)/shard_map/psum | solution.py:48
  232.2 12.7 %all-reduce.3 = (f32[4]{0:T(128)S(1)}, f32[4]{0:T(128)S(1)}) all-reduce(f32[4]{0:T(128)S(1)} %get-tuple-element.18, f32[4]{0:T(128)S(1)} %get-tuple-element.19), channel_id=1, replica_groups=mesh['dp'=4,'shard_0'=8,'shard_1'=8,'shard_2'=2] {'shard_2'}, use_global_device_ids=true, to_apply=%region_18.19 | all-reduce | flops 8 | bytes 64 | tf_op jit(solution)/shard_map/psum | solution.py:48
  (54 shorter events, 31.9 us)
Async XLA Ops:
  0.0 9.0 %copy-start = (f32[1,128,2,4,512]{4,3,2,1,0:T(4,128)S(1)}, f32[1,128,2,4,512]{4,3,2,1,0:T(4,128)}, u32[]{:S(2)}) copy-start(f32[1,128,2,4,512]{4,3,2,1,0:T(4,128)} %param.4) | copy-start | bytes 6291460
  70.2 54.6 %all-to-all-start.1 = ((f32[128,4,512]{2,1,0:T(4,128)}), f32[128,4,512]{2,1,0:T(4,128)S(1)}, u32[]{:S(2)}, u32[]{:S(2)}) async-start(f32[128,4,512]{2,1,0:T(4,128)} %reduce_sum.92), calls=%async_computation.1 | async-start | bytes 2097152 | tf_op jit(solution)/shard_map/all_to_all | solution.py:125
  124.7 37.5 %all-to-all-start.3 = ((bf16[2,128,4,512]{3,2,0,1:T(4,128)(2,1)}), bf16[2,128,4,512]{3,2,0,1:T(4,128)(2,1)}, u32[]{:S(2)}, u32[]{:S(2)}) async-start(bf16[2,128,4,512]{3,2,0,1:T(4,128)(2,1)} %copy.16), calls=%async_computation.3 | async-start | bytes 2097152 | tf_op jit(solution)/shard_map/all_to_all | solution.py:137
  145.9 5.5 %copy-start.1 = (f32[512,512]{1,0:T(8,128)S(1)}, f32[512,512]{1,0:T(8,128)}, u32[]{:S(2)}) copy-start(f32[512,512]{1,0:T(8,128)} %reshape.507) | copy-start | bytes 3145732
  159.2 8.9 %copy-start.2 = (s32[4]{0:T(128)S(1)}, s32[4]{0:T(128)}, u32[]{:S(2)}) copy-start(s32[4]{0:T(128)} %param.7) | copy-start | bytes 52
  163.7 30.8 %all-to-all-start.2 = ((bf16[4,1,512,512]{3,2,1,0:T(8,128)(2,1)}), bf16[4,1,512,512]{3,2,1,0:T(8,128)(2,1)}, u32[]{:S(2)}, u32[]{:S(2)}) async-start(bf16[4,1,512,512]{3,2,1,0:T(8,128)(2,1)} %broadcast_in_dim.132), calls=%async_computation.2 | async-start | bytes 4194304 | tf_op jit(solution)/shard_map/all_to_all | solution.py:33
where the time goes:
time: 248 us; the launch traced here: 247 us
  blocking collectives  93.2 us (38%)
  waiting for transfers between devices  40.4 us (16%)
  local copies, waits for them, and re-layouts  35.6 us (14%)
  starting transfers between devices  35.1 us (14%)
  matrix products  23.9 us (10%)
  other arithmetic  16.9 us (7%)
    all_to_all x1, blocking collectives, sent_and_summed(): tiles = lax.all_to_all(in_blocks(x, dim, peers), axis, 0, 0, tiled=True)  47.8 us
    psum x4, blocking collectives, over_axes(): return functools.reduce(lax.psum, axes, x)  45.4 us
    all_to_all x1, starting transfers between devices, on_device(): lax.all_to_all(outgoing, SHARD, split_axis=0, concat_axis=0, tiled=True)  23.6 us
    dot_general x9, matrix products, product(): jnp.dot(left_side, right_side, precision=highest, preferred_element_type=...  21.3 us
    all_to_all x1, waiting for transfers between devices, copy_for_each(): lax.all_to_all(jnp.broadcast_to(x[None], (peers, *x.shape)), axis, 0, 0,...  20.6 us
    all_to_all x1, waiting for transfers between devices, on_device(): lax.all_to_all(outgoing, SHARD, split_axis=0, concat_axis=0, tiled=True)  18.7 us
    all_to_all x1, starting transfers between devices, on_device(): lax.all_to_all(grad_send, SHARD, split_axis=1, concat_axis=1, tiled=True)  7.05 us
  transfers between devices with their start and end apart: 3, of which 3 were waited for; matrix products, arithmetic and copies ran while one was open for 18% of the time, Pallas kernels for 0%

commit v1 on v0

v1 whole, which is shorter than its diff:
```python
import functools

import jax
import jax.numpy as jnp
from jax import lax
from jax.experimental import pallas as pl
from jax.experimental.pallas import tpu as pltpu
from jax.sharding import Mesh
from jax.sharding import PartitionSpec as P

OCAP = 2
LAYERS = 4
LANES = 128
SHARD = ("z", "y", "c")
bf16, f32, i32 = jnp.bfloat16, jnp.float32, jnp.int32
SMEM = pl.BlockSpec(memory_space=pltpu.SMEM)
VMEM = pl.BlockSpec(memory_space=pltpu.VMEM)


def call(body, out_shape, in_specs, scratch=()):
    return pl.pallas_call(
        body,
        out_shape=out_shape,
        in_specs=in_specs,
        out_specs=jax.tree.map(lambda _: VMEM, out_shape),
        scratch_shapes=list(scratch),
    )


def packed(x):
    n, r, width = x.shape
    return x.reshape(n, r, 4, width // 4).transpose(0, 2, 1, 3).reshape(n, 4 * r, width // 4)


def pack_stats_body(order_ref, stats_ref, out_ref, *, groups, each, blocks):
    for x in range(groups):

        def step(k, carry, x=x):
            info = order_ref[k * groups + x]
            block = lax.rem(info, blocks)
            core = lax.rem(lax.div(info, blocks), 2)
            for c in range(2):
                out_ref[x * 2 + c, k] = stats_ref[2 * block + (core ^ c)].astype(bf16)
            return carry

        lax.fori_loop(0, each, step, 0, unroll=4)


def pack_grad_body(order_ref, place_ref, grad_ref, out_ref, *, groups, each, blocks):
    out_ref[...] = jnp.zeros(out_ref.shape, bf16)
    me = place_ref[0]

    def step(k, carry):
        info = order_ref[k * groups + me]
        column = lax.rem(lax.div(info, 2 * blocks), out_ref.shape[0])
        out_ref[column] = grad_ref[lax.rem(info, blocks)]
        return carry

    lax.fori_loop(0, each, step, 0, unroll=4)


def sum_stats_body(order_ref, place_ref, got_ref, out_ref, *, groups, each, blocks):
    out_ref[...] = jnp.zeros(out_ref.shape, bf16)
    me = place_ref[0]
    rows = got_ref.shape[2]

    def step(k, carry):
        column = lax.rem(lax.div(order_ref[k * groups + me], 2 * blocks), out_ref.shape[0])
        for c in range(2):
            total = got_ref[c, k].astype(f32)
            for x in range(1, groups):
                total = total + got_ref[2 * x + c, k].astype(f32)
            out_ref[column, c * rows : (c + 1) * rows] = total.astype(bf16)
        return carry

    lax.fori_loop(0, each, step, 0, unroll=4)


def dot(a, b):
    return jnp.dot(a, b, preferred_element_type=f32)


def newton_body(got_ref, out_ref, wide_ref, a_ref):
    order = out_ref.shape[0]
    chunk = got_ref.shape[2]
    wide_ref[...] = got_ref[...].astype(f32)
    for c in range(2):
        for q in range(4):
            a_ref[:, 4 * c : 4 * c + 4, q * chunk : (q + 1) * chunk] = wide_ref[
                :, 16 * c + 4 * q : 16 * c + 4 * q + 4, :
            ]
    a = a_ref[...].reshape(order, order)
    mean = jnp.sum(a * a, keepdims=True) * (1.0 / (order * order))
    magnitude = order * jnp.sqrt(mean + 1e-06)
    n = a * (0.25 / magnitude)
    nb = n.astype(bf16)
    e = dot(nb, nb) - 2.5 * n
    eb = e.astype(bf16)
    h = dot(eb, eb) + 3.125 * e
    n1 = dot(h.astype(bf16), nb) + 2.44140625 * n
    n1b = n1.astype(bf16)
    d = dot(nb, n1b) - 1.25 * (n + n1)
    e1 = dot(n1b, n1b) - 2.5 * n1
    e1b = e1.astype(bf16)
    h1 = dot(e1b, e1b) + 3.125 * e1
    n2 = dot(h1.astype(bf16), n1b) + 2.44140625 * n1
    x = 1.25 * d - 1.5625 * n2 - dot(d.astype(bf16), n2.astype(bf16))
    diagonal = lax.broadcasted_iota(i32, x.shape, 0) == lax.broadcasted_iota(i32, x.shape, 1)
    x = x + jnp.where(diagonal, 1.953125, 0.0)
    out_ref[...] = (x * (1.0 / jnp.sqrt(jnp.sqrt(magnitude)))).astype(bf16)


def raw_body(place_ref, factor_ref, other_ref, mine_ref, theirs_ref, out_ref, norm_ref, wide_ref, g_ref):
    order = factor_ref.shape[0]
    chunk = mine_ref.shape[2]
    quarter = order // out_ref.shape[0]
    core, live, is_left, layer = place_ref[1], place_ref[2], place_ref[3], place_ref[4]
    first = core == 0
    mine, theirs = mine_ref[...].astype(f32), theirs_ref[...].astype(f32)
    wide_ref[:, 0:16] = jnp.where(first, mine, theirs)
    wide_ref[:, 16:32] = jnp.where(first, theirs, mine)
    for c in range(2):
        for q in range(4):
            g_ref[:, 4 * c : 4 * c + 4, q * chunk : (q + 1) * chunk] = wide_ref[
                :, 16 * c + 4 * q : 16 * c + 4 * q + 4, :
            ]
    g = g_ref[...].reshape(order, order)
    gb = g.astype(bf16)
    grad_sq = jnp.sum(g * g, keepdims=True)
    lane = lax.broadcasted_iota(i32, (1, LANES), 1)

    def finish(left, right):
        middle = dot(left, gb).astype(bf16)
        raw = dot(middle, right)
        raw_sq = jnp.sum(raw * raw, keepdims=True)
        norms = jnp.where(lane == layer, grad_sq, 0.0) + jnp.where(lane == layer + LAYERS, raw_sq, 0.0)
        norms = jnp.where(live > 0, norms, 0.0)
        norm_ref[...] = jnp.broadcast_to(norms[:, None, :], norm_ref.shape)
        for x in range(out_ref.shape[0]):
            out_ref[x, 0:quarter] = raw[x * quarter : (x + 1) * quarter].astype(bf16)
            out_ref[x, quarter:] = jnp.zeros((out_ref.shape[1] - quarter, order), bf16)

    @pl.when(is_left > 0)
    def _():
        finish(factor_ref[...], other_ref[...])

    @pl.when(is_left == 0)
    def _():
        finish(other_ref[...], factor_ref[...])


def plane_body(norm_ref, raw_ref, out_ref):
    del raw_ref
    total = jnp.sum(norm_ref[...], axis=0)
    high = total.astype(bf16).astype(f32)
    mid = (total - high).astype(bf16).astype(f32)
    low = total - high - mid
    row = lax.broadcasted_iota(i32, (out_ref.shape[1], LANES), 0)
    tile = jnp.where(row == 0, high, 0.0) + jnp.where(row == 1, mid, 0.0) + jnp.where(row == 2, low, 0.0)
    for x in range(out_ref.shape[0]):
        out_ref[x] = jnp.zeros(out_ref.shape[1:], bf16)
        out_ref[x, :, 0:LANES] = tile.astype(bf16)


def scale_body(place_ref, got_ref, out_ref):
    quarter = out_ref.shape[1]
    total = jnp.zeros((1, LANES), f32)
    for x in range(got_ref.shape[0]):
        rows = got_ref[x, quarter:, 0:LANES].astype(f32)
        total = total + jnp.sum(rows, axis=0, keepdims=True)
    lane = lax.broadcasted_iota(i32, (1, LANES), 1)
    for s in range(OCAP):
        live, source, layer = place_ref[5 + 3 * s], place_ref[6 + 3 * s], place_ref[7 + 3 * s]
        grad_total = jnp.sum(jnp.where(lane == layer, total, 0.0), keepdims=True)
        raw_total = jnp.sum(jnp.where(lane == layer + LAYERS, total, 0.0), keepdims=True)
        ratio = jnp.sqrt((grad_total + 1e-06) / (raw_total + 1e-06))
        scaled = (got_ref[source, 0:quarter].astype(f32) * ratio).astype(bf16)
        out_ref[s] = jnp.where(live > 0, scaled, jnp.zeros((), bf16))


def on_device(stats_partial, gradient, owner_of, layer_count):
    groups = lax.axis_size("dp")
    columns = lax.axis_size("z") * lax.axis_size("y")
    x, c = lax.axis_index("dp"), lax.axis_index("c")
    column = lax.axis_index(("z", "y"))
    blocks = owner_of.shape[0]
    each = blocks // groups
    local_rows, order = gradient.shape[1:]
    quarter = order // groups
    chunk = order // 4

    ids = jnp.arange(blocks, dtype=i32)
    same = owner_of[None, :] == owner_of[:, None]
    before = ids[None, :] < ids[:, None]
    rank = jnp.sum(((owner_of[None, :] < owner_of[:, None]) | (same & before)).astype(i32), axis=1)
    slot = jnp.sum((same & before).astype(i32), axis=1)
    ends = jnp.cumsum(layer_count)
    layer = jnp.sum((ids[:, None] >= ends[None, :]).astype(i32), axis=1)
    info = ids + blocks * (owner_of + 2 * columns * (layer + LAYERS * slot))
    hit = rank[:, None] == ids[None, :]
    sorted_info = jnp.sum(jnp.where(hit, info[:, None], 0), axis=0)
    sorted_owner = lax.rem(lax.div(sorted_info, blocks), 2 * columns)
    group = lax.rem(ids, groups)

    def lookup(mask):
        found = jnp.sum(jnp.where(mask, sorted_info + blocks * 2 * columns * LAYERS * OCAP * (1 + group), 0))
        live = (found > 0).astype(i32)
        rest = lax.div(found, blocks * 2 * columns)
        source = jnp.maximum(lax.div(rest, LAYERS * OCAP) - 1, 0)
        return live, source, lax.rem(rest, LAYERS), lax.rem(lax.div(found, blocks), 2)

    mine = (lax.div(sorted_owner, 2) == column) & (group == x)
    live, _, my_layer, owner_core = lookup(mine)
    place = [x, c, live, (owner_core == c).astype(i32), my_layer]
    sorted_slot = lax.div(sorted_info, blocks * 2 * columns * LAYERS)
    for s in range(OCAP):
        place += list(lookup((sorted_owner == column * 2 + c) & (sorted_slot == s))[:3])
    place = jnp.stack(place).astype(i32)

    sizes = dict(groups=groups, each=each, blocks=blocks)
    struct = jax.ShapeDtypeStruct
    stats = packed(stats_partial.reshape(2 * blocks, local_rows, order))
    outgoing = call(
        functools.partial(pack_stats_body, **sizes),
        struct((2 * groups, each, 16, chunk), bf16),
        [SMEM, VMEM],
    )(sorted_info, stats)
    arrived = lax.all_to_all(outgoing, ("dp", "c"), 0, 0, tiled=True)

    grad_out = call(
        functools.partial(pack_grad_body, **sizes),
        struct((columns, 16, chunk), bf16),
        [SMEM, SMEM, VMEM],
    )(sorted_info, place, packed(gradient))
    grad_mine = lax.all_to_all(grad_out, ("z", "y"), 0, 0, tiled=True)
    grad_theirs = lax.ppermute(grad_mine, "c", [(0, 1), (1, 0)])

    summed = call(
        functools.partial(sum_stats_body, **sizes),
        struct((columns, 32, chunk), bf16),
        [SMEM, SMEM, VMEM],
    )(sorted_info, place, arrived)
    statistic = lax.all_to_all(summed, ("z", "y"), 0, 0, tiled=True)

    scratch = [pltpu.VMEM((columns, 32, chunk), f32), pltpu.VMEM((columns, 8, order), f32)]
    factor = call(newton_body, struct((order, order), bf16), [VMEM], scratch)(statistic)
    other = lax.ppermute(factor, "c", [(0, 1), (1, 0)])

    raw, norms = call(
        raw_body,
        (struct((groups, quarter + 8, order), bf16), struct((columns, 1, LANES), f32)),
        [SMEM, VMEM, VMEM, VMEM, VMEM],
        scratch,
    )(place, factor, other, grad_mine, grad_theirs)
    norms = lax.all_to_all(norms, ("z", "y"), 0, 0, tiled=True)
    tail = pl.BlockSpec((groups, 8, order), lambda i: (0, quarter // 8, 0))
    raw = pl.pallas_call(
        plane_body,
        grid=(1,),
        out_shape=struct(raw.shape, bf16),
        in_specs=[pl.BlockSpec(norms.shape, lambda i: (0, 0, 0)), pl.BlockSpec(memory_space=pl.ANY)],
        out_specs=tail,
        input_output_aliases={1: 0},
    )(norms, raw)
    spread = lax.all_to_all(raw, "dp", 0, 0, tiled=True)
    out = call(scale_body, struct((OCAP, quarter, order), bf16), [SMEM, VMEM])(place, spread)
    return out[None]


def solution(mesh):
    shards = mesh.shape["shard"]
    side = 1
    while (2 * side) ** 2 * 2 <= shards:
        side *= 2
    torus = Mesh(
        mesh.devices.reshape(mesh.shape["dp"], shards // (2 * side), side, 2), ("dp", "z", "y", "c")
    )
    placed = (P("dp", None, None, SHARD, None), P(None, SHARD, None), P(), P())
    return jax.shard_map(
        on_device,
        mesh=torus,
        in_specs=placed,
        out_specs=P(SHARD, None, "dp", None),
        check_vma=False,
    )
```

time: 248 us -> 129 us (0.52)
  blocking collectives: 93.2 us -> 28.9 us
  local copies, waits for them, and re-layouts: 35.6 us -> 3.18 us
  matrix products: 23.9 us -> 0 us
  Pallas kernels: 0 us -> 20.6 us
  waiting for transfers between devices: 40.4 us -> 25.4 us
  other arithmetic: 16.9 us -> 3.86 us
  between operations: 1.76 us -> 7.66 us
  starting transfers between devices: 35.1 us -> 38.2 us
    psum x4 -> x0, blocking collectives: 45.4 us -> none  [over_axes(): return functools.reduce(lax.psum, axes, x)]
    dot_general x10 -> x0, matrix products: 23.9 us -> none  [the longest x9 21.3 us: product(): jnp.dot(left_side, right_side, precision=highest, preferred_element_type=...]
    gather x9 -> x0, local copies, waits for them, and re-layouts: 21.5 us -> none  [the longest x2 4.93 us: on_device(): jnp.take(gradient, grad_pick, axis=0)]
    pallas_call x0 -> x7, Pallas kernels: none -> 20.6 us  [the longest x1 5.29 us: on_device(): call(newton_body, struct((order, order), bf16), [VMEM], scratch)(statistic)]
    all_to_all x1 -> x2, blocking collectives: 47.8 us -> 28.9 us  [the longest x1 16.8 us: on_device(): norms = lax.all_to_all(norms, ('z', 'y'), 0, 0, tiled=True)]
    all_to_all x3, waiting for transfers between devices: 40.4 us -> 24.3 us  [the longest x1 14.8 us: on_device(): statistic = lax.all_to_all(summed, ('z', 'y'), 0, 0, tiled=True)]
    ppermute x0 -> x2, starting transfers between devices: none -> 9.11 us  [the longest x1 5.37 us: on_device(): grad_theirs = lax.ppermute(grad_mine, 'c', [(0, 1), (1, 0)])]
    all_to_all x3, starting transfers between devices: 35.1 us -> 29.1 us  [the longest x1 11.8 us: on_device(): statistic = lax.all_to_all(summed, ('z', 'y'), 0, 0, tiled=True)]
  transfers between devices with their start and end apart: 3 -> 5, of which waited for: 3 -> 4; matrix products, arithmetic and copies ran while one was open for 18% -> 1% of each run, Pallas kernels for 0% -> 6%
where the time goes in v1:
time: 129 us; the launch traced here: 128 us
  starting transfers between devices  38.2 us (30%)
  blocking collectives  28.9 us (22%)
  waiting for transfers between devices  25.4 us (20%)
  Pallas kernels  20.6 us (16%)
  between operations  7.66 us (6%)
  other arithmetic  3.86 us (3%)
  local copies, waits for them, and re-layouts  3.18 us (2%)
    all_to_all x1, blocking collectives, on_device(): norms = lax.all_to_all(norms, ('z', 'y'), 0, 0, tiled=True)  16.8 us
    all_to_all x1, waiting for transfers between devices, on_device(): statistic = lax.all_to_all(summed, ('z', 'y'), 0, 0, tiled=True)  14.8 us
    all_to_all x1, blocking collectives, on_device(): spread = lax.all_to_all(raw, 'dp', 0, 0, tiled=True)  12.2 us
    all_to_all x1, starting transfers between devices, on_device(): statistic = lax.all_to_all(summed, ('z', 'y'), 0, 0, tiled=True)  11.8 us
    all_to_all x1, starting transfers between devices, on_device(): arrived = lax.all_to_all(outgoing, ('dp', 'c'), 0, 0, tiled=True)  10.3 us
    all_to_all x1, starting transfers between devices, on_device(): grad_mine = lax.all_to_all(grad_out, ('z', 'y'), 0, 0, tiled=True)  7 us
    all_to_all x1, waiting for transfers between devices, on_device(): arrived = lax.all_to_all(outgoing, ('dp', 'c'), 0, 0, tiled=True)  6 us
    ppermute x1, starting transfers between devices, on_device(): grad_theirs = lax.ppermute(grad_mine, 'c', [(0, 1), (1, 0)])  5.37 us
  transfers between devices with their start and end apart: 5, of which 4 were waited for; matrix products, arithmetic and copies ran while one was open for 1% of the time, Pallas kernels for 6%

profile of v1, /device:TPU:1, one launch (start us, length us, event | category | flops | bytes accessed | tf_op | source)
XLA Modules:
  0.0 127.8 jit_solution(8282052749194700526)
XLA Ops:
  0.0 0.9 convert_reduce_fusion.1
  0.9 0.8 reduce-window.8
  3.1 3.6 %shard_map.46 = bf16[8,32,16,128]{3,2,1,0:T(8,128)(2,1)} custom-call(s32[128]{0:T(128)} %select_reduce_fusion.order_ref, f32[256,16,128]{2,1,0:T(8,128)} %bitcast.24), custom_call_target="tpu_custom_call" | custom-call | tf_op jit(solution)/shard_map/pallas_call | solution.py:223
  6.8 10.3 %all-to-all-start = ((bf16[8,32,16,128]{3,2,1,0:T(8,128)(2,1)}), bf16[8,32,16,128]{3,2,1,0:T(8,128)(2,1)S(1)}, u32[]{:S(2)}, u32[]{:S(2)}) async-start(bf16[8,32,16,128]{3,2,1,0:T(8,128)(2,1)} %shard_map.46), calls=%async_computation | async-start | bytes 2097152 | tf_op jit(solution)/shard_map/all_to_all | solution.py:228
  17.1 0.7 fusion.5
  26.1 6.0 %all-to-all-done.got_ref = bf16[8,32,16,128]{3,2,1,0:T(8,128)(2,1)S(1)} async-done(((bf16[8,32,16,128]{3,2,1,0:T(8,128)(2,1)}), bf16[8,32,16,128]{3,2,1,0:T(8,128)(2,1)S(1)}, u32[]{:S(2)}, u32[]{:S(2)}) %all-to-all-start) | async-done | bytes 1048608 | tf_op jit(solution)/shard_map/all_to_all | solution.py:228
  32.1 1.0 copy-done
  33.1 2.3 %shard_map.47 = bf16[64,32,128]{2,1,0:T(8,128)(2,1)} custom-call(s32[128]{0:T(128)} %select_reduce_fusion.order_ref, s32[11]{0:T(128)} %stack.63.place_ref, bf16[8,32,16,128]{3,2,1,0:T(8,128)(2,1)} %copy-done), custom_call_target="tpu_custom_call" | custom-call | tf_op jit(solution)/shard_map/pallas_call | solution.py:238
  35.4 11.8 %all-to-all-start.1 = ((bf16[64,32,128]{2,1,0:T(8,128)(2,1)}), bf16[64,32,128]{2,1,0:T(8,128)(2,1)S(1)}, u32[]{:S(2)}, u32[]{:S(2)}) async-start(bf16[64,32,128]{2,1,0:T(8,128)(2,1)} %shard_map.47), calls=%async_computation.1 | async-start | bytes 1048576 | tf_op jit(solution)/shard_map/all_to_all | solution.py:243
  47.1 2.0 %shard_map.49 = bf16[64,16,128]{2,1,0:T(8,128)(2,1)} custom-call(s32[128]{0:T(128)} %select_reduce_fusion.order_ref, s32[11]{0:T(128)} %stack.63.place_ref, bf16[128,16,128]{2,1,0:T(8,128)(2,1)} %bitcast.25), custom_call_target="tpu_custom_call" | custom-call | tf_op jit(solution)/shard_map/pallas_call | solution.py:230
  49.2 14.8 %all-to-all-done.1.got_ref = bf16[64,32,128]{2,1,0:T(8,128)(2,1)S(1)} async-done(((bf16[64,32,128]{2,1,0:T(8,128)(2,1)}), bf16[64,32,128]{2,1,0:T(8,128)(2,1)S(1)}, u32[]{:S(2)}, u32[]{:S(2)}) %all-to-all-start.1) | async-done | bytes 524320 | tf_op jit(solution)/shard_map/all_to_all | solution.py:243
  64.0 7.0 %all-to-all-start.2 = ((bf16[64,16,128]{2,1,0:T(8,128)(2,1)}), bf16[64,16,128]{2,1,0:T(8,128)(2,1)S(1)}, u32[]{:S(2)}, u32[]{:S(2)}) async-start(bf16[64,16,128]{2,1,0:T(8,128)(2,1)} %shard_map.49), calls=%async_computation.2 | async-start | bytes 524288 | tf_op jit(solution)/shard_map/all_to_all | solution.py:235
  71.0 5.3 %shard_map.48.factor_ref = bf16[512,512]{1,0:T(8,128)(2,1)} custom-call(bf16[64,32,128]{2,1,0:T(8,128)(2,1)} %copy-done.1), custom_call_target="tpu_custom_call" | custom-call | tf_op jit(solution)/shard_map/pallas_call | solution.py:246
  76.3 3.7 %collective-permute-start = (bf16[512,512]{1,0:T(8,128)(2,1)}, bf16[512,512]{1,0:T(8,128)(2,1)S(1)}, u32[]{:S(2)}, u32[]{:S(2)}) collective-permute-start(bf16[512,512]{1,0:T(8,128)(2,1)} %shard_map.48.factor_ref), channel_id=1, source_target_pairs={{0,1},{1,0},{2,3},{3,2},{4,5},{5,4},{6,7},{7,6},{8,9},{9,8},{10,11... | collective-permute-start | bytes 1572872 | tf_op jit(solution)/shard_map/ppermute | solution.py:247
  80.0 3.5 %all-to-all-done.2.mine_ref = bf16[64,16,128]{2,1,0:T(8,128)(2,1)S(1)} async-done(((bf16[64,16,128]{2,1,0:T(8,128)(2,1)}), bf16[64,16,128]{2,1,0:T(8,128)(2,1)S(1)}, u32[]{:S(2)}, u32[]{:S(2)}) %all-to-all-start.2) | async-done | bytes 262176 | tf_op jit(solution)/shard_map/all_to_all | solution.py:235
  83.5 5.4 %collective-permute-start.1 = (bf16[64,16,128]{2,1,0:T(8,128)(2,1)S(1)}, bf16[64,16,128]{2,1,0:T(8,128)(2,1)S(1)}, u32[]{:S(2)}, u32[]{:S(2)}) collective-permute-start(bf16[64,16,128]{2,1,0:T(8,128)(2,1)S(1)} %all-to-all-done.2.mine_ref), channel_id=1, source_target_pairs={{0,1},{1,0},{2,3},{3,2},{4,5},{5,4},{6,7},{7,6},{8,9},{9,8},{10,11... | collective-permute-start | bytes 786440 | tf_op jit(solution)/shard_map/ppermute | solution.py:236
  88.9 1.1 collective-permute-done.1.theirs_ref
  90.0 0.7 copy-done.4
  90.7 0.8 copy-done.3
  91.5 3.9 %shard_map.50 = (bf16[4,136,512]{2,1,0:T(8,128)(2,1)}, f32[64,1,128]{2,1,0:T(1,128)}) custom-call(s32[11]{0:T(128)} %stack.63.place_ref, bf16[512,512]{1,0:T(8,128)(2,1)} %shard_map.48.factor_ref, bf16[512,512]{1,0:T(8,128)(2,1)} %copy-done.3, bf16[64,16,128]{2,1,0:T(8,128)(2,1)} %copy-done.2, bf16[64,16,128]{2,1,0:T(8,128)(2,1)} %copy-done.4), custom_call_target="tpu_custom_call" | custom-call | tf_op jit(solution)/shard_map/pallas_call | solution.py:249
  95.5 16.8 %all_to_all.25.norm_ref = f32[64,1,128]{2,1,0:T(1,128)} all-to-all(f32[64,1,128]{2,1,0:T(1,128)} %get-tuple-element.7), channel_id=1, replica_groups=mesh['dp'=4,'z'=8,'y'=8,'c'=2] {'z','y'}, dimensions={0} | all-to-all | bytes 65536 | tf_op jit(solution)/shard_map/all_to_all | solution.py:255
  112.2 1.5 %shard_map.51 = bf16[4,136,512]{2,1,0:T(8,128)(2,1)} custom-call(f32[64,1,128]{2,1,0:T(1,128)} %all_to_all.25.norm_ref, bf16[4,136,512]{2,1,0:T(8,128)(2,1)} %get-tuple-element.8.raw_ref), custom_call_target="tpu_custom_call", output_to_operand_aliasing={{}: (1, {})} | custom-call | tf_op jit(solution)/shard_map/pallas_call | solution.py:257
  113.7 12.2 %all_to_all.26.got_ref = bf16[4,136,512]{2,1,0:T(8,128)(2,1)} all-to-all(bf16[4,136,512]{2,1,0:T(8,128)(2,1)} %shard_map.51), channel_id=1, replica_groups=mesh['dp'=4,'z'=8,'y'=8,'c'=2] {'dp'}, dimensions={0} | all-to-all | bytes 1114112 | tf_op jit(solution)/shard_map/all_to_all | solution.py:265
  125.8 2.0 %shard_map.52 = bf16[2,128,512]{2,1,0:T(8,128)(2,1)} custom-call(s32[11]{0:T(128)} %stack.63.place_ref, bf16[4,136,512]{2,1,0:T(8,128)(2,1)} %all_to_all.26.got_ref), custom_call_target="tpu_custom_call" | custom-call | tf_op jit(solution)/shard_map/pallas_call | solution.py:266
  (14 shorter events, 2.1 us)
Async XLA Ops:
  3.1 13.9 %copy-start.5 = (s32[128]{0:T(128)S(1)}, s32[128]{0:T(128)}, u32[]{:S(2)}) copy-start(s32[128]{0:T(128)} %select_reduce_fusion.order_ref) | copy-start | bytes 1540
  6.8 25.3 %all-to-all-start = ((bf16[8,32,16,128]{3,2,1,0:T(8,128)(2,1)}), bf16[8,32,16,128]{3,2,1,0:T(8,128)(2,1)S(1)}, u32[]{:S(2)}, u32[]{:S(2)}) async-start(bf16[8,32,16,128]{3,2,1,0:T(8,128)(2,1)} %shard_map.46), calls=%async_computation | async-start | bytes 2097152 | tf_op jit(solution)/shard_map/all_to_all | solution.py:228
  32.1 1.0 copy-start
  35.4 28.6 %all-to-all-start.1 = ((bf16[64,32,128]{2,1,0:T(8,128)(2,1)}), bf16[64,32,128]{2,1,0:T(8,128)(2,1)S(1)}, u32[]{:S(2)}, u32[]{:S(2)}) async-start(bf16[64,32,128]{2,1,0:T(8,128)(2,1)} %shard_map.47), calls=%async_computation.1 | async-start | bytes 1048576 | tf_op jit(solution)/shard_map/all_to_all | solution.py:243
  64.0 7.0 %copy-start.1 = (bf16[64,32,128]{2,1,0:T(8,128)(2,1)}, bf16[64,32,128]{2,1,0:T(8,128)(2,1)S(1)}, u32[]{:S(2)}) copy-start(bf16[64,32,128]{2,1,0:T(8,128)(2,1)S(1)} %all-to-all-done.1.got_ref) | copy-start | bytes 1572868
  64.0 19.5 %all-to-all-start.2 = ((bf16[64,16,128]{2,1,0:T(8,128)(2,1)}), bf16[64,16,128]{2,1,0:T(8,128)(2,1)S(1)}, u32[]{:S(2)}, u32[]{:S(2)}) async-start(bf16[64,16,128]{2,1,0:T(8,128)(2,1)} %shard_map.49), calls=%async_computation.2 | async-start | bytes 524288 | tf_op jit(solution)/shard_map/all_to_all | solution.py:235
  76.3 13.7 %collective-permute-start = (bf16[512,512]{1,0:T(8,128)(2,1)}, bf16[512,512]{1,0:T(8,128)(2,1)S(1)}, u32[]{:S(2)}, u32[]{:S(2)}) collective-permute-start(bf16[512,512]{1,0:T(8,128)(2,1)} %shard_map.48.factor_ref), channel_id=1, source_target_pairs={{0,1},{1,0},{2,3},{3,2},{4,5},{5,4},{6,7},{7,6},{8,9},{9,8},{10,11... | collective-permute-start | bytes 1572872 | tf_op jit(solution)/shard_map/ppermute | solution.py:247
  83.5 6.5 %copy-start.2 = (bf16[64,16,128]{2,1,0:T(8,128)(2,1)}, bf16[64,16,128]{2,1,0:T(8,128)(2,1)S(1)}, u32[]{:S(2)}) copy-start(bf16[64,16,128]{2,1,0:T(8,128)(2,1)S(1)} %all-to-all-done.2.mine_ref) | copy-start | bytes 786436
  83.5 6.5 %collective-permute-start.1 = (bf16[64,16,128]{2,1,0:T(8,128)(2,1)S(1)}, bf16[64,16,128]{2,1,0:T(8,128)(2,1)S(1)}, u32[]{:S(2)}, u32[]{:S(2)}) collective-permute-start(bf16[64,16,128]{2,1,0:T(8,128)(2,1)S(1)} %all-to-all-done.2.mine_ref), channel_id=1, source_target_pairs={{0,1},{1,0},{2,3},{3,2},{4,5},{5,4},{6,7},{7,6},{8,9},{9,8},{10,11... | collective-permute-start | bytes 786440 | tf_op jit(solution)/shard_map/ppermute | solution.py:236
  90.0 0.7 copy-start.4
  90.7 0.8 copy-start.3

commit v2 on v1

v2 whole, which is shorter than its diff:
```python
import functools

import jax
import jax.numpy as jnp
from jax import lax
from jax.experimental import pallas as pl
from jax.experimental.pallas import tpu as pltpu
from jax.sharding import Mesh
from jax.sharding import PartitionSpec as P

OCAP = 2
LAYERS = 4
LANES = 128
SHARD = ("z", "y", "c")
bf16, f32, i32 = jnp.bfloat16, jnp.float32, jnp.int32
SMEM = pl.BlockSpec(memory_space=pltpu.SMEM)
VMEM = pl.BlockSpec(memory_space=pltpu.VMEM)


ANY = pl.BlockSpec(memory_space=pl.ANY)


def bits(size):
    assert size & (size - 1) == 0
    return size.bit_length() - 1


def call(body, out_shape, in_specs, scratch=()):
    return pl.pallas_call(
        body,
        out_shape=out_shape,
        in_specs=in_specs,
        out_specs=jax.tree.map(lambda _: VMEM, out_shape),
        scratch_shapes=list(scratch),
    )


def packed(x):
    n, r, width = x.shape
    return x.reshape(n, r, 4, width // 4).transpose(0, 2, 1, 3).reshape(n, 4 * r, width // 4)


def index_body(owner_ref, count_ref, sorted_ref, place_ref, *, groups, columns):
    blocks = owner_ref.shape[1]
    me_x, me_c, me_column = lax.axis_index("dp"), lax.axis_index("c"), lax.axis_index(("z", "y"))
    owner = owner_ref[...]
    row = jnp.broadcast_to(owner, (blocks, blocks))
    col = row.T
    sub = lax.broadcasted_iota(i32, row.shape, 0)
    lane = lax.broadcasted_iota(i32, row.shape, 1)
    same = (col == row) & (sub < lane)
    rank = jnp.sum(jnp.where((col < row) | same, 1, 0), axis=0, keepdims=True)
    slot = jnp.sum(jnp.where(same, 1, 0), axis=0, keepdims=True)
    one_lane = lax.broadcasted_iota(i32, owner.shape, 1)
    layer = jnp.zeros(owner.shape, i32)
    end = jnp.int32(0)
    for number in range(LAYERS - 1):
        end = end + count_ref[number]
        layer = layer + jnp.where(one_lane >= end, 1, 0)
    owner_at = bits(blocks)
    layer_at = owner_at + bits(2 * columns)
    slot_at = layer_at + bits(LAYERS)
    top = slot_at + bits(OCAP)
    info = one_lane + (owner << owner_at) + (layer << layer_at) + (slot << slot_at)
    both = jnp.broadcast_to(info + (rank << top), row.shape).T
    ordered = jnp.sum(
        jnp.where((both >> top) == lane, both & ((1 << top) - 1), 0), axis=0, keepdims=True
    )
    sorted_ref[...] = ordered
    ordered_owner = (ordered >> owner_at) & (2 * columns - 1)
    group = one_lane & (groups - 1)
    coded = ordered + ((group + 1) << top)

    def lookup(mask):
        found = jnp.sum(jnp.where(mask, coded, 0), axis=1, keepdims=True)
        live = jnp.where(found > 0, 1, 0)
        source = jnp.maximum((found >> top) - 1, 0)
        return live, source, (found >> layer_at) & (LAYERS - 1), (found >> owner_at) & 1

    live, _, my_layer, core = lookup(((ordered_owner >> 1) == me_column) & (group == me_x))
    place = [live, core, my_layer]
    for s in range(OCAP):
        mask = (ordered_owner == me_column * 2 + me_c) & ((ordered >> slot_at) == s)
        place += list(lookup(mask)[:3])
    wide = lax.broadcasted_iota(i32, place_ref.shape, 1)
    out = jnp.zeros(place_ref.shape, i32)
    for number, value in enumerate(place):
        out = jnp.where(wide == number, value, out)
    place_ref[...] = out


def pack_stats_body(
    owner_ref, count_ref, stats_ref, out_ref, sorted_ref, place_ref, stats_vmem, out_vmem, order_ref, sems, *, groups, columns
):
    blocks = owner_ref.shape[1]
    each = out_ref.shape[1]
    load = pltpu.make_async_copy(stats_ref, stats_vmem, sems.at[0])
    load.start()
    index_body(owner_ref, count_ref, sorted_ref, place_ref, groups=groups, columns=columns)
    move = pltpu.make_async_copy(sorted_ref, order_ref, sems.at[1])
    move.start()
    move.wait()
    load.wait()
    stores = []
    for x in range(groups):

        def step(k, carry, x=x):
            info = order_ref[0, k * groups + x]
            block = info & (blocks - 1)
            core = (info >> bits(blocks)) & 1
            for c in range(2):
                out_vmem[x * 2 + c, k] = stats_vmem[2 * block + (core ^ c)].astype(bf16)
            return carry

        lax.fori_loop(0, each, step, 0, unroll=8 if each % 8 == 0 else 1)
        part = slice(2 * x, 2 * x + 2)
        stores.append(pltpu.make_async_copy(out_vmem.at[part], out_ref.at[part], sems.at[2 + x]))
        stores[-1].start()
    for store in stores:
        store.wait()


def grad_half_body(order_ref, grad_ref, out_ref, *, groups, blocks):
    me = lax.axis_index("dp")
    at = 8 * (1 - lax.axis_index("c"))

    def step(k, carry):
        block = order_ref[0, k * groups + me] & (blocks - 1)
        out_ref[k] = grad_ref[block, pl.ds(pl.multiple_of(at, 8), 8), :]
        return carry

    each = blocks // groups
    lax.fori_loop(0, each, step, 0, unroll=8 if each % 8 == 0 else 1)


def joined(first, second):
    top = lax.broadcasted_iota(i32, first.shape, 0) < 4
    even = jnp.where(top, first, pltpu.roll(second, 4, 0))
    odd = jnp.where(top, pltpu.roll(first, 4, 0), second)
    return even, odd


def sum_stats_body(order_ref, got_ref, grad_ref, theirs_ref, out_ref, *, groups, blocks):
    out_ref[...] = jnp.zeros(out_ref.shape, bf16)
    me = lax.axis_index("dp")
    core = lax.axis_index("c")

    def step(k, carry):
        info = order_ref[0, k * groups + me]
        column = (info >> (bits(blocks) + 1)) & (out_ref.shape[0] - 1)
        sums = []
        for c in range(2):
            total = got_ref[c, k].astype(f32)
            for x in range(1, groups):
                total = total + got_ref[2 * x + c, k].astype(f32)
            sums.append(total)
        tiles = []
        for v in range(2):
            tiles += joined(sums[0][8 * v : 8 * v + 8], sums[1][8 * v : 8 * v + 8])
        mine = grad_ref[info & (blocks - 1), pl.ds(pl.multiple_of(8 * core, 8), 8), :].astype(f32)
        theirs = theirs_ref[k].astype(f32)
        tiles += joined(jnp.where(core == 0, mine, theirs), jnp.where(core == 0, theirs, mine))
        for v in range(3):
            pair = jnp.concatenate(tiles[2 * v : 2 * v + 2], axis=0)
            out_ref[column, 16 * v : 16 * v + 16] = pair.astype(bf16)
        return carry

    each = blocks // groups
    lax.fori_loop(0, each, step, 0, unroll=4 if each % 4 == 0 else 1)


def dot(a, b):
    return jnp.dot(a, b, preferred_element_type=f32)


def newton_body(got_ref, out_ref, a_ref):
    order = out_ref.shape[1]
    chunk = got_ref.shape[2]
    for q in range(4):
        tile = got_ref[:, 8 * q : 8 * q + 8, :].astype(f32).reshape(order, chunk)
        a_ref[:, q * chunk : (q + 1) * chunk] = tile
    for q in range(2):
        tile = got_ref[:, 32 + 8 * q : 40 + 8 * q, :].astype(f32).reshape(order, chunk).astype(bf16)
        for v in range(2):
            place = slice((2 * v + q) * chunk, (2 * v + q + 1) * chunk)
            out_ref[order:, place] = tile[v * order // 2 : (v + 1) * order // 2]
    a = a_ref[...]
    mean = jnp.sum(a * a, keepdims=True) * (1.0 / (order * order))
    magnitude = order * jnp.sqrt(mean + 1e-06)
    n = a * (0.25 / magnitude)
    nb = n.astype(bf16)
    e = dot(nb, nb) - 2.5 * n
    eb = e.astype(bf16)
    h = dot(eb, eb) + 3.125 * e
    n1 = dot(h.astype(bf16), nb) + 2.44140625 * n
    n1b = n1.astype(bf16)
    d = dot(nb, n1b) - 1.25 * (n + n1)
    e1 = dot(n1b, n1b) - 2.5 * n1
    e1b = e1.astype(bf16)
    h1 = dot(e1b, e1b) + 3.125 * e1
    n2 = dot(h1.astype(bf16), n1b) + 2.44140625 * n1
    x = 1.25 * d - 1.5625 * n2 - dot(d.astype(bf16), n2.astype(bf16))
    diagonal = lax.broadcasted_iota(i32, x.shape, 0) == lax.broadcasted_iota(i32, x.shape, 1)
    x = x + jnp.where(diagonal, 1.953125, 0.0)
    out_ref[0:order] = (x * (1.0 / jnp.sqrt(jnp.sqrt(magnitude)))).astype(bf16)


def raw_body(place_ref, mine_ref, other_ref, out_ref, norm_ref, both_ref, sems):
    quarter = out_ref.shape[1]
    order = mine_ref.shape[1]
    half = order // 2
    live, core, layer = place_ref[0, 0], place_ref[0, 1], place_ref[0, 2]
    me_c, me_x = lax.axis_index("c"), lax.axis_index("dp")
    loads = [
        pltpu.make_async_copy(mine_ref, both_ref.at[me_c], sems.at[0]),
        pltpu.make_async_copy(other_ref, both_ref.at[1 - me_c], sems.at[1]),
    ]
    for load in loads:
        load.start()
    for load in loads:
        load.wait()
    raw = jnp.zeros((order, order), f32)
    grad_sq = jnp.zeros((1, 1), f32)
    for c in range(2):
        middle = jnp.zeros((order, half), f32)
        for v in range(2):
            grad = both_ref[c, order:, v * half : (v + 1) * half]
            middle = middle + dot(both_ref[core, 0:order, v * half : (v + 1) * half], grad)
            wide = grad.astype(f32)
            grad_sq = grad_sq + jnp.sum(wide * wide, keepdims=True)
        raw = raw + dot(middle.astype(bf16), both_ref[1 - core, c * half : (c + 1) * half])
    raw_sq = jnp.sum(raw * raw, keepdims=True)
    lane = lax.broadcasted_iota(i32, (1, LANES), 1)
    norms = jnp.where(lane == layer, grad_sq, 0.0) + jnp.where(lane == layer + LAYERS, raw_sq, 0.0)
    norms = jnp.where(live > 0, norms, 0.0)
    norm_ref[...] = jnp.broadcast_to(norms[:, None, :], norm_ref.shape)
    groups = out_ref.shape[0]
    for x in range(groups):
        out_ref[(x - me_x) & (groups - 1)] = raw[x * quarter : (x + 1) * quarter].astype(bf16)


def scale_body(place_ref, norm_ref, raw_ref, *refs):
    out_ref = refs[-1]
    groups = len(refs)
    total = jnp.sum(norm_ref[...], axis=0)
    lane = lax.broadcasted_iota(i32, (1, LANES), 1)
    me_x = lax.axis_index("dp")
    for s in range(OCAP):
        live, source, layer = place_ref[0, 3 + 3 * s], place_ref[0, 4 + 3 * s], place_ref[0, 5 + 3 * s]
        grad_total = jnp.sum(jnp.where(lane == layer, total, 0.0), keepdims=True)
        raw_total = jnp.sum(jnp.where(lane == layer + LAYERS, total, 0.0), keepdims=True)
        ratio = jnp.sqrt((grad_total + 1e-06) / (raw_total + 1e-06))
        ratio = jnp.where(live > 0, ratio, 0.0)
        step = jnp.where(live > 0, (me_x - source) & (groups - 1), groups)
        for number in range(groups):

            @pl.when(step == number)
            def _(number=number, s=s, ratio=ratio):
                block = raw_ref[0] if number == 0 else refs[number - 1][0]
                out_ref[s] = (block.astype(f32) * ratio).astype(bf16)

        @pl.when(step == groups)
        def _(s=s):
            out_ref[s] = jnp.zeros(out_ref.shape[1:], bf16)


def on_device(stats_partial, gradient, owner_of, layer_count):
    groups = lax.axis_size("dp")
    columns = lax.axis_size("z") * lax.axis_size("y")
    blocks = owner_of.shape[0]
    each = blocks // groups
    local_rows, order = gradient.shape[1:]
    quarter = order // groups
    chunk = order // 4
    struct = jax.ShapeDtypeStruct
    swap = [(0, 1), (1, 0)]

    stats = packed(stats_partial.reshape(2 * blocks, local_rows, order))
    out_shape = (2 * groups, each, 16, chunk)
    outgoing, order_info, place = pl.pallas_call(
        functools.partial(pack_stats_body, groups=groups, columns=columns),
        out_shape=(struct(out_shape, bf16), struct((1, blocks), i32), struct((1, 128), i32)),
        in_specs=[VMEM, SMEM, ANY],
        out_specs=(ANY, VMEM, VMEM),
        scratch_shapes=[
            pltpu.VMEM(stats.shape, f32),
            pltpu.VMEM(out_shape, bf16),
            pltpu.SMEM((1, blocks), i32),
            pltpu.SemaphoreType.DMA((2 + groups,)),
        ],
    )(owner_of[None], layer_count, stats)
    arrived = lax.all_to_all(outgoing, ("dp", "c"), 0, 0, tiled=True)
    grad = packed(gradient)
    grad_half = call(
        functools.partial(grad_half_body, groups=groups, blocks=blocks),
        struct((each, 8, chunk), bf16),
        [SMEM, VMEM],
    )(order_info, grad)
    grad_theirs = lax.ppermute(grad_half, "c", swap)
    summed = call(
        functools.partial(sum_stats_body, groups=groups, blocks=blocks),
        struct((columns, 48, chunk), bf16),
        [SMEM, VMEM, VMEM, VMEM],
    )(order_info, arrived, grad, grad_theirs)
    statistic = lax.all_to_all(summed, ("z", "y"), 0, 0, tiled=True)
    bundle_shape = (order + order // 2, order)
    bundle = call(
        newton_body, struct(bundle_shape, bf16), [VMEM], [pltpu.VMEM((order, order), f32)]
    )(statistic)
    other = lax.ppermute(bundle, "c", swap)
    raw, norms = call(
        raw_body,
        (struct((groups, quarter, order), bf16), struct((groups * columns, 1, LANES), f32)),
        [SMEM, ANY, ANY],
        [pltpu.VMEM((2, *bundle_shape), bf16), pltpu.SemaphoreType.DMA((2,))],
    )(place, bundle, other)
    norms = lax.all_to_all(norms, ("dp", "z", "y"), 0, 0, tiled=True)
    spread = []
    for step in range(1, groups):
        pairs = [(i, (i + step) % groups) for i in range(groups)]
        spread.append(lax.ppermute(raw[step : step + 1], "dp", pairs))
    own = raw[0:1]
    out = call(
        scale_body, struct((OCAP, quarter, order), bf16), [SMEM, VMEM] + [VMEM] * groups
    )(place, norms, own, *spread)
    return out[None]


def solution(mesh):
    shards = mesh.shape["shard"]
    side = 1
    while (2 * side) ** 2 * 2 <= shards:
        side *= 2
    torus = Mesh(
        mesh.devices.reshape(mesh.shape["dp"], shards // (2 * side), side, 2), ("dp", "z", "y", "c")
    )
    placed = (P("dp", None, None, SHARD, None), P(None, SHARD, None), P(), P())
    return jax.shard_map(
        on_device,
        mesh=torus,
        in_specs=placed,
        out_specs=P(SHARD, None, "dp", None),
        check_vma=False,
    )
```

time: 129 us -> 115 us (0.89)
  between operations: 7.66 us -> 0.1 us
  waiting for transfers between devices: 25.4 us -> 20 us
  blocking collectives: 28.9 us -> 33.3 us
  other arithmetic: 3.86 us -> 0 us
  starting transfers between devices: 38.2 us -> 36.7 us
    all_to_all x2 -> x1, waiting for transfers between devices: 18.3 us -> 0.01 us  [on_device(): norms = lax.all_to_all(norms, ('dp', 'z', 'y'), 0, 0, tiled=True)]
    ppermute x2 -> x5, waiting for transfers between devices: 1.14 us -> 10.1 us  [the longest x3 6.66 us: on_device(): spread.append(lax.ppermute(raw[step:step + 1], 'dp', pairs))]
    all_to_all x2 -> x1, starting transfers between devices: 18.8 us -> 10.3 us  [on_device(): norms = lax.all_to_all(norms, ('dp', 'z', 'y'), 0, 0, tiled=True)]
    ppermute x2 -> x5, starting transfers between devices: 9.11 us -> 16.1 us  [the longest x3 8.53 us: on_device(): spread.append(lax.ppermute(raw[step:step + 1], 'dp', pairs))]
    all_to_all x2 -> x1, blocking collectives: 28.9 us -> 33.3 us  [on_device(): statistic = lax.all_to_all(summed, ('z', 'y'), 0, 0, tiled=True)]
    all_to_all x1, waiting for transfers between devices: 6 us -> 9.87 us  [on_device(): arrived = lax.all_to_all(outgoing, ('dp', 'c'), 0, 0, tiled=True)]
    reduce_sum x4 -> x0, other arithmetic: 2.37 us -> none  [the longest x1 0.91 us: on_device(): jnp.sum(((owner_of[None, :] < owner_of[:, None]) | same & before).astype(...]
    slice x0 -> x1, local copies, waits for them, and re-layouts: none -> 1.78 us  [on_device(): spread.append(lax.ppermute(raw[step:step + 1], 'dp', pairs))]
  transfers between devices with their start and end apart: 5 -> 7, of which waited for: 4 -> 5; matrix products, arithmetic and copies ran while one was open for 1% -> 2% of each run, Pallas kernels for 6% -> 2%
where the time goes in v2:
time: 115 us
  starting transfers between devices  36.7 us (32%)
  blocking collectives  33.3 us (29%)
  Pallas kernels  20.1 us (17%)
  waiting for transfers between devices  20 us (17%)
  local copies, waits for them, and re-layouts  4.39 us (4%)
    all_to_all x1, blocking collectives, on_device(): statistic = lax.all_to_all(summed, ('z', 'y'), 0, 0, tiled=True)  33.3 us
    all_to_all x1, starting transfers between devices, on_device(): arrived = lax.all_to_all(outgoing, ('dp', 'c'), 0, 0, tiled=True)  10.3 us
    all_to_all x1, starting transfers between devices, on_device(): norms = lax.all_to_all(norms, ('dp', 'z', 'y'), 0, 0, tiled=True)  10.3 us
    all_to_all x1, waiting for transfers between devices, on_device(): arrived = lax.all_to_all(outgoing, ('dp', 'c'), 0, 0, tiled=True)  9.87 us
    ppermute x3, starting transfers between devices, on_device(): spread.append(lax.ppermute(raw[step:step + 1], 'dp', pairs))  8.53 us
    ppermute x3, waiting for transfers between devices, on_device(): spread.append(lax.ppermute(raw[step:step + 1], 'dp', pairs))  6.66 us
    ppermute x1, starting transfers between devices, on_device(): other = lax.ppermute(bundle, 'c', swap)  5.59 us
    pallas_call x1, Pallas kernels, on_device(): call(newton_body, struct(bundle_shape, bf16), [VMEM], [pltpu.VMEM((order,...  5.15 us
  transfers between devices with their start and end apart: 7, of which 5 were waited for; matrix products, arithmetic and copies ran while one was open for 2% of the time, Pallas kernels for 2%

profile of v2, /device:TPU:1, one launch (start us, length us, event | category | flops | bytes accessed | tf_op | source)
XLA Modules:
  0.0 114.5 jit_solution(17693186362438338903)
XLA Ops:
  0.0 4.3 %shard_map.46 = (bf16[8,32,16,128]{3,2,1,0:T(8,128)(2,1)}, s32[1,128]{1,0:T(1,128)}, s32[1,128]{1,0:T(1,128)}) custom-call(s32[1,128]{1,0:T(1,128)} %bitcast.15, s32[4]{0:T(128)} %count_ref.1, f32[256,16,128]{2,1,0:T(8,128)} %bitcast.12), custom_call_target="tpu_custom_call" | custom-call | tf_op jit(solution)/shard_map/pallas_call | solution.py:280
  4.3 10.3 %all-to-all-start = ((bf16[8,32,16,128]{3,2,1,0:T(8,128)(2,1)}), bf16[8,32,16,128]{3,2,1,0:T(8,128)(2,1)S(1)}, u32[]{:S(2)}, u32[]{:S(2)}) async-start(bf16[8,32,16,128]{3,2,1,0:T(8,128)(2,1)} %get-tuple-element.12), calls=%async_computation | async-start | bytes 2097152 | tf_op jit(solution)/shard_map/all_to_all | solution.py:292
  14.6 1.8 %shard_map.47 = bf16[32,8,128]{2,1,0:T(8,128)(2,1)} custom-call(s32[1,128]{1,0:T(1,128)} %get-tuple-element.11.order_ref, bf16[128,16,128]{2,1,0:T(8,128)(2,1)} %bitcast.13), custom_call_target="tpu_custom_call" | custom-call | tf_op jit(solution)/shard_map/pallas_call | solution.py:294
  16.4 2.0 %collective-permute-start = (bf16[32,8,128]{2,1,0:T(8,128)(2,1)}, bf16[32,8,128]{2,1,0:T(8,128)(2,1)S(1)}, u32[]{:S(2)}, u32[]{:S(2)}) collective-permute-start(bf16[32,8,128]{2,1,0:T(8,128)(2,1)} %shard_map.47), channel_id=1, source_target_pairs={{0,1},{1,0},{2,3},{3,2},{4,5},{5,4},{6,7},{7,6},{8,9},{9,8},{10,11... | collective-permute-start | bytes 196616 | tf_op jit(solution)/shard_map/ppermute | solution.py:299
  18.4 1.3 %collective-permute-done.theirs_ref = bf16[32,8,128]{2,1,0:T(8,128)(2,1)S(1)} collective-permute-done((bf16[32,8,128]{2,1,0:T(8,128)(2,1)}, bf16[32,8,128]{2,1,0:T(8,128)(2,1)S(1)}, u32[]{:S(2)}, u32[]{:S(2)}) %collective-permute-start) | collective-permute-done | bytes 65568 | tf_op jit(solution)/shard_map/ppermute | solution.py:299
  19.7 9.9 %all-to-all-done.got_ref = bf16[8,32,16,128]{3,2,1,0:T(8,128)(2,1)S(1)} async-done(((bf16[8,32,16,128]{3,2,1,0:T(8,128)(2,1)}), bf16[8,32,16,128]{3,2,1,0:T(8,128)(2,1)S(1)}, u32[]{:S(2)}, u32[]{:S(2)}) %all-to-all-start) | async-done | bytes 1048608 | tf_op jit(solution)/shard_map/all_to_all | solution.py:292
  29.6 1.0 copy-done
  30.6 2.6 %shard_map.48 = bf16[64,48,128]{2,1,0:T(8,128)(2,1)} custom-call(s32[1,128]{1,0:T(1,128)} %get-tuple-element.11.order_ref, bf16[8,32,16,128]{3,2,1,0:T(8,128)(2,1)} %copy-done, bf16[128,16,128]{2,1,0:T(8,128)(2,1)} %bitcast.14, bf16[32,8,128]{2,1,0:T(8,128)(2,1)} %copy-done.6), custom_call_target="tpu_custom_call" | custom-call | tf_op jit(solution)/shard_map/pallas_call | solution.py:300
  33.2 33.3 %all_to_all.15.got_ref = bf16[64,48,128]{2,1,0:T(8,128)(2,1)} all-to-all(bf16[64,48,128]{2,1,0:T(8,128)(2,1)} %shard_map.48), channel_id=1, replica_groups=mesh['dp'=4,'z'=8,'y'=8,'c'=2] {'z','y'}, dimensions={0} | all-to-all | bytes 1572864 | tf_op jit(solution)/shard_map/all_to_all | solution.py:305
  66.5 5.1 %shard_map.49.mine_ref = bf16[768,512]{1,0:T(8,128)(2,1)} custom-call(bf16[64,48,128]{2,1,0:T(8,128)(2,1)} %all_to_all.15.got_ref), custom_call_target="tpu_custom_call" | custom-call | tf_op jit(solution)/shard_map/pallas_call | solution.py:307
  71.7 5.6 %collective-permute-start.1 = (bf16[768,512]{1,0:T(8,128)(2,1)}, bf16[768,512]{1,0:T(8,128)(2,1)S(1)}, u32[]{:S(2)}, u32[]{:S(2)}) collective-permute-start(bf16[768,512]{1,0:T(8,128)(2,1)} %shard_map.49.mine_ref), channel_id=1, source_target_pairs={{0,1},{1,0},{2,3},{3,2},{4,5},{5,4},{6,7},{7,6},{8,9},{9,8},{10,11... | collective-permute-start | bytes 2359304 | tf_op jit(solution)/shard_map/ppermute | solution.py:310
  77.3 2.1 %collective-permute-done.1.other_ref = bf16[768,512]{1,0:T(8,128)(2,1)S(1)} collective-permute-done((bf16[768,512]{1,0:T(8,128)(2,1)}, bf16[768,512]{1,0:T(8,128)(2,1)S(1)}, u32[]{:S(2)}, u32[]{:S(2)}) %collective-permute-start.1) | collective-permute-done | bytes 786464 | tf_op jit(solution)/shard_map/ppermute | solution.py:310
  79.4 0.9 copy-done.1
  80.3 3.8 %shard_map.50 = (bf16[4,128,512]{2,1,0:T(8,128)(2,1)}, f32[256,1,128]{2,1,0:T(1,128)}) custom-call(s32[1,128]{1,0:T(1,128)} %get-tuple-element.10.place_ref, bf16[768,512]{1,0:T(8,128)(2,1)} %shard_map.49.mine_ref, bf16[768,512]{1,0:T(8,128)(2,1)} %copy-done.1), custom_call_target="tpu_custom_call" | custom-call | tf_op jit(solution)/shard_map/pallas_call | solution.py:311
  84.1 10.3 %all-to-all-start.2 = ((f32[256,1,128]{2,1,0:T(1,128)}), f32[256,1,128]{2,1,0:T(1,128)S(1)}, u32[]{:S(2)}, u32[]{:S(2)}) async-start(f32[256,1,128]{2,1,0:T(1,128)} %get-tuple-element.13), calls=%async_computation.2 | async-start | bytes 262144 | tf_op jit(solution)/shard_map/all_to_all | solution.py:317
  94.4 1.8 %fusion = (bf16[1,128,512]{2,1,0:T(8,128)(2,1)S(1)}, bf16[1,128,512]{2,1,0:T(8,128)(2,1)S(1)}, bf16[1,128,512]{2,1,0:T(8,128)(2,1)S(1)}, bf16[1,128,512]{2,1,0:T(8,128)(2,1)}) fusion(bf16[4,128,512]{2,1,0:T(8,128)(2,1)} %get-tuple-element.14), kind=kLoop, calls=%fused_computation | loop fusion | bytes 1048576 | tf_op jit(solution)/shard_map/slice | solution.py:321
  96.2 4.0 %collective-permute-start.4 = (bf16[1,128,512]{2,1,0:T(8,128)(2,1)S(1)}, bf16[1,128,512]{2,1,0:T(8,128)(2,1)S(1)}, u32[]{:S(2)}, u32[]{:S(2)}) collective-permute-start(bf16[1,128,512]{2,1,0:T(8,128)(2,1)S(1)} %get-tuple-element.15), channel_id=1, source_target_pairs={{0,384},{128,0},{256,128},{384,256},{1,385},{129,1},{257,129},{385... | collective-permute-start | bytes 393224 | tf_op jit(solution)/shard_map/ppermute | solution.py:321
  100.2 1.9 %collective-permute-start.3 = (bf16[1,128,512]{2,1,0:T(8,128)(2,1)S(1)}, bf16[1,128,512]{2,1,0:T(8,128)(2,1)S(1)}, u32[]{:S(2)}, u32[]{:S(2)}) collective-permute-start(bf16[1,128,512]{2,1,0:T(8,128)(2,1)S(1)} %get-tuple-element.16), channel_id=1, source_target_pairs={{0,256},{128,384},{256,0},{384,128},{1,257},{129,385},{257,1},{385... | collective-permute-start | bytes 393224 | tf_op jit(solution)/shard_map/ppermute | solution.py:321
  102.1 2.6 %collective-permute-start.2 = (bf16[1,128,512]{2,1,0:T(8,128)(2,1)S(1)}, bf16[1,128,512]{2,1,0:T(8,128)(2,1)S(1)}, u32[]{:S(2)}, u32[]{:S(2)}) collective-permute-start(bf16[1,128,512]{2,1,0:T(8,128)(2,1)S(1)} %get-tuple-element.17), channel_id=1, source_target_pairs={{0,128},{128,256},{256,384},{384,0},{1,129},{129,257},{257,385},{3... | collective-permute-start | bytes 393224 | tf_op jit(solution)/shard_map/ppermute | solution.py:321
  104.7 3.0 %collective-permute-done.3.refs_1_ = bf16[1,128,512]{2,1,0:T(8,128)(2,1)S(1)} collective-permute-done((bf16[1,128,512]{2,1,0:T(8,128)(2,1)S(1)}, bf16[1,128,512]{2,1,0:T(8,128)(2,1)S(1)}, u32[]{:S(2)}, u32[]{:S(2)}) %collective-permute-start.3) | collective-permute-done | bytes 131104 | tf_op jit(solution)/shard_map/ppermute | solution.py:321
  107.7 3.7 %collective-permute-done.2.refs_0_ = bf16[1,128,512]{2,1,0:T(8,128)(2,1)S(1)} collective-permute-done((bf16[1,128,512]{2,1,0:T(8,128)(2,1)S(1)}, bf16[1,128,512]{2,1,0:T(8,128)(2,1)S(1)}, u32[]{:S(2)}, u32[]{:S(2)}) %collective-permute-start.2) | collective-permute-done | bytes 131104 | tf_op jit(solution)/shard_map/ppermute | solution.py:321
  111.4 0.6 copy-done.5
  112.0 0.1 copy-done.2
  112.1 2.5 %shard_map.51 = bf16[2,128,512]{2,1,0:T(8,128)(2,1)} custom-call(s32[1,128]{1,0:T(1,128)} %get-tuple-element.10.place_ref, f32[256,1,128]{2,1,0:T(1,128)} %copy-done.2, bf16[1,128,512]{2,1,0:T(8,128)(2,1)} %get-tuple-element.18.raw_ref, bf16[1,128,512]{2,1,0:T(8,128)(2,1)} %copy-done.5, bf16[1,128,512]{2,1,0:T(8,128)(2,1)} %copy-done.4, ...), custom_call_target="tpu_custom_call" | custom-call | tf_op jit(solution)/shard_map/pallas_call | solution.py:323
  (12 shorter events, 0.0 us)
Async XLA Ops:
  4.3 25.3 %all-to-all-start = ((bf16[8,32,16,128]{3,2,1,0:T(8,128)(2,1)}), bf16[8,32,16,128]{3,2,1,0:T(8,128)(2,1)S(1)}, u32[]{:S(2)}, u32[]{:S(2)}) async-start(bf16[8,32,16,128]{3,2,1,0:T(8,128)(2,1)} %get-tuple-element.12), calls=%async_computation | async-start | bytes 2097152 | tf_op jit(solution)/shard_map/all_to_all | solution.py:292
  16.4 3.3 %collective-permute-start = (bf16[32,8,128]{2,1,0:T(8,128)(2,1)}, bf16[32,8,128]{2,1,0:T(8,128)(2,1)S(1)}, u32[]{:S(2)}, u32[]{:S(2)}) collective-permute-start(bf16[32,8,128]{2,1,0:T(8,128)(2,1)} %shard_map.47), channel_id=1, source_target_pairs={{0,1},{1,0},{2,3},{3,2},{4,5},{5,4},{6,7},{7,6},{8,9},{9,8},{10,11... | collective-permute-start | bytes 196616 | tf_op jit(solution)/shard_map/ppermute | solution.py:299
  19.7 9.9 %copy-start.6 = (bf16[32,8,128]{2,1,0:T(8,128)(2,1)}, bf16[32,8,128]{2,1,0:T(8,128)(2,1)S(1)}, u32[]{:S(2)}) copy-start(bf16[32,8,128]{2,1,0:T(8,128)(2,1)S(1)} %collective-permute-done.theirs_ref) | copy-start | bytes 196612
  29.6 1.0 copy-start
  71.7 7.7 %collective-permute-start.1 = (bf16[768,512]{1,0:T(8,128)(2,1)}, bf16[768,512]{1,0:T(8,128)(2,1)S(1)}, u32[]{:S(2)}, u32[]{:S(2)}) collective-permute-start(bf16[768,512]{1,0:T(8,128)(2,1)} %shard_map.49.mine_ref), channel_id=1, source_target_pairs={{0,1},{1,0},{2,3},{3,2},{4,5},{5,4},{6,7},{7,6},{8,9},{9,8},{10,11... | collective-permute-start | bytes 2359304 | tf_op jit(solution)/shard_map/ppermute | solution.py:310
  79.4 0.9 copy-start.1
  84.1 27.3 %all-to-all-start.2 = ((f32[256,1,128]{2,1,0:T(1,128)}), f32[256,1,128]{2,1,0:T(1,128)S(1)}, u32[]{:S(2)}, u32[]{:S(2)}) async-start(f32[256,1,128]{2,1,0:T(1,128)} %get-tuple-element.13), calls=%async_computation.2 | async-start | bytes 262144 | tf_op jit(solution)/shard_map/all_to_all | solution.py:317
  96.2 8.6 %collective-permute-start.4 = (bf16[1,128,512]{2,1,0:T(8,128)(2,1)S(1)}, bf16[1,128,512]{2,1,0:T(8,128)(2,1)S(1)}, u32[]{:S(2)}, u32[]{:S(2)}) collective-permute-start(bf16[1,128,512]{2,1,0:T(8,128)(2,1)S(1)} %get-tuple-element.15), channel_id=1, source_target_pairs={{0,384},{128,0},{256,128},{384,256},{1,385},{129,1},{257,129},{385... | collective-permute-start | bytes 393224 | tf_op jit(solution)/shard_map/ppermute | solution.py:321
  100.2 7.6 %collective-permute-start.3 = (bf16[1,128,512]{2,1,0:T(8,128)(2,1)S(1)}, bf16[1,128,512]{2,1,0:T(8,128)(2,1)S(1)}, u32[]{:S(2)}, u32[]{:S(2)}) collective-permute-start(bf16[1,128,512]{2,1,0:T(8,128)(2,1)S(1)} %get-tuple-element.16), channel_id=1, source_target_pairs={{0,256},{128,384},{256,0},{384,128},{1,257},{129,385},{257,1},{385... | collective-permute-start | bytes 393224 | tf_op jit(solution)/shard_map/ppermute | solution.py:321
  102.1 9.3 %collective-permute-start.2 = (bf16[1,128,512]{2,1,0:T(8,128)(2,1)S(1)}, bf16[1,128,512]{2,1,0:T(8,128)(2,1)S(1)}, u32[]{:S(2)}, u32[]{:S(2)}) collective-permute-start(bf16[1,128,512]{2,1,0:T(8,128)(2,1)S(1)} %get-tuple-element.17), channel_id=1, source_target_pairs={{0,128},{128,256},{256,384},{384,0},{1,129},{129,257},{257,385},{3... | collective-permute-start | bytes 393224 | tf_op jit(solution)/shard_map/ppermute | solution.py:321
  104.7 6.7 %copy-start.3 = (bf16[1,128,512]{2,1,0:T(8,128)(2,1)}, bf16[1,128,512]{2,1,0:T(8,128)(2,1)S(1)}, u32[]{:S(2)}) copy-start(bf16[1,128,512]{2,1,0:T(8,128)(2,1)S(1)} %collective-permute-done.4.refs_2_) | copy-start | bytes 393220
  107.7 3.7 %copy-start.4 = (bf16[1,128,512]{2,1,0:T(8,128)(2,1)}, bf16[1,128,512]{2,1,0:T(8,128)(2,1)S(1)}, u32[]{:S(2)}) copy-start(bf16[1,128,512]{2,1,0:T(8,128)(2,1)S(1)} %collective-permute-done.3.refs_1_) | copy-start | bytes 393220
  111.4 0.6 copy-start.5
  111.4 0.7 copy-start.2

commit v3 on v2

--- a/solution.py
+++ b/solution.py
@@ -25,13 +25,22 @@
     return size.bit_length() - 1
 
 
-def call(body, out_shape, in_specs, scratch=()):
+def held(x):
+    return pltpu.with_memory_space_constraint(x, pltpu.VMEM)
+
+
+def in_hbm(x):
+    return pltpu.with_memory_space_constraint(x, pltpu.HBM)
+
+
+def call(body, out_shape, in_specs, scratch=(), out_specs=None):
     return pl.pallas_call(
         body,
         out_shape=out_shape,
         in_specs=in_specs,
-        out_specs=jax.tree.map(lambda _: VMEM, out_shape),
+        out_specs=VMEM if out_specs is None else out_specs,
         scratch_shapes=list(scratch),
+        compiler_params=pltpu.CompilerParams(vmem_limit_bytes=24 * 2**20),
     )
 
 
@@ -90,7 +99,7 @@
 
 
 def pack_stats_body(
-    owner_ref, count_ref, stats_ref, out_ref, sorted_ref, place_ref, stats_vmem, out_vmem, order_ref, sems, *, groups, columns
+    owner_ref, count_ref, stats_ref, out_ref, sorted_ref, place_ref, stats_vmem, order_ref, sems, *, groups, columns
 ):
     blocks = owner_ref.shape[1]
     each = out_ref.shape[1]
@@ -101,7 +110,6 @@
     move.start()
     move.wait()
     load.wait()
-    stores = []
     for x in range(groups):
 
         def step(k, carry, x=x):
@@ -109,15 +117,10 @@
             block = info & (blocks - 1)
             core = (info >> bits(blocks)) & 1
             for c in range(2):
-                out_vmem[x * 2 + c, k] = stats_vmem[2 * block + (core ^ c)].astype(bf16)
+                out_ref[x * 2 + c, k] = stats_vmem[2 * block + (core ^ c)].astype(bf16)
             return carry
 
         lax.fori_loop(0, each, step, 0, unroll=8 if each % 8 == 0 else 1)
-        part = slice(2 * x, 2 * x + 2)
-        stores.append(pltpu.make_async_copy(out_vmem.at[part], out_ref.at[part], sems.at[2 + x]))
-        stores[-1].start()
-    for store in stores:
-        store.wait()
 
 
 def grad_half_body(order_ref, grad_ref, out_ref, *, groups, blocks):
@@ -205,10 +208,12 @@
     out_ref[0:order] = (x * (1.0 / jnp.sqrt(jnp.sqrt(magnitude)))).astype(bf16)
 
 
-def raw_body(place_ref, mine_ref, other_ref, out_ref, norm_ref, both_ref, sems):
-    quarter = out_ref.shape[1]
+def raw_body(place_ref, mine_ref, other_ref, *refs):
+    norm_ref, both_ref, raw_ref, sems = refs[-4:]
+    out_refs = refs[:-4]
+    groups = len(out_refs)
     order = mine_ref.shape[1]
-    half = order // 2
+    half, quarter = order // 2, order // groups
     live, core, layer = place_ref[0, 0], place_ref[0, 1], place_ref[0, 2]
     me_c, me_x = lax.axis_index("c"), lax.axis_index("dp")
     loads = [
@@ -234,9 +239,10 @@
     norms = jnp.where(lane == layer, grad_sq, 0.0) + jnp.where(lane == layer + LAYERS, raw_sq, 0.0)
     norms = jnp.where(live > 0, norms, 0.0)
     norm_ref[...] = jnp.broadcast_to(norms[:, None, :], norm_ref.shape)
-    groups = out_ref.shape[0]
-    for x in range(groups):
-        out_ref[(x - me_x) & (groups - 1)] = raw[x * quarter : (x + 1) * quarter].astype(bf16)
+    raw_ref[...] = raw.astype(bf16)
+    for number, out_ref in enumerate(out_refs):
+        start = ((me_x + number) & (groups - 1)) * quarter
+        out_ref[...] = raw_ref[pl.ds(pl.multiple_of(start, quarter), quarter), :]
 
 
 def scale_body(place_ref, norm_ref, raw_ref, *refs):
@@ -256,7 +262,7 @@
 
             @pl.when(step == number)
             def _(number=number, s=s, ratio=ratio):
-                block = raw_ref[0] if number == 0 else refs[number - 1][0]
+                block = raw_ref[...] if number == 0 else refs[number - 1][...]
                 out_ref[s] = (block.astype(f32) * ratio).astype(bf16)
 
         @pl.when(step == groups)
@@ -277,52 +283,56 @@
 
     stats = packed(stats_partial.reshape(2 * blocks, local_rows, order))
     out_shape = (2 * groups, each, 16, chunk)
-    outgoing, order_info, place = pl.pallas_call(
+    outgoing, order_info, place = call(
         functools.partial(pack_stats_body, groups=groups, columns=columns),
-        out_shape=(struct(out_shape, bf16), struct((1, blocks), i32), struct((1, 128), i32)),
-        in_specs=[VMEM, SMEM, ANY],
-        out_specs=(ANY, VMEM, VMEM),
-        scratch_shapes=[
+        (pltpu.VMEM(out_shape, bf16), struct((1, blocks), i32), struct((1, 128), i32)),
+        [VMEM, SMEM, ANY],
+        [
             pltpu.VMEM(stats.shape, f32),
-            pltpu.VMEM(out_shape, bf16),
             pltpu.SMEM((1, blocks), i32),
-            pltpu.SemaphoreType.DMA((2 + groups,)),
+            pltpu.SemaphoreType.DMA((2,)),
         ],
-    )(owner_of[None], layer_count, stats)
+        (VMEM, VMEM, VMEM),
+    )(in_hbm(owner_of[None]), in_hbm(layer_count), in_hbm(stats))
     arrived = lax.all_to_all(outgoing, ("dp", "c"), 0, 0, tiled=True)
     grad = packed(gradient)
     grad_half = call(
         functools.partial(grad_half_body, groups=groups, blocks=blocks),
-        struct((each, 8, chunk), bf16),
+        pltpu.VMEM((each, 8, chunk), bf16),
         [SMEM, VMEM],
     )(order_info, grad)
     grad_theirs = lax.ppermute(grad_half, "c", swap)
     summed = call(
         functools.partial(sum_stats_body, groups=groups, blocks=blocks),
-        struct((columns, 48, chunk), bf16),
+        pltpu.VMEM((columns, 48, chunk), bf16),
         [SMEM, VMEM, VMEM, VMEM],
-    )(order_info, arrived, grad, grad_theirs)
+    )(order_info, held(arrived), grad, held(grad_theirs))
     statistic = lax.all_to_all(summed, ("z", "y"), 0, 0, tiled=True)
     bundle_shape = (order + order // 2, order)
     bundle = call(
-        newton_body, struct(bundle_shape, bf16), [VMEM], [pltpu.VMEM((order, order), f32)]
-    )(statistic)
+        newton_body, pltpu.VMEM(bundle_shape, bf16), [VMEM], [pltpu.VMEM((order, order), f32)]
+    )(held(statistic))
     other = lax.ppermute(bundle, "c", swap)
-    raw, norms = call(
+    *quarters, norms = call(
         raw_body,
-        (struct((groups, quarter, order), bf16), struct((groups * columns, 1, LANES), f32)),
+        tuple(pltpu.VMEM((quarter, order), bf16) for _ in range(groups))
+        + (pltpu.VMEM((groups * columns, 1, LANES), f32),),
         [SMEM, ANY, ANY],
-        [pltpu.VMEM((2, *bundle_shape), bf16), pltpu.SemaphoreType.DMA((2,))],
-    )(place, bundle, other)
+        [
+            pltpu.VMEM((2, *bundle_shape), bf16),
+            pltpu.VMEM((order, order), bf16),
+            pltpu.SemaphoreType.DMA((2,)),
+        ],
+        (VMEM,) * (groups + 1),
+    )(place, held(bundle), held(other))
     norms = lax.all_to_all(norms, ("dp", "z", "y"), 0, 0, tiled=True)
-    spread = []
+    spread = [held(quarters[0])]
     for step in range(1, groups):
         pairs = [(i, (i + step) % groups) for i in range(groups)]
-        spread.append(lax.ppermute(raw[step : step + 1], "dp", pairs))
-    own = raw[0:1]
+        spread.append(held(lax.ppermute(quarters[step], "dp", pairs)))
     out = call(
-        scale_body, struct((OCAP, quarter, order), bf16), [SMEM, VMEM] + [VMEM] * groups
-    )(place, norms, own, *spread)
+        scale_body, struct((OCAP, quarter, order), bf16), [SMEM] + [VMEM] * (groups + 1)
+    )(place, held(norms), *spread)
     return out[None]
 
 

time: 115 us -> 103 us (0.90)
  Pallas kernels: 20.1 us -> 12.9 us
  local copies, waits for them, and re-layouts: 4.39 us -> 0.01 us
  waiting for transfers between devices: 20 us -> 17.5 us
  starting transfers between devices: 36.7 us -> 38 us
    pallas_call x6, Pallas kernels: 20.1 us -> 12.9 us  [the longest x1 3.92 us: on_device(): call(functools.partial(pack_stats_body, groups=groups, columns=columns),...]
    ppermute x3, waiting for transfers between devices: 6.66 us -> 3.34 us  [on_device(): spread.append(held(lax.ppermute(quarters[step], 'dp', pairs)))]
    unnamed x14 -> x2, local copies, waits for them, and re-layouts: 2.6 us -> 0.01 us
    slice x1 -> x0, local copies, waits for them, and re-layouts: 1.78 us -> none  [on_device(): spread.append(lax.ppermute(raw[step:step + 1], 'dp', pairs))]
    all_to_all x1, waiting for transfers between devices: 9.87 us -> 11.2 us  [on_device(): arrived = lax.all_to_all(outgoing, ('dp', 'c'), 0, 0, tiled=True)]
    ppermute x3, starting transfers between devices: 8.53 us -> 9.75 us  [on_device(): spread.append(held(lax.ppermute(quarters[step], 'dp', pairs)))]
  transfers between devices with their start and end apart: 7 -> 7, of which waited for: 5 -> 5; matrix products, arithmetic and copies ran while one was open for 2% -> 0% of each run, Pallas kernels for 2% -> 1%
where the time goes in v3:
time: 103 us; the launch traced here: 102 us
  starting transfers between devices  38 us (37%)
  blocking collectives  33 us (32%)
  waiting for transfers between devices  17.5 us (17%)
  Pallas kernels  12.9 us (13%)
    all_to_all x1, blocking collectives, on_device(): statistic = lax.all_to_all(summed, ('z', 'y'), 0, 0, tiled=True)  33 us
    all_to_all x1, waiting for transfers between devices, on_device(): arrived = lax.all_to_all(outgoing, ('dp', 'c'), 0, 0, tiled=True)  11.2 us
    all_to_all x1, starting transfers between devices, on_device(): arrived = lax.all_to_all(outgoing, ('dp', 'c'), 0, 0, tiled=True)  10.3 us
    all_to_all x1, starting transfers between devices, on_device(): norms = lax.all_to_all(norms, ('dp', 'z', 'y'), 0, 0, tiled=True)  10.3 us
    ppermute x3, starting transfers between devices, on_device(): spread.append(held(lax.ppermute(quarters[step], 'dp', pairs)))  9.75 us
    ppermute x1, starting transfers between devices, on_device(): other = lax.ppermute(bundle, 'c', swap)  5.6 us
    pallas_call x1, Pallas kernels, on_device(): call(functools.partial(pack_stats_body, groups=groups, columns=columns),...  3.92 us
    ppermute x3, waiting for transfers between devices, on_device(): spread.append(held(lax.ppermute(quarters[step], 'dp', pairs)))  3.34 us
  transfers between devices with their start and end apart: 7, of which 5 were waited for; matrix products, arithmetic and copies ran while one was open for 0% of the time, Pallas kernels for 1%

profile of v3, /device:TPU:1, one launch (start us, length us, event | category | flops | bytes accessed | tf_op | source)
XLA Modules:
  0.0 101.5 jit_solution(2891030338975060397)
XLA Ops:
  0.0 0.0 copy-start
  0.0 3.9 %shard_map.46 = (bf16[8,32,16,128]{3,2,1,0:T(8,128)(2,1)}, s32[1,128]{1,0:T(1,128)S(1)}, s32[1,128]{1,0:T(1,128)S(1)}) custom-call(s32[1,128]{1,0:T(1,128)} %bitcast.15, s32[4]{0:T(128)} %count_ref.1, f32[256,16,128]{2,1,0:T(8,128)} %bitcast.14), custom_call_target="tpu_custom_call" | custom-call | tf_op jit(solution)/shard_map/pallas_call | solution.py:286
  3.9 10.3 %all-to-all-start = ((bf16[8,32,16,128]{3,2,1,0:T(8,128)(2,1)}), bf16[8,32,16,128]{3,2,1,0:T(8,128)(2,1)S(1)}, u32[]{:S(2)}, u32[]{:S(2)}) async-start(bf16[8,32,16,128]{3,2,1,0:T(8,128)(2,1)} %get-tuple-element.15), calls=%async_computation | async-start | bytes 2097152 | tf_op jit(solution)/shard_map/all_to_all | solution.py:297
  14.2 0.0 copy-done
  14.2 0.6 shard_map.47
  14.9 2.0 %collective-permute-start = (bf16[32,8,128]{2,1,0:T(8,128)(2,1)S(1)}, bf16[32,8,128]{2,1,0:T(8,128)(2,1)S(1)}, u32[]{:S(2)}, u32[]{:S(2)}) collective-permute-start(bf16[32,8,128]{2,1,0:T(8,128)(2,1)S(1)} %shard_map.47), channel_id=1, source_target_pairs={{0,1},{1,0},{2,3},{3,2},{4,5},{5,4},{6,7},{7,6},{8,9},{9,8},{10,11... | collective-permute-start | bytes 196616 | tf_op jit(solution)/shard_map/ppermute | solution.py:304
  16.9 1.1 %collective-permute-done.theirs_ref = bf16[32,8,128]{2,1,0:T(8,128)(2,1)S(1)} collective-permute-done((bf16[32,8,128]{2,1,0:T(8,128)(2,1)S(1)}, bf16[32,8,128]{2,1,0:T(8,128)(2,1)S(1)}, u32[]{:S(2)}, u32[]{:S(2)}) %collective-permute-start) | collective-permute-done | bytes 65568 | tf_op jit(solution)/shard_map/ppermute | solution.py:304
  18.0 11.2 %all-to-all-done.got_ref = bf16[8,32,16,128]{3,2,1,0:T(8,128)(2,1)S(1)} async-done(((bf16[8,32,16,128]{3,2,1,0:T(8,128)(2,1)}), bf16[8,32,16,128]{3,2,1,0:T(8,128)(2,1)S(1)}, u32[]{:S(2)}, u32[]{:S(2)}) %all-to-all-start) | async-done | bytes 1048608 | tf_op jit(solution)/shard_map/all_to_all | solution.py:297
  29.2 0.9 shard_map.48
  30.1 33.0 %all_to_all.15.got_ref = bf16[64,48,128]{2,1,0:T(8,128)(2,1)S(1)} all-to-all(bf16[64,48,128]{2,1,0:T(8,128)(2,1)S(1)} %shard_map.48), channel_id=1, replica_groups=mesh['dp'=4,'z'=8,'y'=8,'c'=2] {'z','y'}, dimensions={0} | all-to-all | bytes 1572864 | tf_op jit(solution)/shard_map/all_to_all | solution.py:310
  63.1 3.2 %shard_map.49.mine_ref = bf16[768,512]{1,0:T(8,128)(2,1)S(1)} custom-call(bf16[64,48,128]{2,1,0:T(8,128)(2,1)S(1)} %all_to_all.15.got_ref), custom_call_target="tpu_custom_call" | custom-call | tf_op jit(solution)/shard_map/pallas_call | solution.py:312
  66.3 5.6 %collective-permute-start.1 = (bf16[768,512]{1,0:T(8,128)(2,1)S(1)}, bf16[768,512]{1,0:T(8,128)(2,1)S(1)}, u32[]{:S(2)}, u32[]{:S(2)}) collective-permute-start(bf16[768,512]{1,0:T(8,128)(2,1)S(1)} %shard_map.49.mine_ref), channel_id=1, source_target_pairs={{0,1},{1,0},{2,3},{3,2},{4,5},{5,4},{6,7},{7,6},{8,9},{9,8},{10,11... | collective-permute-start | bytes 2359304 | tf_op jit(solution)/shard_map/ppermute | solution.py:315
  71.9 1.9 %collective-permute-done.1.other_ref = bf16[768,512]{1,0:T(8,128)(2,1)S(1)} collective-permute-done((bf16[768,512]{1,0:T(8,128)(2,1)S(1)}, bf16[768,512]{1,0:T(8,128)(2,1)S(1)}, u32[]{:S(2)}, u32[]{:S(2)}) %collective-permute-start.1) | collective-permute-done | bytes 786464 | tf_op jit(solution)/shard_map/ppermute | solution.py:315
  73.8 2.5 %shard_map.50 = (bf16[128,512]{1,0:T(8,128)(2,1)S(1)}, bf16[128,512]{1,0:T(8,128)(2,1)S(1)}, bf16[128,512]{1,0:T(8,128)(2,1)S(1)}, bf16[128,512]{1,0:T(8,128)(2,1)S(1)}, f32[256,1,128]{2,1,0:T(1,128)}) custom-call(s32[1,128]{1,0:T(1,128)S(1)} %get-tuple-element.13.place_ref, bf16[768,512]{1,0:T(8,128)(2,1)S(1)} %shard_map.49.mine_ref, ...), custom_call_target="tpu_custom_call" | custom-call | tf_op jit(solution)/shard_map/pallas_call | solution.py:316
  76.3 10.3 %all-to-all-start.2 = ((f32[256,1,128]{2,1,0:T(1,128)}), f32[256,1,128]{2,1,0:T(1,128)S(1)}, u32[]{:S(2)}, u32[]{:S(2)}) async-start(f32[256,1,128]{2,1,0:T(1,128)} %get-tuple-element.16), calls=%async_computation.2 | async-start | bytes 262144 | tf_op jit(solution)/shard_map/all_to_all | solution.py:328
  86.6 1.9 %collective-permute-start.2 = (bf16[128,512]{1,0:T(8,128)(2,1)S(1)}, bf16[128,512]{1,0:T(8,128)(2,1)S(1)}, u32[]{:S(2)}, u32[]{:S(2)}) collective-permute-start(bf16[128,512]{1,0:T(8,128)(2,1)S(1)} %get-tuple-element.18), channel_id=1, source_target_pairs={{0,128},{128,256},{256,384},{384,0},{1,129},{129,257},{257,385},{3... | collective-permute-start | bytes 393224 | tf_op jit(solution)/shard_map/ppermute | solution.py:332
  88.5 5.2 %collective-permute-start.3 = (bf16[128,512]{1,0:T(8,128)(2,1)S(1)}, bf16[128,512]{1,0:T(8,128)(2,1)S(1)}, u32[]{:S(2)}, u32[]{:S(2)}) collective-permute-start(bf16[128,512]{1,0:T(8,128)(2,1)S(1)} %get-tuple-element.19), channel_id=1, source_target_pairs={{0,256},{128,384},{256,0},{384,128},{1,257},{129,385},{257,1},{385... | collective-permute-start | bytes 393224 | tf_op jit(solution)/shard_map/ppermute | solution.py:332
  93.7 2.7 %collective-permute-start.4 = (bf16[128,512]{1,0:T(8,128)(2,1)S(1)}, bf16[128,512]{1,0:T(8,128)(2,1)S(1)}, u32[]{:S(2)}, u32[]{:S(2)}) collective-permute-start(bf16[128,512]{1,0:T(8,128)(2,1)S(1)} %get-tuple-element.20), channel_id=1, source_target_pairs={{0,384},{128,0},{256,128},{384,256},{1,385},{129,1},{257,129},{385... | collective-permute-start | bytes 393224 | tf_op jit(solution)/shard_map/ppermute | solution.py:332
  96.3 0.0 collective-permute-done.2.refs_0_
  96.3 2.1 %collective-permute-done.3.refs_1_ = bf16[128,512]{1,0:T(8,128)(2,1)S(1)} collective-permute-done((bf16[128,512]{1,0:T(8,128)(2,1)S(1)}, bf16[128,512]{1,0:T(8,128)(2,1)S(1)}, u32[]{:S(2)}, u32[]{:S(2)}) %collective-permute-start.3) | collective-permute-done | bytes 131104 | tf_op jit(solution)/shard_map/ppermute | solution.py:332
  98.4 1.2 %collective-permute-done.4.refs_2_ = bf16[128,512]{1,0:T(8,128)(2,1)S(1)} collective-permute-done((bf16[128,512]{1,0:T(8,128)(2,1)S(1)}, bf16[128,512]{1,0:T(8,128)(2,1)S(1)}, u32[]{:S(2)}, u32[]{:S(2)}) %collective-permute-start.4) | collective-permute-done | bytes 131104 | tf_op jit(solution)/shard_map/ppermute | solution.py:332
  99.7 0.0 all-to-all-done.2.norm_ref
  99.7 1.8 %shard_map.51 = bf16[2,128,512]{2,1,0:T(8,128)(2,1)} custom-call(s32[1,128]{1,0:T(1,128)S(1)} %get-tuple-element.13.place_ref, f32[256,1,128]{2,1,0:T(1,128)S(1)} %all-to-all-done.2.norm_ref, bf16[128,512]{1,0:T(8,128)(2,1)S(1)} %get-tuple-element.17.raw_ref, bf16[128,512]{1,0:T(8,128)(2,1)S(1)} %collective-permute-done.2.refs_0_, ...), custom_call_target="tpu_custom_call" | custom-call | tf_op jit(solution)/shard_map/pallas_call | solution.py:333
Async XLA Ops:
  0.0 14.2 %copy-start = (bf16[128,4,512]{2,1,0:T(4,128)(2,1)S(1)}, bf16[128,4,512]{2,1,0:T(4,128)(2,1)}, u32[]{:S(2)}) copy-start(bf16[128,4,512]{2,1,0:T(4,128)(2,1)} %param.5) | copy-start | bytes 1572868
  3.9 25.3 %all-to-all-start = ((bf16[8,32,16,128]{3,2,1,0:T(8,128)(2,1)}), bf16[8,32,16,128]{3,2,1,0:T(8,128)(2,1)S(1)}, u32[]{:S(2)}, u32[]{:S(2)}) async-start(bf16[8,32,16,128]{3,2,1,0:T(8,128)(2,1)} %get-tuple-element.15), calls=%async_computation | async-start | bytes 2097152 | tf_op jit(solution)/shard_map/all_to_all | solution.py:297
  14.9 3.1 %collective-permute-start = (bf16[32,8,128]{2,1,0:T(8,128)(2,1)S(1)}, bf16[32,8,128]{2,1,0:T(8,128)(2,1)S(1)}, u32[]{:S(2)}, u32[]{:S(2)}) collective-permute-start(bf16[32,8,128]{2,1,0:T(8,128)(2,1)S(1)} %shard_map.47), channel_id=1, source_target_pairs={{0,1},{1,0},{2,3},{3,2},{4,5},{5,4},{6,7},{7,6},{8,9},{9,8},{10,11... | collective-permute-start | bytes 196616 | tf_op jit(solution)/shard_map/ppermute | solution.py:304
  66.3 7.5 %collective-permute-start.1 = (bf16[768,512]{1,0:T(8,128)(2,1)S(1)}, bf16[768,512]{1,0:T(8,128)(2,1)S(1)}, u32[]{:S(2)}, u32[]{:S(2)}) collective-permute-start(bf16[768,512]{1,0:T(8,128)(2,1)S(1)} %shard_map.49.mine_ref), channel_id=1, source_target_pairs={{0,1},{1,0},{2,3},{3,2},{4,5},{5,4},{6,7},{7,6},{8,9},{9,8},{10,11... | collective-permute-start | bytes 2359304 | tf_op jit(solution)/shard_map/ppermute | solution.py:315
  76.3 23.4 %all-to-all-start.2 = ((f32[256,1,128]{2,1,0:T(1,128)}), f32[256,1,128]{2,1,0:T(1,128)S(1)}, u32[]{:S(2)}, u32[]{:S(2)}) async-start(f32[256,1,128]{2,1,0:T(1,128)} %get-tuple-element.16), calls=%async_computation.2 | async-start | bytes 262144 | tf_op jit(solution)/shard_map/all_to_all | solution.py:328
  86.6 9.8 %collective-permute-start.2 = (bf16[128,512]{1,0:T(8,128)(2,1)S(1)}, bf16[128,512]{1,0:T(8,128)(2,1)S(1)}, u32[]{:S(2)}, u32[]{:S(2)}) collective-permute-start(bf16[128,512]{1,0:T(8,128)(2,1)S(1)} %get-tuple-element.18), channel_id=1, source_target_pairs={{0,128},{128,256},{256,384},{384,0},{1,129},{129,257},{257,385},{3... | collective-permute-start | bytes 393224 | tf_op jit(solution)/shard_map/ppermute | solution.py:332
  88.5 9.9 %collective-permute-start.3 = (bf16[128,512]{1,0:T(8,128)(2,1)S(1)}, bf16[128,512]{1,0:T(8,128)(2,1)S(1)}, u32[]{:S(2)}, u32[]{:S(2)}) collective-permute-start(bf16[128,512]{1,0:T(8,128)(2,1)S(1)} %get-tuple-element.19), channel_id=1, source_target_pairs={{0,256},{128,384},{256,0},{384,128},{1,257},{129,385},{257,1},{385... | collective-permute-start | bytes 393224 | tf_op jit(solution)/shard_map/ppermute | solution.py:332
  93.7 6.0 %collective-permute-start.4 = (bf16[128,512]{1,0:T(8,128)(2,1)S(1)}, bf16[128,512]{1,0:T(8,128)(2,1)S(1)}, u32[]{:S(2)}, u32[]{:S(2)}) collective-permute-start(bf16[128,512]{1,0:T(8,128)(2,1)S(1)} %get-tuple-element.20), channel_id=1, source_target_pairs={{0,384},{128,0},{256,128},{384,256},{1,385},{129,1},{257,129},{385... | collective-permute-start | bytes 393224 | tf_op jit(solution)/shard_map/ppermute | solution.py:332

commit v4 on v3

--- a/solution.py
+++ b/solution.py
@@ -47,6 +47,17 @@
 def packed(x):
     n, r, width = x.shape
     return x.reshape(n, r, 4, width // 4).transpose(0, 2, 1, 3).reshape(n, 4 * r, width // 4)
+
+
+SINGLE = (3, 2, 0, 1)
+MISSING = (2, 3, 1, 0)
+
+
+def joined(first, second):
+    top = lax.broadcasted_iota(i32, first.shape, 0) < 4
+    even = jnp.where(top, first, pltpu.roll(second, 4, 0))
+    odd = jnp.where(top, pltpu.roll(first, 4, 0), second)
+    return even, odd
 
 
 def index_body(owner_ref, count_ref, sorted_ref, place_ref, *, groups, columns):
@@ -102,7 +113,7 @@
     owner_ref, count_ref, stats_ref, out_ref, sorted_ref, place_ref, stats_vmem, order_ref, sems, *, groups, columns
 ):
     blocks = owner_ref.shape[1]
-    each = out_ref.shape[1]
+    pairs_each = out_ref.shape[1]
     load = pltpu.make_async_copy(stats_ref, stats_vmem, sems.at[0])
     load.start()
     index_body(owner_ref, count_ref, sorted_ref, place_ref, groups=groups, columns=columns)
@@ -110,17 +121,26 @@
     move.start()
     move.wait()
     load.wait()
+    row_block = lax.axis_index(("z", "y")) * 8 // out_ref.shape[3]
+    paired = pl.ds(pl.multiple_of(8 * (row_block >> 1), 8), 8)
+    single = pl.ds(pl.multiple_of(8 * (1 - (row_block >> 1)), 8), 8)
+    lower = ((row_block + 1) & 2) == 0
     for x in range(groups):
 
-        def step(k, carry, x=x):
-            info = order_ref[0, k * groups + x]
-            block = info & (blocks - 1)
-            core = (info >> bits(blocks)) & 1
+        def step(i, carry, x=x):
+            places = []
+            for k in range(2):
+                info = order_ref[0, (2 * i + k) * groups + x]
+                places.append((2 * (info & (blocks - 1)), (info >> bits(blocks)) & 1))
             for c in range(2):
-                out_ref[x * 2 + c, k] = stats_vmem[2 * block + (core ^ c)].astype(bf16)
+                slabs = [block + (core ^ c) for block, core in places]
+                pairs = [stats_vmem[slab, paired, :] for slab in slabs]
+                even, odd = joined(*[stats_vmem[slab, single, :] for slab in slabs])
+                out_ref[x * 2 + c, i, 0:16] = jnp.concatenate(pairs, axis=0).astype(bf16)
+                out_ref[x * 2 + c, i, 16:24] = jnp.where(lower, odd, even).astype(bf16)
             return carry
 
-        lax.fori_loop(0, each, step, 0, unroll=8 if each % 8 == 0 else 1)
+        lax.fori_loop(0, pairs_each, step, 0, unroll=4 if pairs_each % 4 == 0 else 1)
 
 
 def grad_half_body(order_ref, grad_ref, out_ref, *, groups, blocks):
@@ -136,40 +156,34 @@
     lax.fori_loop(0, each, step, 0, unroll=8 if each % 8 == 0 else 1)
 
 
-def joined(first, second):
-    top = lax.broadcasted_iota(i32, first.shape, 0) < 4
-    even = jnp.where(top, first, pltpu.roll(second, 4, 0))
-    odd = jnp.where(top, pltpu.roll(first, 4, 0), second)
-    return even, odd
-
-
 def sum_stats_body(order_ref, got_ref, grad_ref, theirs_ref, out_ref, *, groups, blocks):
     out_ref[...] = jnp.zeros(out_ref.shape, bf16)
     me = lax.axis_index("dp")
     core = lax.axis_index("c")
-
-    def step(k, carry):
-        info = order_ref[0, k * groups + me]
-        column = (info >> (bits(blocks) + 1)) & (out_ref.shape[0] - 1)
+    half = pl.ds(pl.multiple_of(8 * core, 8), 8)
+
+    def step(i, carry):
         sums = []
         for c in range(2):
-            total = got_ref[c, k].astype(f32)
+            total = got_ref[c, i].astype(f32)
             for x in range(1, groups):
-                total = total + got_ref[2 * x + c, k].astype(f32)
+                total = total + got_ref[2 * x + c, i].astype(f32)
             sums.append(total)
-        tiles = []
-        for v in range(2):
-            tiles += joined(sums[0][8 * v : 8 * v + 8], sums[1][8 * v : 8 * v + 8])
-        mine = grad_ref[info & (blocks - 1), pl.ds(pl.multiple_of(8 * core, 8), 8), :].astype(f32)
-        theirs = theirs_ref[k].astype(f32)
-        tiles += joined(jnp.where(core == 0, mine, theirs), jnp.where(core == 0, theirs, mine))
-        for v in range(3):
-            pair = jnp.concatenate(tiles[2 * v : 2 * v + 2], axis=0)
-            out_ref[column, 16 * v : 16 * v + 16] = pair.astype(bf16)
+        joints = [joined(sums[0][8 * v : 8 * v + 8], sums[1][8 * v : 8 * v + 8]) for v in range(3)]
+        for k in range(2):
+            info = order_ref[0, (2 * i + k) * groups + me]
+            column = (info >> (bits(blocks) + 1)) & (out_ref.shape[0] - 1)
+            mine = grad_ref[info & (blocks - 1), half, :].astype(f32)
+            theirs = theirs_ref[2 * i + k].astype(f32)
+            grad = joined(jnp.where(core == 0, mine, theirs), jnp.where(core == 0, theirs, mine))
+            out_ref[column, 0:16] = jnp.concatenate(joints[k], axis=0).astype(bf16)
+            rest = jnp.concatenate([joints[2][k], grad[0]], axis=0)
+            out_ref[column, 16:32] = rest.astype(bf16)
+            out_ref[column, 32:40] = grad[1].astype(bf16)
         return carry
 
-    each = blocks // groups
-    lax.fori_loop(0, each, step, 0, unroll=4 if each % 4 == 0 else 1)
+    pairs = got_ref.shape[1]
+    lax.fori_loop(0, pairs, step, 0, unroll=2 if pairs % 2 == 0 else 1)
 
 
 def dot(a, b):
@@ -179,11 +193,17 @@
 def newton_body(got_ref, out_ref, a_ref):
     order = out_ref.shape[1]
     chunk = got_ref.shape[2]
-    for q in range(4):
-        tile = got_ref[:, 8 * q : 8 * q + 8, :].astype(f32).reshape(order, chunk)
-        a_ref[:, q * chunk : (q + 1) * chunk] = tile
+    each = chunk // 8
+    for row in range(4):
+        rows = slice(row * chunk, (row + 1) * chunk)
+        for number, q in enumerate((row // 2 * 2, row // 2 * 2 + 1, SINGLE[row])):
+            tile = got_ref[row * each : (row + 1) * each, 8 * number : 8 * number + 8, :]
+            tile = tile.astype(f32).reshape(chunk, chunk)
+            a_ref[rows, q * chunk : (q + 1) * chunk] = tile
+            if MISSING[q] == row:
+                a_ref[q * chunk : (q + 1) * chunk, rows] = tile.T
     for q in range(2):
-        tile = got_ref[:, 32 + 8 * q : 40 + 8 * q, :].astype(f32).reshape(order, chunk).astype(bf16)
+        tile = got_ref[:, 24 + 8 * q : 32 + 8 * q, :].astype(f32).reshape(order, chunk).astype(bf16)
         for v in range(2):
             place = slice((2 * v + q) * chunk, (2 * v + q + 1) * chunk)
             out_ref[order:, place] = tile[v * order // 2 : (v + 1) * order // 2]
@@ -282,7 +302,7 @@
     swap = [(0, 1), (1, 0)]
 
     stats = packed(stats_partial.reshape(2 * blocks, local_rows, order))
-    out_shape = (2 * groups, each, 16, chunk)
+    out_shape = (2 * groups, each // 2, 24, chunk)
     outgoing, order_info, place = call(
         functools.partial(pack_stats_body, groups=groups, columns=columns),
         (pltpu.VMEM(out_shape, bf16), struct((1, blocks), i32), struct((1, 128), i32)),
@@ -304,7 +324,7 @@
     grad_theirs = lax.ppermute(grad_half, "c", swap)
     summed = call(
         functools.partial(sum_stats_body, groups=groups, blocks=blocks),
-        pltpu.VMEM((columns, 48, chunk), bf16),
+        pltpu.VMEM((columns, 40, chunk), bf16),
         [SMEM, VMEM, VMEM, VMEM],
     )(order_info, held(arrived), grad, held(grad_theirs))
     statistic = lax.all_to_all(summed, ("z", "y"), 0, 0, tiled=True)

time: 103 us -> 97.2 us (0.944)
  waiting for transfers between devices: 17.5 us -> 14.7 us
  blocking collectives: 33 us -> 30.4 us
    all_to_all x1, waiting for transfers between devices: 11.2 us -> 8.39 us  [on_device(): arrived = lax.all_to_all(outgoing, ('dp', 'c'), 0, 0, tiled=True)]
    all_to_all x1, blocking collectives: 33 us -> 30.4 us  [on_device(): statistic = lax.all_to_all(summed, ('z', 'y'), 0, 0, tiled=True)]
where the time goes in v4:
time: 97.2 us; the launch traced here: 96 us
  starting transfers between devices  37.6 us (39%)
  blocking collectives  30.4 us (31%)
  waiting for transfers between devices  14.7 us (15%)
  Pallas kernels  13.1 us (13%)
    all_to_all x1, blocking collectives, on_device(): statistic = lax.all_to_all(summed, ('z', 'y'), 0, 0, tiled=True)  30.4 us
    all_to_all x1, starting transfers between devices, on_device(): arrived = lax.all_to_all(outgoing, ('dp', 'c'), 0, 0, tiled=True)  10.3 us
    ppermute x3, starting transfers between devices, on_device(): spread.append(held(lax.ppermute(quarters[step], 'dp', pairs)))  9.75 us
    all_to_all x1, starting transfers between devices, on_device(): norms = lax.all_to_all(norms, ('dp', 'z', 'y'), 0, 0, tiled=True)  9.3 us
    all_to_all x1, waiting for transfers between devices, on_device(): arrived = lax.all_to_all(outgoing, ('dp', 'c'), 0, 0, tiled=True)  8.39 us
    ppermute x1, starting transfers between devices, on_device(): other = lax.ppermute(bundle, 'c', swap)  6.24 us
    pallas_call x1, Pallas kernels, on_device(): call(functools.partial(pack_stats_body, groups=groups, columns=columns),...  4.07 us
    ppermute x3, waiting for transfers between devices, on_device(): spread.append(held(lax.ppermute(quarters[step], 'dp', pairs)))  3.34 us
  transfers between devices with their start and end apart: 7, of which 5 were waited for; matrix products, arithmetic and copies ran while one was open for 0% of the time, Pallas kernels for 1%

profile of v4, /device:TPU:1, one launch (start us, length us, event | category | flops | bytes accessed | tf_op | source)
XLA Modules:
  0.0 96.0 jit_solution(1938494068999749180)
XLA Ops:
  0.0 0.0 copy-start
  0.0 4.1 %shard_map.46 = (bf16[8,16,24,128]{3,2,1,0:T(8,128)(2,1)}, s32[1,128]{1,0:T(1,128)S(1)}, s32[1,128]{1,0:T(1,128)S(1)}) custom-call(s32[1,128]{1,0:T(1,128)} %bitcast.15, s32[4]{0:T(128)} %count_ref.1, f32[256,16,128]{2,1,0:T(8,128)} %bitcast.14), custom_call_target="tpu_custom_call" | custom-call | tf_op jit(solution)/shard_map/pallas_call | solution.py:306
  4.1 10.3 %all-to-all-start = ((bf16[8,16,24,128]{3,2,1,0:T(8,128)(2,1)}), bf16[8,16,24,128]{3,2,1,0:T(8,128)(2,1)S(1)}, u32[]{:S(2)}, u32[]{:S(2)}) async-start(bf16[8,16,24,128]{3,2,1,0:T(8,128)(2,1)} %get-tuple-element.15), calls=%async_computation | async-start | bytes 1572864 | tf_op jit(solution)/shard_map/all_to_all | solution.py:317
  14.4 0.0 copy-done
  14.4 0.6 shard_map.47
  15.0 2.0 %collective-permute-start = (bf16[32,8,128]{2,1,0:T(8,128)(2,1)S(1)}, bf16[32,8,128]{2,1,0:T(8,128)(2,1)S(1)}, u32[]{:S(2)}, u32[]{:S(2)}) collective-permute-start(bf16[32,8,128]{2,1,0:T(8,128)(2,1)S(1)} %shard_map.47), channel_id=1, source_target_pairs={{0,1},{1,0},{2,3},{3,2},{4,5},{5,4},{6,7},{7,6},{8,9},{9,8},{10,11... | collective-permute-start | bytes 196616 | tf_op jit(solution)/shard_map/ppermute | solution.py:324
  17.1 1.1 %collective-permute-done.theirs_ref = bf16[32,8,128]{2,1,0:T(8,128)(2,1)S(1)} collective-permute-done((bf16[32,8,128]{2,1,0:T(8,128)(2,1)S(1)}, bf16[32,8,128]{2,1,0:T(8,128)(2,1)S(1)}, u32[]{:S(2)}, u32[]{:S(2)}) %collective-permute-start) | collective-permute-done | bytes 65568 | tf_op jit(solution)/shard_map/ppermute | solution.py:324
  18.2 8.4 %all-to-all-done.got_ref = bf16[8,16,24,128]{3,2,1,0:T(8,128)(2,1)S(1)} async-done(((bf16[8,16,24,128]{3,2,1,0:T(8,128)(2,1)}), bf16[8,16,24,128]{3,2,1,0:T(8,128)(2,1)S(1)}, u32[]{:S(2)}, u32[]{:S(2)}) %all-to-all-start) | async-done | bytes 786464 | tf_op jit(solution)/shard_map/all_to_all | solution.py:317
  26.6 0.8 shard_map.48
  27.4 30.4 %all_to_all.15.got_ref = bf16[64,40,128]{2,1,0:T(8,128)(2,1)S(1)} all-to-all(bf16[64,40,128]{2,1,0:T(8,128)(2,1)S(1)} %shard_map.48), channel_id=1, replica_groups=mesh['dp'=4,'z'=8,'y'=8,'c'=2] {'z','y'}, dimensions={0} | all-to-all | bytes 1310720 | tf_op jit(solution)/shard_map/all_to_all | solution.py:330
  57.9 3.2 %shard_map.49.mine_ref = bf16[768,512]{1,0:T(8,128)(2,1)S(1)} custom-call(bf16[64,40,128]{2,1,0:T(8,128)(2,1)S(1)} %all_to_all.15.got_ref), custom_call_target="tpu_custom_call" | custom-call | tf_op jit(solution)/shard_map/pallas_call | solution.py:332
  61.1 6.2 %collective-permute-start.1 = (bf16[768,512]{1,0:T(8,128)(2,1)S(1)}, bf16[768,512]{1,0:T(8,128)(2,1)S(1)}, u32[]{:S(2)}, u32[]{:S(2)}) collective-permute-start(bf16[768,512]{1,0:T(8,128)(2,1)S(1)} %shard_map.49.mine_ref), channel_id=1, source_target_pairs={{0,1},{1,0},{2,3},{3,2},{4,5},{5,4},{6,7},{7,6},{8,9},{9,8},{10,11... | collective-permute-start | bytes 2359304 | tf_op jit(solution)/shard_map/ppermute | solution.py:335
  67.3 1.9 %collective-permute-done.1.other_ref = bf16[768,512]{1,0:T(8,128)(2,1)S(1)} collective-permute-done((bf16[768,512]{1,0:T(8,128)(2,1)S(1)}, bf16[768,512]{1,0:T(8,128)(2,1)S(1)}, u32[]{:S(2)}, u32[]{:S(2)}) %collective-permute-start.1) | collective-permute-done | bytes 786464 | tf_op jit(solution)/shard_map/ppermute | solution.py:335
  69.2 2.5 %shard_map.50 = (bf16[128,512]{1,0:T(8,128)(2,1)S(1)}, bf16[128,512]{1,0:T(8,128)(2,1)S(1)}, bf16[128,512]{1,0:T(8,128)(2,1)S(1)}, bf16[128,512]{1,0:T(8,128)(2,1)S(1)}, f32[256,1,128]{2,1,0:T(1,128)}) custom-call(s32[1,128]{1,0:T(1,128)S(1)} %get-tuple-element.13.place_ref, bf16[768,512]{1,0:T(8,128)(2,1)S(1)} %shard_map.49.mine_ref, ...), custom_call_target="tpu_custom_call" | custom-call | tf_op jit(solution)/shard_map/pallas_call | solution.py:336
  71.7 9.3 %all-to-all-start.2 = ((f32[256,1,128]{2,1,0:T(1,128)}), f32[256,1,128]{2,1,0:T(1,128)S(1)}, u32[]{:S(2)}, u32[]{:S(2)}) async-start(f32[256,1,128]{2,1,0:T(1,128)} %get-tuple-element.16), calls=%async_computation.2 | async-start | bytes 262144 | tf_op jit(solution)/shard_map/all_to_all | solution.py:348
  81.0 1.9 %collective-permute-start.2 = (bf16[128,512]{1,0:T(8,128)(2,1)S(1)}, bf16[128,512]{1,0:T(8,128)(2,1)S(1)}, u32[]{:S(2)}, u32[]{:S(2)}) collective-permute-start(bf16[128,512]{1,0:T(8,128)(2,1)S(1)} %get-tuple-element.18), channel_id=1, source_target_pairs={{0,128},{128,256},{256,384},{384,0},{1,129},{129,257},{257,385},{3... | collective-permute-start | bytes 393224 | tf_op jit(solution)/shard_map/ppermute | solution.py:352
  82.9 5.2 %collective-permute-start.3 = (bf16[128,512]{1,0:T(8,128)(2,1)S(1)}, bf16[128,512]{1,0:T(8,128)(2,1)S(1)}, u32[]{:S(2)}, u32[]{:S(2)}) collective-permute-start(bf16[128,512]{1,0:T(8,128)(2,1)S(1)} %get-tuple-element.19), channel_id=1, source_target_pairs={{0,256},{128,384},{256,0},{384,128},{1,257},{129,385},{257,1},{385... | collective-permute-start | bytes 393224 | tf_op jit(solution)/shard_map/ppermute | solution.py:352
  88.1 2.7 %collective-permute-start.4 = (bf16[128,512]{1,0:T(8,128)(2,1)S(1)}, bf16[128,512]{1,0:T(8,128)(2,1)S(1)}, u32[]{:S(2)}, u32[]{:S(2)}) collective-permute-start(bf16[128,512]{1,0:T(8,128)(2,1)S(1)} %get-tuple-element.20), channel_id=1, source_target_pairs={{0,384},{128,0},{256,128},{384,256},{1,385},{129,1},{257,129},{385... | collective-permute-start | bytes 393224 | tf_op jit(solution)/shard_map/ppermute | solution.py:352
  90.8 0.0 collective-permute-done.2.refs_0_
  90.8 2.1 %collective-permute-done.3.refs_1_ = bf16[128,512]{1,0:T(8,128)(2,1)S(1)} collective-permute-done((bf16[128,512]{1,0:T(8,128)(2,1)S(1)}, bf16[128,512]{1,0:T(8,128)(2,1)S(1)}, u32[]{:S(2)}, u32[]{:S(2)}) %collective-permute-start.3) | collective-permute-done | bytes 131104 | tf_op jit(solution)/shard_map/ppermute | solution.py:352
  92.9 1.2 %collective-permute-done.4.refs_2_ = bf16[128,512]{1,0:T(8,128)(2,1)S(1)} collective-permute-done((bf16[128,512]{1,0:T(8,128)(2,1)S(1)}, bf16[128,512]{1,0:T(8,128)(2,1)S(1)}, u32[]{:S(2)}, u32[]{:S(2)}) %collective-permute-start.4) | collective-permute-done | bytes 131104 | tf_op jit(solution)/shard_map/ppermute | solution.py:352
  94.1 0.0 all-to-all-done.2.norm_ref
  94.1 1.8 %shard_map.51 = bf16[2,128,512]{2,1,0:T(8,128)(2,1)} custom-call(s32[1,128]{1,0:T(1,128)S(1)} %get-tuple-element.13.place_ref, f32[256,1,128]{2,1,0:T(1,128)S(1)} %all-to-all-done.2.norm_ref, bf16[128,512]{1,0:T(8,128)(2,1)S(1)} %get-tuple-element.17.raw_ref, bf16[128,512]{1,0:T(8,128)(2,1)S(1)} %collective-permute-done.2.refs_0_, ...), custom_call_target="tpu_custom_call" | custom-call | tf_op jit(solution)/shard_map/pallas_call | solution.py:353
Async XLA Ops:
  0.0 14.4 %copy-start = (bf16[128,4,512]{2,1,0:T(4,128)(2,1)S(1)}, bf16[128,4,512]{2,1,0:T(4,128)(2,1)}, u32[]{:S(2)}) copy-start(bf16[128,4,512]{2,1,0:T(4,128)(2,1)} %param.5) | copy-start | bytes 1572868
  4.1 22.5 %all-to-all-start = ((bf16[8,16,24,128]{3,2,1,0:T(8,128)(2,1)}), bf16[8,16,24,128]{3,2,1,0:T(8,128)(2,1)S(1)}, u32[]{:S(2)}, u32[]{:S(2)}) async-start(bf16[8,16,24,128]{3,2,1,0:T(8,128)(2,1)} %get-tuple-element.15), calls=%async_computation | async-start | bytes 1572864 | tf_op jit(solution)/shard_map/all_to_all | solution.py:317
  15.0 3.1 %collective-permute-start = (bf16[32,8,128]{2,1,0:T(8,128)(2,1)S(1)}, bf16[32,8,128]{2,1,0:T(8,128)(2,1)S(1)}, u32[]{:S(2)}, u32[]{:S(2)}) collective-permute-start(bf16[32,8,128]{2,1,0:T(8,128)(2,1)S(1)} %shard_map.47), channel_id=1, source_target_pairs={{0,1},{1,0},{2,3},{3,2},{4,5},{5,4},{6,7},{7,6},{8,9},{9,8},{10,11... | collective-permute-start | bytes 196616 | tf_op jit(solution)/shard_map/ppermute | solution.py:324
  61.1 8.1 %collective-permute-start.1 = (bf16[768,512]{1,0:T(8,128)(2,1)S(1)}, bf16[768,512]{1,0:T(8,128)(2,1)S(1)}, u32[]{:S(2)}, u32[]{:S(2)}) collective-permute-start(bf16[768,512]{1,0:T(8,128)(2,1)S(1)} %shard_map.49.mine_ref), channel_id=1, source_target_pairs={{0,1},{1,0},{2,3},{3,2},{4,5},{5,4},{6,7},{7,6},{8,9},{9,8},{10,11... | collective-permute-start | bytes 2359304 | tf_op jit(solution)/shard_map/ppermute | solution.py:335
  71.7 22.4 %all-to-all-start.2 = ((f32[256,1,128]{2,1,0:T(1,128)}), f32[256,1,128]{2,1,0:T(1,128)S(1)}, u32[]{:S(2)}, u32[]{:S(2)}) async-start(f32[256,1,128]{2,1,0:T(1,128)} %get-tuple-element.16), calls=%async_computation.2 | async-start | bytes 262144 | tf_op jit(solution)/shard_map/all_to_all | solution.py:348
  81.0 9.8 %collective-permute-start.2 = (bf16[128,512]{1,0:T(8,128)(2,1)S(1)}, bf16[128,512]{1,0:T(8,128)(2,1)S(1)}, u32[]{:S(2)}, u32[]{:S(2)}) collective-permute-start(bf16[128,512]{1,0:T(8,128)(2,1)S(1)} %get-tuple-element.18), channel_id=1, source_target_pairs={{0,128},{128,256},{256,384},{384,0},{1,129},{129,257},{257,385},{3... | collective-permute-start | bytes 393224 | tf_op jit(solution)/shard_map/ppermute | solution.py:352
  82.9 10.0 %collective-permute-start.3 = (bf16[128,512]{1,0:T(8,128)(2,1)S(1)}, bf16[128,512]{1,0:T(8,128)(2,1)S(1)}, u32[]{:S(2)}, u32[]{:S(2)}) collective-permute-start(bf16[128,512]{1,0:T(8,128)(2,1)S(1)} %get-tuple-element.19), channel_id=1, source_target_pairs={{0,256},{128,384},{256,0},{384,128},{1,257},{129,385},{257,1},{385... | collective-permute-start | bytes 393224 | tf_op jit(solution)/shard_map/ppermute | solution.py:352
  88.1 6.0 %collective-permute-start.4 = (bf16[128,512]{1,0:T(8,128)(2,1)S(1)}, bf16[128,512]{1,0:T(8,128)(2,1)S(1)}, u32[]{:S(2)}, u32[]{:S(2)}) collective-permute-start(bf16[128,512]{1,0:T(8,128)(2,1)S(1)} %get-tuple-element.20), channel_id=1, source_target_pairs={{0,384},{128,0},{256,128},{384,256},{1,385},{129,1},{257,129},{385... | collective-permute-start | bytes 393224 | tf_op jit(solution)/shard_map/ppermute | solution.py:352

commit v5 on v4

--- a/solution.py
+++ b/solution.py
@@ -27,6 +27,10 @@
 
 def held(x):
     return pltpu.with_memory_space_constraint(x, pltpu.VMEM)
+
+
+def in_smem(x):
+    return pltpu.with_memory_space_constraint(x, pltpu.SMEM)
 
 
 def in_hbm(x):
@@ -110,17 +114,40 @@
 
 
 def pack_stats_body(
-    owner_ref, count_ref, stats_ref, out_ref, sorted_ref, place_ref, stats_vmem, order_ref, sems, *, groups, columns
+    owner_ref,
+    count_ref,
+    stats_ref,
+    out_ref,
+    sorted_ref,
+    place_ref,
+    owner_vmem,
+    count_smem,
+    stats_vmem,
+    out_vmem,
+    order_ref,
+    sems,
+    *,
+    groups,
+    columns,
 ):
     blocks = owner_ref.shape[1]
     pairs_each = out_ref.shape[1]
+    small = [
+        pltpu.make_async_copy(owner_ref, owner_vmem, sems.at[1]),
+        pltpu.make_async_copy(count_ref, count_smem, sems.at[2]),
+    ]
     load = pltpu.make_async_copy(stats_ref, stats_vmem, sems.at[0])
+    for copy in small:
+        copy.start()
     load.start()
-    index_body(owner_ref, count_ref, sorted_ref, place_ref, groups=groups, columns=columns)
-    move = pltpu.make_async_copy(sorted_ref, order_ref, sems.at[1])
+    for copy in small:
+        copy.wait()
+    index_body(owner_vmem, count_smem, sorted_ref, place_ref, groups=groups, columns=columns)
+    move = pltpu.make_async_copy(sorted_ref, order_ref, sems.at[3])
     move.start()
     move.wait()
     load.wait()
+    stores = []
     row_block = lax.axis_index(("z", "y")) * 8 // out_ref.shape[3]
     paired = pl.ds(pl.multiple_of(8 * (row_block >> 1), 8), 8)
     single = pl.ds(pl.multiple_of(8 * (1 - (row_block >> 1)), 8), 8)
@@ -136,11 +163,16 @@
                 slabs = [block + (core ^ c) for block, core in places]
                 pairs = [stats_vmem[slab, paired, :] for slab in slabs]
                 even, odd = joined(*[stats_vmem[slab, single, :] for slab in slabs])
-                out_ref[x * 2 + c, i, 0:16] = jnp.concatenate(pairs, axis=0).astype(bf16)
-                out_ref[x * 2 + c, i, 16:24] = jnp.where(lower, odd, even).astype(bf16)
+                out_vmem[x * 2 + c, i, 0:16] = jnp.concatenate(pairs, axis=0).astype(bf16)
+                out_vmem[x * 2 + c, i, 16:24] = jnp.where(lower, odd, even).astype(bf16)
             return carry
 
         lax.fori_loop(0, pairs_each, step, 0, unroll=4 if pairs_each % 4 == 0 else 1)
+        part = pl.ds(2 * x, 2)
+        stores.append(pltpu.make_async_copy(out_vmem.at[part], out_ref.at[part], sems.at[4 + x]))
+        stores[-1].start()
+    for store in stores:
+        store.wait()
 
 
 def grad_half_body(order_ref, grad_ref, out_ref, *, groups, blocks):
@@ -229,37 +261,43 @@
 
 
 def raw_body(place_ref, mine_ref, other_ref, *refs):
-    norm_ref, both_ref, raw_ref, sems = refs[-4:]
-    out_refs = refs[:-4]
+    norm_ref, raw_ref = refs[-2:]
+    out_refs = refs[:-2]
     groups = len(out_refs)
     order = mine_ref.shape[1]
     half, quarter = order // 2, order // groups
     live, core, layer = place_ref[0, 0], place_ref[0, 1], place_ref[0, 2]
     me_c, me_x = lax.axis_index("c"), lax.axis_index("dp")
-    loads = [
-        pltpu.make_async_copy(mine_ref, both_ref.at[me_c], sems.at[0]),
-        pltpu.make_async_copy(other_ref, both_ref.at[1 - me_c], sems.at[1]),
-    ]
-    for load in loads:
-        load.start()
-    for load in loads:
-        load.wait()
-    raw = jnp.zeros((order, order), f32)
     grad_sq = jnp.zeros((1, 1), f32)
-    for c in range(2):
-        middle = jnp.zeros((order, half), f32)
-        for v in range(2):
-            grad = both_ref[c, order:, v * half : (v + 1) * half]
-            middle = middle + dot(both_ref[core, 0:order, v * half : (v + 1) * half], grad)
-            wide = grad.astype(f32)
-            grad_sq = grad_sq + jnp.sum(wide * wide, keepdims=True)
-        raw = raw + dot(middle.astype(bf16), both_ref[1 - core, c * half : (c + 1) * half])
-    raw_sq = jnp.sum(raw * raw, keepdims=True)
+    for ref in (mine_ref, other_ref):
+        wide = ref[order:].astype(f32)
+        grad_sq = grad_sq + jnp.sum(wide * wide, keepdims=True)
     lane = lax.broadcasted_iota(i32, (1, LANES), 1)
-    norms = jnp.where(lane == layer, grad_sq, 0.0) + jnp.where(lane == layer + LAYERS, raw_sq, 0.0)
-    norms = jnp.where(live > 0, norms, 0.0)
-    norm_ref[...] = jnp.broadcast_to(norms[:, None, :], norm_ref.shape)
-    raw_ref[...] = raw.astype(bf16)
+
+    def finish(left_ref, right_ref):
+        raw = jnp.zeros((order, order), f32)
+        for ref, at in ((mine_ref, me_c), (other_ref, 1 - me_c)):
+            middle = jnp.zeros((order, half), f32)
+            for v in range(2):
+                cols = slice(v * half, (v + 1) * half)
+                middle = middle + dot(left_ref[0:order, cols], ref[order:, cols])
+            right = right_ref[pl.ds(pl.multiple_of(at * half, half), half), :]
+            raw = raw + dot(middle.astype(bf16), right)
+        raw_sq = jnp.sum(raw * raw, keepdims=True)
+        norms = jnp.where(lane == layer, grad_sq, 0.0)
+        norms = norms + jnp.where(lane == layer + LAYERS, raw_sq, 0.0)
+        norms = jnp.where(live > 0, norms, 0.0)
+        norm_ref[...] = jnp.broadcast_to(norms[:, None, :], norm_ref.shape)
+        raw_ref[...] = raw.astype(bf16)
+
+    @pl.when(core == me_c)
+    def _():
+        finish(mine_ref, other_ref)
+
+    @pl.when(core != me_c)
+    def _():
+        finish(other_ref, mine_ref)
+
     for number, out_ref in enumerate(out_refs):
         start = ((me_x + number) & (groups - 1)) * quarter
         out_ref[...] = raw_ref[pl.ds(pl.multiple_of(start, quarter), quarter), :]
@@ -305,15 +343,19 @@
     out_shape = (2 * groups, each // 2, 24, chunk)
     outgoing, order_info, place = call(
         functools.partial(pack_stats_body, groups=groups, columns=columns),
-        (pltpu.VMEM(out_shape, bf16), struct((1, blocks), i32), struct((1, 128), i32)),
-        [VMEM, SMEM, ANY],
+        (struct(out_shape, bf16), struct((1, blocks), i32), struct((1, 128), i32)),
+        [ANY, ANY, ANY],
         [
+            pltpu.VMEM((1, blocks), i32),
+            pltpu.SMEM((LAYERS,), i32),
             pltpu.VMEM(stats.shape, f32),
+            pltpu.VMEM(out_shape, bf16),
             pltpu.SMEM((1, blocks), i32),
-            pltpu.SemaphoreType.DMA((2,)),
+            pltpu.SemaphoreType.DMA((4 + groups,)),
         ],
-        (VMEM, VMEM, VMEM),
+        (ANY, VMEM, VMEM),
     )(in_hbm(owner_of[None]), in_hbm(layer_count), in_hbm(stats))
+    order_info, place = in_smem(order_info), in_smem(place)
     arrived = lax.all_to_all(outgoing, ("dp", "c"), 0, 0, tiled=True)
     grad = packed(gradient)
     grad_half = call(
@@ -337,12 +379,8 @@
         raw_body,
         tuple(pltpu.VMEM((quarter, order), bf16) for _ in range(groups))
         + (pltpu.VMEM((groups * columns, 1, LANES), f32),),
-        [SMEM, ANY, ANY],
-        [
-            pltpu.VMEM((2, *bundle_shape), bf16),
-            pltpu.VMEM((order, order), bf16),
-            pltpu.SemaphoreType.DMA((2,)),
-        ],
+        [SMEM, VMEM, VMEM],
+        [pltpu.VMEM((order, order), bf16)],
         (VMEM,) * (groups + 1),
     )(place, held(bundle), held(other))
     norms = lax.all_to_all(norms, ("dp", "z", "y"), 0, 0, tiled=True)

time: 97.2 us -> 96.3 us (level)
  no operation moved by 1% of the time
where the time goes in v5:
time: 96.3 us; the launch traced here: 95.1 us
  starting transfers between devices  37.6 us (39%)
  blocking collectives  30.4 us (32%)
  waiting for transfers between devices  14.7 us (15%)
  Pallas kernels  12.2 us (13%)
    all_to_all x1, blocking collectives, on_device(): statistic = lax.all_to_all(summed, ('z', 'y'), 0, 0, tiled=True)  30.4 us
    all_to_all x1, starting transfers between devices, on_device(): arrived = lax.all_to_all(outgoing, ('dp', 'c'), 0, 0, tiled=True)  10.3 us
    ppermute x3, starting transfers between devices, on_device(): spread.append(held(lax.ppermute(quarters[step], 'dp', pairs)))  9.75 us
    all_to_all x1, starting transfers between devices, on_device(): norms = lax.all_to_all(norms, ('dp', 'z', 'y'), 0, 0, tiled=True)  9.28 us
    all_to_all x1, waiting for transfers between devices, on_device(): arrived = lax.all_to_all(outgoing, ('dp', 'c'), 0, 0, tiled=True)  8.39 us
    ppermute x1, starting transfers between devices, on_device(): other = lax.ppermute(bundle, 'c', swap)  6.24 us
    ppermute x3, waiting for transfers between devices, on_device(): spread.append(held(lax.ppermute(quarters[step], 'dp', pairs)))  3.34 us
    pallas_call x1, Pallas kernels, on_device(): call(newton_body, pltpu.VMEM(bundle_shape, bf16), [VMEM], [pltpu.VMEM((or...  3.22 us
  transfers between devices with their start and end apart: 7, of which 5 were waited for; matrix products, arithmetic and copies ran while one was open for 0% of the time, Pallas kernels for 1%

profile of v5, /device:TPU:1, one launch (start us, length us, event | category | flops | bytes accessed | tf_op | source)
XLA Modules:
  0.0 95.1 jit_solution(13967457114008495547)
XLA Ops:
  0.0 0.0 copy-start
  0.0 3.2 %shard_map.46 = (bf16[8,16,24,128]{3,2,1,0:T(8,128)(2,1)}, s32[1,128]{1,0:T(1,128)S(1)}, s32[1,128]{1,0:T(1,128)S(1)}) custom-call(s32[1,128]{1,0:T(1,128)} %bitcast.15, s32[4]{0:T(128)} %count_ref.1, f32[256,16,128]{2,1,0:T(8,128)} %bitcast.14), custom_call_target="tpu_custom_call" | custom-call | tf_op jit(solution)/shard_map/pallas_call | solution.py:344
  3.2 10.3 %all-to-all-start = ((bf16[8,16,24,128]{3,2,1,0:T(8,128)(2,1)}), bf16[8,16,24,128]{3,2,1,0:T(8,128)(2,1)S(1)}, u32[]{:S(2)}, u32[]{:S(2)}) async-start(bf16[8,16,24,128]{3,2,1,0:T(8,128)(2,1)} %get-tuple-element.15), calls=%async_computation | async-start | bytes 1572864 | tf_op jit(solution)/shard_map/all_to_all | solution.py:359
  13.5 0.0 copy-done
  13.5 0.6 shard_map.47
  14.1 2.0 %collective-permute-start = (bf16[32,8,128]{2,1,0:T(8,128)(2,1)S(1)}, bf16[32,8,128]{2,1,0:T(8,128)(2,1)S(1)}, u32[]{:S(2)}, u32[]{:S(2)}) collective-permute-start(bf16[32,8,128]{2,1,0:T(8,128)(2,1)S(1)} %shard_map.47), channel_id=1, source_target_pairs={{0,1},{1,0},{2,3},{3,2},{4,5},{5,4},{6,7},{7,6},{8,9},{9,8},{10,11... | collective-permute-start | bytes 196616 | tf_op jit(solution)/shard_map/ppermute | solution.py:366
  16.2 1.1 %collective-permute-done.theirs_ref = bf16[32,8,128]{2,1,0:T(8,128)(2,1)S(1)} collective-permute-done((bf16[32,8,128]{2,1,0:T(8,128)(2,1)S(1)}, bf16[32,8,128]{2,1,0:T(8,128)(2,1)S(1)}, u32[]{:S(2)}, u32[]{:S(2)}) %collective-permute-start) | collective-permute-done | bytes 65568 | tf_op jit(solution)/shard_map/ppermute | solution.py:366
  17.3 8.4 %all-to-all-done.got_ref = bf16[8,16,24,128]{3,2,1,0:T(8,128)(2,1)S(1)} async-done(((bf16[8,16,24,128]{3,2,1,0:T(8,128)(2,1)}), bf16[8,16,24,128]{3,2,1,0:T(8,128)(2,1)S(1)}, u32[]{:S(2)}, u32[]{:S(2)}) %all-to-all-start) | async-done | bytes 786464 | tf_op jit(solution)/shard_map/all_to_all | solution.py:359
  25.7 0.8 shard_map.48
  26.5 30.4 %all_to_all.15.got_ref = bf16[64,40,128]{2,1,0:T(8,128)(2,1)S(1)} all-to-all(bf16[64,40,128]{2,1,0:T(8,128)(2,1)S(1)} %shard_map.48), channel_id=1, replica_groups=mesh['dp'=4,'z'=8,'y'=8,'c'=2] {'z','y'}, dimensions={0} | all-to-all | bytes 1310720 | tf_op jit(solution)/shard_map/all_to_all | solution.py:372
  57.0 3.2 %shard_map.49.mine_ref = bf16[768,512]{1,0:T(8,128)(2,1)S(1)} custom-call(bf16[64,40,128]{2,1,0:T(8,128)(2,1)S(1)} %all_to_all.15.got_ref), custom_call_target="tpu_custom_call" | custom-call | tf_op jit(solution)/shard_map/pallas_call | solution.py:374
  60.2 6.2 %collective-permute-start.1 = (bf16[768,512]{1,0:T(8,128)(2,1)S(1)}, bf16[768,512]{1,0:T(8,128)(2,1)S(1)}, u32[]{:S(2)}, u32[]{:S(2)}) collective-permute-start(bf16[768,512]{1,0:T(8,128)(2,1)S(1)} %shard_map.49.mine_ref), channel_id=1, source_target_pairs={{0,1},{1,0},{2,3},{3,2},{4,5},{5,4},{6,7},{7,6},{8,9},{9,8},{10,11... | collective-permute-start | bytes 2359304 | tf_op jit(solution)/shard_map/ppermute | solution.py:377
  66.4 1.9 %collective-permute-done.1.other_ref = bf16[768,512]{1,0:T(8,128)(2,1)S(1)} collective-permute-done((bf16[768,512]{1,0:T(8,128)(2,1)S(1)}, bf16[768,512]{1,0:T(8,128)(2,1)S(1)}, u32[]{:S(2)}, u32[]{:S(2)}) %collective-permute-start.1) | collective-permute-done | bytes 786464 | tf_op jit(solution)/shard_map/ppermute | solution.py:377
  68.3 2.5 %shard_map.50 = (bf16[128,512]{1,0:T(8,128)(2,1)S(1)}, bf16[128,512]{1,0:T(8,128)(2,1)S(1)}, bf16[128,512]{1,0:T(8,128)(2,1)S(1)}, bf16[128,512]{1,0:T(8,128)(2,1)S(1)}, f32[256,1,128]{2,1,0:T(1,128)}) custom-call(s32[1,128]{1,0:T(1,128)S(1)} %get-tuple-element.13.place_ref, bf16[768,512]{1,0:T(8,128)(2,1)S(1)} %shard_map.49.mine_ref, ...), custom_call_target="tpu_custom_call" | custom-call | tf_op jit(solution)/shard_map/pallas_call | solution.py:378
  70.9 9.3 %all-to-all-start.2 = ((f32[256,1,128]{2,1,0:T(1,128)}), f32[256,1,128]{2,1,0:T(1,128)S(1)}, u32[]{:S(2)}, u32[]{:S(2)}) async-start(f32[256,1,128]{2,1,0:T(1,128)} %get-tuple-element.16), calls=%async_computation.2 | async-start | bytes 262144 | tf_op jit(solution)/shard_map/all_to_all | solution.py:386
  80.2 1.9 %collective-permute-start.2 = (bf16[128,512]{1,0:T(8,128)(2,1)S(1)}, bf16[128,512]{1,0:T(8,128)(2,1)S(1)}, u32[]{:S(2)}, u32[]{:S(2)}) collective-permute-start(bf16[128,512]{1,0:T(8,128)(2,1)S(1)} %get-tuple-element.18), channel_id=1, source_target_pairs={{0,128},{128,256},{256,384},{384,0},{1,129},{129,257},{257,385},{3... | collective-permute-start | bytes 393224 | tf_op jit(solution)/shard_map/ppermute | solution.py:390
  82.1 5.2 %collective-permute-start.3 = (bf16[128,512]{1,0:T(8,128)(2,1)S(1)}, bf16[128,512]{1,0:T(8,128)(2,1)S(1)}, u32[]{:S(2)}, u32[]{:S(2)}) collective-permute-start(bf16[128,512]{1,0:T(8,128)(2,1)S(1)} %get-tuple-element.19), channel_id=1, source_target_pairs={{0,256},{128,384},{256,0},{384,128},{1,257},{129,385},{257,1},{385... | collective-permute-start | bytes 393224 | tf_op jit(solution)/shard_map/ppermute | solution.py:390
  87.3 2.7 %collective-permute-start.4 = (bf16[128,512]{1,0:T(8,128)(2,1)S(1)}, bf16[128,512]{1,0:T(8,128)(2,1)S(1)}, u32[]{:S(2)}, u32[]{:S(2)}) collective-permute-start(bf16[128,512]{1,0:T(8,128)(2,1)S(1)} %get-tuple-element.20), channel_id=1, source_target_pairs={{0,384},{128,0},{256,128},{384,256},{1,385},{129,1},{257,129},{385... | collective-permute-start | bytes 393224 | tf_op jit(solution)/shard_map/ppermute | solution.py:390
  89.9 0.0 collective-permute-done.2.refs_0_
  90.0 2.1 %collective-permute-done.3.refs_1_ = bf16[128,512]{1,0:T(8,128)(2,1)S(1)} collective-permute-done((bf16[128,512]{1,0:T(8,128)(2,1)S(1)}, bf16[128,512]{1,0:T(8,128)(2,1)S(1)}, u32[]{:S(2)}, u32[]{:S(2)}) %collective-permute-start.3) | collective-permute-done | bytes 131104 | tf_op jit(solution)/shard_map/ppermute | solution.py:390
  92.0 1.2 %collective-permute-done.4.refs_2_ = bf16[128,512]{1,0:T(8,128)(2,1)S(1)} collective-permute-done((bf16[128,512]{1,0:T(8,128)(2,1)S(1)}, bf16[128,512]{1,0:T(8,128)(2,1)S(1)}, u32[]{:S(2)}, u32[]{:S(2)}) %collective-permute-start.4) | collective-permute-done | bytes 131104 | tf_op jit(solution)/shard_map/ppermute | solution.py:390
  93.3 0.0 all-to-all-done.2.norm_ref
  93.3 1.8 %shard_map.51 = bf16[2,128,512]{2,1,0:T(8,128)(2,1)} custom-call(s32[1,128]{1,0:T(1,128)S(1)} %get-tuple-element.13.place_ref, f32[256,1,128]{2,1,0:T(1,128)S(1)} %all-to-all-done.2.norm_ref, bf16[128,512]{1,0:T(8,128)(2,1)S(1)} %get-tuple-element.17.raw_ref, bf16[128,512]{1,0:T(8,128)(2,1)S(1)} %collective-permute-done.2.refs_0_, ...), custom_call_target="tpu_custom_call" | custom-call | tf_op jit(solution)/shard_map/pallas_call | solution.py:391
Async XLA Ops:
  0.0 13.5 %copy-start = (bf16[128,4,512]{2,1,0:T(4,128)(2,1)S(1)}, bf16[128,4,512]{2,1,0:T(4,128)(2,1)}, u32[]{:S(2)}) copy-start(bf16[128,4,512]{2,1,0:T(4,128)(2,1)} %param.5) | copy-start | bytes 1572868
  3.2 22.5 %all-to-all-start = ((bf16[8,16,24,128]{3,2,1,0:T(8,128)(2,1)}), bf16[8,16,24,128]{3,2,1,0:T(8,128)(2,1)S(1)}, u32[]{:S(2)}, u32[]{:S(2)}) async-start(bf16[8,16,24,128]{3,2,1,0:T(8,128)(2,1)} %get-tuple-element.15), calls=%async_computation | async-start | bytes 1572864 | tf_op jit(solution)/shard_map/all_to_all | solution.py:359
  14.1 3.1 %collective-permute-start = (bf16[32,8,128]{2,1,0:T(8,128)(2,1)S(1)}, bf16[32,8,128]{2,1,0:T(8,128)(2,1)S(1)}, u32[]{:S(2)}, u32[]{:S(2)}) collective-permute-start(bf16[32,8,128]{2,1,0:T(8,128)(2,1)S(1)} %shard_map.47), channel_id=1, source_target_pairs={{0,1},{1,0},{2,3},{3,2},{4,5},{5,4},{6,7},{7,6},{8,9},{9,8},{10,11... | collective-permute-start | bytes 196616 | tf_op jit(solution)/shard_map/ppermute | solution.py:366
  60.2 8.1 %collective-permute-start.1 = (bf16[768,512]{1,0:T(8,128)(2,1)S(1)}, bf16[768,512]{1,0:T(8,128)(2,1)S(1)}, u32[]{:S(2)}, u32[]{:S(2)}) collective-permute-start(bf16[768,512]{1,0:T(8,128)(2,1)S(1)} %shard_map.49.mine_ref), channel_id=1, source_target_pairs={{0,1},{1,0},{2,3},{3,2},{4,5},{5,4},{6,7},{7,6},{8,9},{9,8},{10,11... | collective-permute-start | bytes 2359304 | tf_op jit(solution)/shard_map/ppermute | solution.py:377
  70.9 22.4 %all-to-all-start.2 = ((f32[256,1,128]{2,1,0:T(1,128)}), f32[256,1,128]{2,1,0:T(1,128)S(1)}, u32[]{:S(2)}, u32[]{:S(2)}) async-start(f32[256,1,128]{2,1,0:T(1,128)} %get-tuple-element.16), calls=%async_computation.2 | async-start | bytes 262144 | tf_op jit(solution)/shard_map/all_to_all | solution.py:386
  80.2 9.8 %collective-permute-start.2 = (bf16[128,512]{1,0:T(8,128)(2,1)S(1)}, bf16[128,512]{1,0:T(8,128)(2,1)S(1)}, u32[]{:S(2)}, u32[]{:S(2)}) collective-permute-start(bf16[128,512]{1,0:T(8,128)(2,1)S(1)} %get-tuple-element.18), channel_id=1, source_target_pairs={{0,128},{128,256},{256,384},{384,0},{1,129},{129,257},{257,385},{3... | collective-permute-start | bytes 393224 | tf_op jit(solution)/shard_map/ppermute | solution.py:390
  82.1 9.9 %collective-permute-start.3 = (bf16[128,512]{1,0:T(8,128)(2,1)S(1)}, bf16[128,512]{1,0:T(8,128)(2,1)S(1)}, u32[]{:S(2)}, u32[]{:S(2)}) collective-permute-start(bf16[128,512]{1,0:T(8,128)(2,1)S(1)} %get-tuple-element.19), channel_id=1, source_target_pairs={{0,256},{128,384},{256,0},{384,128},{1,257},{129,385},{257,1},{385... | collective-permute-start | bytes 393224 | tf_op jit(solution)/shard_map/ppermute | solution.py:390
  87.3 6.0 %collective-permute-start.4 = (bf16[128,512]{1,0:T(8,128)(2,1)S(1)}, bf16[128,512]{1,0:T(8,128)(2,1)S(1)}, u32[]{:S(2)}, u32[]{:S(2)}) collective-permute-start(bf16[128,512]{1,0:T(8,128)(2,1)S(1)} %get-tuple-element.20), channel_id=1, source_target_pairs={{0,384},{128,0},{256,128},{384,256},{1,385},{129,1},{257,129},{385... | collective-permute-start | bytes 393224 | tf_op jit(solution)/shard_map/ppermute | solution.py:390

commit v6 on v5

--- a/solution.py
+++ b/solution.py
@@ -27,10 +27,6 @@
 
 def held(x):
     return pltpu.with_memory_space_constraint(x, pltpu.VMEM)
-
-
-def in_smem(x):
-    return pltpu.with_memory_space_constraint(x, pltpu.SMEM)
 
 
 def in_hbm(x):
@@ -46,6 +42,11 @@
         scratch_shapes=list(scratch),
         compiler_params=pltpu.CompilerParams(vmem_limit_bytes=24 * 2**20),
     )
+
+
+def square_sum(x):
+    rows, width = x.shape
+    return jnp.sum(jnp.sum((x * x).reshape(rows // 8, 8, width), axis=0), keepdims=True)
 
 
 def packed(x):
@@ -188,8 +189,11 @@
     lax.fori_loop(0, each, step, 0, unroll=8 if each % 8 == 0 else 1)
 
 
-def sum_stats_body(order_ref, got_ref, grad_ref, theirs_ref, out_ref, *, groups, blocks):
+def sum_stats_body(info_ref, got_ref, grad_ref, theirs_ref, out_ref, order_ref, sem, *, groups, blocks):
+    move = pltpu.make_async_copy(info_ref, order_ref, sem)
+    move.start()
     out_ref[...] = jnp.zeros(out_ref.shape, bf16)
+    move.wait()
     me = lax.axis_index("dp")
     core = lax.axis_index("c")
     half = pl.ds(pl.multiple_of(8 * core, 8), 8)
@@ -240,7 +244,7 @@
             place = slice((2 * v + q) * chunk, (2 * v + q + 1) * chunk)
             out_ref[order:, place] = tile[v * order // 2 : (v + 1) * order // 2]
     a = a_ref[...]
-    mean = jnp.sum(a * a, keepdims=True) * (1.0 / (order * order))
+    mean = square_sum(a) * (1.0 / (order * order))
     magnitude = order * jnp.sqrt(mean + 1e-06)
     n = a * (0.25 / magnitude)
     nb = n.astype(bf16)
@@ -260,18 +264,18 @@
     out_ref[0:order] = (x * (1.0 / jnp.sqrt(jnp.sqrt(magnitude)))).astype(bf16)
 
 
-def raw_body(place_ref, mine_ref, other_ref, *refs):
-    norm_ref, raw_ref = refs[-2:]
-    out_refs = refs[:-2]
+def raw_body(scalars_ref, mine_ref, other_ref, *refs):
+    norm_ref, raw_ref, place_ref, sem = refs[-4:]
+    out_refs = refs[:-4]
+    move = pltpu.make_async_copy(scalars_ref, place_ref, sem)
+    move.start()
     groups = len(out_refs)
     order = mine_ref.shape[1]
     half, quarter = order // 2, order // groups
+    me_c, me_x = lax.axis_index("c"), lax.axis_index("dp")
+    grad_sq = square_sum(mine_ref[order:].astype(f32)) + square_sum(other_ref[order:].astype(f32))
+    move.wait()
     live, core, layer = place_ref[0, 0], place_ref[0, 1], place_ref[0, 2]
-    me_c, me_x = lax.axis_index("c"), lax.axis_index("dp")
-    grad_sq = jnp.zeros((1, 1), f32)
-    for ref in (mine_ref, other_ref):
-        wide = ref[order:].astype(f32)
-        grad_sq = grad_sq + jnp.sum(wide * wide, keepdims=True)
     lane = lax.broadcasted_iota(i32, (1, LANES), 1)
 
     def finish(left_ref, right_ref):
@@ -283,7 +287,7 @@
                 middle = middle + dot(left_ref[0:order, cols], ref[order:, cols])
             right = right_ref[pl.ds(pl.multiple_of(at * half, half), half), :]
             raw = raw + dot(middle.astype(bf16), right)
-        raw_sq = jnp.sum(raw * raw, keepdims=True)
+        raw_sq = square_sum(raw)
         norms = jnp.where(lane == layer, grad_sq, 0.0)
         norms = norms + jnp.where(lane == layer + LAYERS, raw_sq, 0.0)
         norms = jnp.where(live > 0, norms, 0.0)
@@ -303,29 +307,42 @@
         out_ref[...] = raw_ref[pl.ds(pl.multiple_of(start, quarter), quarter), :]
 
 
-def scale_body(place_ref, norm_ref, raw_ref, *refs):
-    out_ref = refs[-1]
-    groups = len(refs)
-    total = jnp.sum(norm_ref[...], axis=0)
+def scale_body(scalars_ref, norm_ref, raw_ref, *refs):
+    out_ref, out_vmem, place_ref, sems = refs[-4:]
+    others = refs[:-4]
+    groups = len(others) + 1
+    move = pltpu.make_async_copy(scalars_ref, place_ref, sems.at[0])
+    move.start()
+    chains = 8
+    length = norm_ref.shape[0] // chains
+    total = jnp.zeros((1, LANES), f32)
+    for number in range(chains):
+        total = total + jnp.sum(norm_ref[number * length : (number + 1) * length], axis=0)
     lane = lax.broadcasted_iota(i32, (1, LANES), 1)
     me_x = lax.axis_index("dp")
+    move.wait()
+    stores = []
     for s in range(OCAP):
         live, source, layer = place_ref[0, 3 + 3 * s], place_ref[0, 4 + 3 * s], place_ref[0, 5 + 3 * s]
         grad_total = jnp.sum(jnp.where(lane == layer, total, 0.0), keepdims=True)
         raw_total = jnp.sum(jnp.where(lane == layer + LAYERS, total, 0.0), keepdims=True)
         ratio = jnp.sqrt((grad_total + 1e-06) / (raw_total + 1e-06))
-        ratio = jnp.where(live > 0, ratio, 0.0)
         step = jnp.where(live > 0, (me_x - source) & (groups - 1), groups)
         for number in range(groups):
 
             @pl.when(step == number)
             def _(number=number, s=s, ratio=ratio):
-                block = raw_ref[...] if number == 0 else refs[number - 1][...]
-                out_ref[s] = (block.astype(f32) * ratio).astype(bf16)
+                block = raw_ref[...] if number == 0 else others[number - 1][...]
+                out_vmem[s] = (block.astype(f32) * ratio).astype(bf16)
 
         @pl.when(step == groups)
         def _(s=s):
-            out_ref[s] = jnp.zeros(out_ref.shape[1:], bf16)
+            out_vmem[s] = jnp.zeros(out_vmem.shape[1:], bf16)
+
+        stores.append(pltpu.make_async_copy(out_vmem.at[s], out_ref.at[s], sems.at[1 + s]))
+        stores[-1].start()
+    for store in stores:
+        store.wait()
 
 
 def on_device(stats_partial, gradient, owner_of, layer_count):
@@ -355,7 +372,7 @@
         ],
         (ANY, VMEM, VMEM),
     )(in_hbm(owner_of[None]), in_hbm(layer_count), in_hbm(stats))
-    order_info, place = in_smem(order_info), in_smem(place)
+    order_info, place = held(order_info), held(place)
     arrived = lax.all_to_all(outgoing, ("dp", "c"), 0, 0, tiled=True)
     grad = packed(gradient)
     grad_half = call(
@@ -367,7 +384,8 @@
     summed = call(
         functools.partial(sum_stats_body, groups=groups, blocks=blocks),
         pltpu.VMEM((columns, 40, chunk), bf16),
-        [SMEM, VMEM, VMEM, VMEM],
+        [VMEM, VMEM, VMEM, VMEM],
+        [pltpu.SMEM((1, blocks), i32), pltpu.SemaphoreType.DMA],
     )(order_info, held(arrived), grad, held(grad_theirs))
     statistic = lax.all_to_all(summed, ("z", "y"), 0, 0, tiled=True)
     bundle_shape = (order + order // 2, order)
@@ -379,8 +397,8 @@
         raw_body,
         tuple(pltpu.VMEM((quarter, order), bf16) for _ in range(groups))
         + (pltpu.VMEM((groups * columns, 1, LANES), f32),),
-        [SMEM, VMEM, VMEM],
-        [pltpu.VMEM((order, order), bf16)],
+        [VMEM, VMEM, VMEM],
+        [pltpu.VMEM((order, order), bf16), pltpu.SMEM(place.shape, i32), pltpu.SemaphoreType.DMA],
         (VMEM,) * (groups + 1),
     )(place, held(bundle), held(other))
     norms = lax.all_to_all(norms, ("dp", "z", "y"), 0, 0, tiled=True)
@@ -388,8 +406,17 @@
     for step in range(1, groups):
         pairs = [(i, (i + step) % groups) for i in range(groups)]
         spread.append(held(lax.ppermute(quarters[step], "dp", pairs)))
+    out_shape = (OCAP, quarter, order)
     out = call(
-        scale_body, struct((OCAP, quarter, order), bf16), [SMEM] + [VMEM] * (groups + 1)
+        scale_body,
+        struct(out_shape, bf16),
+        [VMEM] * (groups + 2),
+        [
+            pltpu.VMEM(out_shape, bf16),
+            pltpu.SMEM(place.shape, i32),
+            pltpu.SemaphoreType.DMA((1 + OCAP,)),
+        ],
+        ANY,
     )(place, held(norms), *spread)
     return out[None]
 

time: 96.3 us -> 95.4 us (level)
  no operation moved by 1% of the time
where the time goes in v6:
time: 95.4 us; the launch traced here: 94.2 us
  starting transfers between devices  37.6 us (39%)
  blocking collectives  30.4 us (32%)
  waiting for transfers between devices  14.7 us (15%)
  Pallas kernels  11.3 us (12%)
    all_to_all x1, blocking collectives, on_device(): statistic = lax.all_to_all(summed, ('z', 'y'), 0, 0, tiled=True)  30.4 us
    all_to_all x1, starting transfers between devices, on_device(): arrived = lax.all_to_all(outgoing, ('dp', 'c'), 0, 0, tiled=True)  10.3 us
    ppermute x3, starting transfers between devices, on_device(): spread.append(held(lax.ppermute(quarters[step], 'dp', pairs)))  9.75 us
    all_to_all x1, starting transfers between devices, on_device(): norms = lax.all_to_all(norms, ('dp', 'z', 'y'), 0, 0, tiled=True)  9.29 us
    all_to_all x1, waiting for transfers between devices, on_device(): arrived = lax.all_to_all(outgoing, ('dp', 'c'), 0, 0, tiled=True)  8.39 us
    ppermute x1, starting transfers between devices, on_device(): other = lax.ppermute(bundle, 'c', swap)  6.24 us
    ppermute x3, waiting for transfers between devices, on_device(): spread.append(held(lax.ppermute(quarters[step], 'dp', pairs)))  3.34 us
    pallas_call x1, Pallas kernels, on_device(): call(functools.partial(pack_stats_body, groups=groups, columns=columns),...  3.18 us
  transfers between devices with their start and end apart: 7, of which 5 were waited for; matrix products, arithmetic and copies ran while one was open for 0% of the time, Pallas kernels for 1%

profile of v6, /device:TPU:1, one launch (start us, length us, event | category | flops | bytes accessed | tf_op | source)
XLA Modules:
  0.0 94.2 jit_solution(9732000041036801116)
XLA Ops:
  0.0 0.0 copy-start
  0.0 3.2 %shard_map.46 = (bf16[8,16,24,128]{3,2,1,0:T(8,128)(2,1)}, s32[1,128]{1,0:T(1,128)S(1)}, s32[1,128]{1,0:T(1,128)S(1)}) custom-call(s32[1,128]{1,0:T(1,128)} %bitcast.15, s32[4]{0:T(128)} %count_ref.1, f32[256,16,128]{2,1,0:T(8,128)} %bitcast.14), custom_call_target="tpu_custom_call" | custom-call | tf_op jit(solution)/shard_map/pallas_call | solution.py:361
  3.2 10.3 %all-to-all-start = ((bf16[8,16,24,128]{3,2,1,0:T(8,128)(2,1)}), bf16[8,16,24,128]{3,2,1,0:T(8,128)(2,1)S(1)}, u32[]{:S(2)}, u32[]{:S(2)}) async-start(bf16[8,16,24,128]{3,2,1,0:T(8,128)(2,1)} %get-tuple-element.15), calls=%async_computation | async-start | bytes 1572864 | tf_op jit(solution)/shard_map/all_to_all | solution.py:376
  13.5 0.0 copy-done
  13.5 0.6 shard_map.47
  14.1 2.0 %collective-permute-start = (bf16[32,8,128]{2,1,0:T(8,128)(2,1)S(1)}, bf16[32,8,128]{2,1,0:T(8,128)(2,1)S(1)}, u32[]{:S(2)}, u32[]{:S(2)}) collective-permute-start(bf16[32,8,128]{2,1,0:T(8,128)(2,1)S(1)} %shard_map.47), channel_id=1, source_target_pairs={{0,1},{1,0},{2,3},{3,2},{4,5},{5,4},{6,7},{7,6},{8,9},{9,8},{10,11... | collective-permute-start | bytes 196616 | tf_op jit(solution)/shard_map/ppermute | solution.py:383
  16.2 1.1 %collective-permute-done.theirs_ref = bf16[32,8,128]{2,1,0:T(8,128)(2,1)S(1)} collective-permute-done((bf16[32,8,128]{2,1,0:T(8,128)(2,1)S(1)}, bf16[32,8,128]{2,1,0:T(8,128)(2,1)S(1)}, u32[]{:S(2)}, u32[]{:S(2)}) %collective-permute-start) | collective-permute-done | bytes 65568 | tf_op jit(solution)/shard_map/ppermute | solution.py:383
  17.3 8.4 %all-to-all-done.got_ref = bf16[8,16,24,128]{3,2,1,0:T(8,128)(2,1)S(1)} async-done(((bf16[8,16,24,128]{3,2,1,0:T(8,128)(2,1)}), bf16[8,16,24,128]{3,2,1,0:T(8,128)(2,1)S(1)}, u32[]{:S(2)}, u32[]{:S(2)}) %all-to-all-start) | async-done | bytes 786464 | tf_op jit(solution)/shard_map/all_to_all | solution.py:376
  25.7 0.8 shard_map.48
  26.5 30.4 %all_to_all.15.got_ref = bf16[64,40,128]{2,1,0:T(8,128)(2,1)S(1)} all-to-all(bf16[64,40,128]{2,1,0:T(8,128)(2,1)S(1)} %shard_map.48), channel_id=1, replica_groups=mesh['dp'=4,'z'=8,'y'=8,'c'=2] {'z','y'}, dimensions={0} | all-to-all | bytes 1310720 | tf_op jit(solution)/shard_map/all_to_all | solution.py:390
  56.9 3.0 %shard_map.49.mine_ref = bf16[768,512]{1,0:T(8,128)(2,1)S(1)} custom-call(bf16[64,40,128]{2,1,0:T(8,128)(2,1)S(1)} %all_to_all.15.got_ref), custom_call_target="tpu_custom_call" | custom-call | tf_op jit(solution)/shard_map/pallas_call | solution.py:392
  59.9 6.2 %collective-permute-start.1 = (bf16[768,512]{1,0:T(8,128)(2,1)S(1)}, bf16[768,512]{1,0:T(8,128)(2,1)S(1)}, u32[]{:S(2)}, u32[]{:S(2)}) collective-permute-start(bf16[768,512]{1,0:T(8,128)(2,1)S(1)} %shard_map.49.mine_ref), channel_id=1, source_target_pairs={{0,1},{1,0},{2,3},{3,2},{4,5},{5,4},{6,7},{7,6},{8,9},{9,8},{10,11... | collective-permute-start | bytes 2359304 | tf_op jit(solution)/shard_map/ppermute | solution.py:395
  66.2 1.9 %collective-permute-done.1.other_ref = bf16[768,512]{1,0:T(8,128)(2,1)S(1)} collective-permute-done((bf16[768,512]{1,0:T(8,128)(2,1)S(1)}, bf16[768,512]{1,0:T(8,128)(2,1)S(1)}, u32[]{:S(2)}, u32[]{:S(2)}) %collective-permute-start.1) | collective-permute-done | bytes 786464 | tf_op jit(solution)/shard_map/ppermute | solution.py:395
  68.1 2.2 %shard_map.50 = (bf16[128,512]{1,0:T(8,128)(2,1)S(1)}, bf16[128,512]{1,0:T(8,128)(2,1)S(1)}, bf16[128,512]{1,0:T(8,128)(2,1)S(1)}, bf16[128,512]{1,0:T(8,128)(2,1)S(1)}, f32[256,1,128]{2,1,0:T(1,128)}) custom-call(s32[1,128]{1,0:T(1,128)S(1)} %get-tuple-element.13.scalars_ref, bf16[768,512]{1,0:T(8,128)(2,1)S(1)} %shard_map.49.mine_ref, ...), custom_call_target="tpu_custom_call" | custom-call | tf_op jit(solution)/shard_map/pallas_call | solution.py:396
  70.3 9.3 %all-to-all-start.2 = ((f32[256,1,128]{2,1,0:T(1,128)}), f32[256,1,128]{2,1,0:T(1,128)S(1)}, u32[]{:S(2)}, u32[]{:S(2)}) async-start(f32[256,1,128]{2,1,0:T(1,128)} %get-tuple-element.16), calls=%async_computation.2 | async-start | bytes 262144 | tf_op jit(solution)/shard_map/all_to_all | solution.py:404
  79.6 1.9 %collective-permute-start.2 = (bf16[128,512]{1,0:T(8,128)(2,1)S(1)}, bf16[128,512]{1,0:T(8,128)(2,1)S(1)}, u32[]{:S(2)}, u32[]{:S(2)}) collective-permute-start(bf16[128,512]{1,0:T(8,128)(2,1)S(1)} %get-tuple-element.18), channel_id=1, source_target_pairs={{0,128},{128,256},{256,384},{384,0},{1,129},{129,257},{257,385},{3... | collective-permute-start | bytes 393224 | tf_op jit(solution)/shard_map/ppermute | solution.py:408
  81.5 5.2 %collective-permute-start.3 = (bf16[128,512]{1,0:T(8,128)(2,1)S(1)}, bf16[128,512]{1,0:T(8,128)(2,1)S(1)}, u32[]{:S(2)}, u32[]{:S(2)}) collective-permute-start(bf16[128,512]{1,0:T(8,128)(2,1)S(1)} %get-tuple-element.19), channel_id=1, source_target_pairs={{0,256},{128,384},{256,0},{384,128},{1,257},{129,385},{257,1},{385... | collective-permute-start | bytes 393224 | tf_op jit(solution)/shard_map/ppermute | solution.py:408
  86.7 2.7 %collective-permute-start.4 = (bf16[128,512]{1,0:T(8,128)(2,1)S(1)}, bf16[128,512]{1,0:T(8,128)(2,1)S(1)}, u32[]{:S(2)}, u32[]{:S(2)}) collective-permute-start(bf16[128,512]{1,0:T(8,128)(2,1)S(1)} %get-tuple-element.20), channel_id=1, source_target_pairs={{0,384},{128,0},{256,128},{384,256},{1,385},{129,1},{257,129},{385... | collective-permute-start | bytes 393224 | tf_op jit(solution)/shard_map/ppermute | solution.py:408
  89.3 0.0 collective-permute-done.2.refs_0_
  89.3 2.1 %collective-permute-done.3.refs_1_ = bf16[128,512]{1,0:T(8,128)(2,1)S(1)} collective-permute-done((bf16[128,512]{1,0:T(8,128)(2,1)S(1)}, bf16[128,512]{1,0:T(8,128)(2,1)S(1)}, u32[]{:S(2)}, u32[]{:S(2)}) %collective-permute-start.3) | collective-permute-done | bytes 131104 | tf_op jit(solution)/shard_map/ppermute | solution.py:408
  91.4 1.2 %collective-permute-done.4.refs_2_ = bf16[128,512]{1,0:T(8,128)(2,1)S(1)} collective-permute-done((bf16[128,512]{1,0:T(8,128)(2,1)S(1)}, bf16[128,512]{1,0:T(8,128)(2,1)S(1)}, u32[]{:S(2)}, u32[]{:S(2)}) %collective-permute-start.4) | collective-permute-done | bytes 131104 | tf_op jit(solution)/shard_map/ppermute | solution.py:408
  92.7 0.0 all-to-all-done.2.norm_ref
  92.7 1.5 %shard_map.51 = bf16[2,128,512]{2,1,0:T(8,128)(2,1)} custom-call(s32[1,128]{1,0:T(1,128)S(1)} %get-tuple-element.13.scalars_ref, f32[256,1,128]{2,1,0:T(1,128)S(1)} %all-to-all-done.2.norm_ref, bf16[128,512]{1,0:T(8,128)(2,1)S(1)} %get-tuple-element.17.raw_ref, bf16[128,512]{1,0:T(8,128)(2,1)S(1)} %collective-permute-done.2.refs_0_, ...), custom_call_target="tpu_custom_call" | custom-call | tf_op jit(solution)/shard_map/pallas_call | solution.py:410
Async XLA Ops:
  0.0 13.5 %copy-start = (bf16[128,4,512]{2,1,0:T(4,128)(2,1)S(1)}, bf16[128,4,512]{2,1,0:T(4,128)(2,1)}, u32[]{:S(2)}) copy-start(bf16[128,4,512]{2,1,0:T(4,128)(2,1)} %param.5) | copy-start | bytes 1572868
  3.2 22.5 %all-to-all-start = ((bf16[8,16,24,128]{3,2,1,0:T(8,128)(2,1)}), bf16[8,16,24,128]{3,2,1,0:T(8,128)(2,1)S(1)}, u32[]{:S(2)}, u32[]{:S(2)}) async-start(bf16[8,16,24,128]{3,2,1,0:T(8,128)(2,1)} %get-tuple-element.15), calls=%async_computation | async-start | bytes 1572864 | tf_op jit(solution)/shard_map/all_to_all | solution.py:376
  14.1 3.1 %collective-permute-start = (bf16[32,8,128]{2,1,0:T(8,128)(2,1)S(1)}, bf16[32,8,128]{2,1,0:T(8,128)(2,1)S(1)}, u32[]{:S(2)}, u32[]{:S(2)}) collective-permute-start(bf16[32,8,128]{2,1,0:T(8,128)(2,1)S(1)} %shard_map.47), channel_id=1, source_target_pairs={{0,1},{1,0},{2,3},{3,2},{4,5},{5,4},{6,7},{7,6},{8,9},{9,8},{10,11... | collective-permute-start | bytes 196616 | tf_op jit(solution)/shard_map/ppermute | solution.py:383
  59.9 8.1 %collective-permute-start.1 = (bf16[768,512]{1,0:T(8,128)(2,1)S(1)}, bf16[768,512]{1,0:T(8,128)(2,1)S(1)}, u32[]{:S(2)}, u32[]{:S(2)}) collective-permute-start(bf16[768,512]{1,0:T(8,128)(2,1)S(1)} %shard_map.49.mine_ref), channel_id=1, source_target_pairs={{0,1},{1,0},{2,3},{3,2},{4,5},{5,4},{6,7},{7,6},{8,9},{9,8},{10,11... | collective-permute-start | bytes 2359304 | tf_op jit(solution)/shard_map/ppermute | solution.py:395
  70.3 22.4 %all-to-all-start.2 = ((f32[256,1,128]{2,1,0:T(1,128)}), f32[256,1,128]{2,1,0:T(1,128)S(1)}, u32[]{:S(2)}, u32[]{:S(2)}) async-start(f32[256,1,128]{2,1,0:T(1,128)} %get-tuple-element.16), calls=%async_computation.2 | async-start | bytes 262144 | tf_op jit(solution)/shard_map/all_to_all | solution.py:404
  79.6 9.8 %collective-permute-start.2 = (bf16[128,512]{1,0:T(8,128)(2,1)S(1)}, bf16[128,512]{1,0:T(8,128)(2,1)S(1)}, u32[]{:S(2)}, u32[]{:S(2)}) collective-permute-start(bf16[128,512]{1,0:T(8,128)(2,1)S(1)} %get-tuple-element.18), channel_id=1, source_target_pairs={{0,128},{128,256},{256,384},{384,0},{1,129},{129,257},{257,385},{3... | collective-permute-start | bytes 393224 | tf_op jit(solution)/shard_map/ppermute | solution.py:408
  81.5 9.9 %collective-permute-start.3 = (bf16[128,512]{1,0:T(8,128)(2,1)S(1)}, bf16[128,512]{1,0:T(8,128)(2,1)S(1)}, u32[]{:S(2)}, u32[]{:S(2)}) collective-permute-start(bf16[128,512]{1,0:T(8,128)(2,1)S(1)} %get-tuple-element.19), channel_id=1, source_target_pairs={{0,256},{128,384},{256,0},{384,128},{1,257},{129,385},{257,1},{385... | collective-permute-start | bytes 393224 | tf_op jit(solution)/shard_map/ppermute | solution.py:408
  86.7 6.0 %collective-permute-start.4 = (bf16[128,512]{1,0:T(8,128)(2,1)S(1)}, bf16[128,512]{1,0:T(8,128)(2,1)S(1)}, u32[]{:S(2)}, u32[]{:S(2)}) collective-permute-start(bf16[128,512]{1,0:T(8,128)(2,1)S(1)} %get-tuple-element.20), channel_id=1, source_target_pairs={{0,384},{128,0},{256,128},{384,256},{1,385},{129,1},{257,129},{385... | collective-permute-start | bytes 393224 | tf_op jit(solution)/shard_map/ppermute | solution.py:408

commit v7 on v6

--- a/solution.py
+++ b/solution.py
@@ -189,7 +189,7 @@
     lax.fori_loop(0, each, step, 0, unroll=8 if each % 8 == 0 else 1)
 
 
-def sum_stats_body(info_ref, got_ref, grad_ref, theirs_ref, out_ref, order_ref, sem, *, groups, blocks):
+def sum_stats_body(info_ref, got_ref, grad_ref, theirs_ref, out_ref, order_ref, sem, *, groups, blocks, tall, wide):
     move = pltpu.make_async_copy(info_ref, order_ref, sem)
     move.start()
     out_ref[...] = jnp.zeros(out_ref.shape, bf16)
@@ -209,6 +209,7 @@
         for k in range(2):
             info = order_ref[0, (2 * i + k) * groups + me]
             column = (info >> (bits(blocks) + 1)) & (out_ref.shape[0] - 1)
+            column = ((column & (wide - 1)) << bits(tall)) + (column >> bits(wide))
             mine = grad_ref[info & (blocks - 1), half, :].astype(f32)
             theirs = theirs_ref[2 * i + k].astype(f32)
             grad = joined(jnp.where(core == 0, mine, theirs), jnp.where(core == 0, theirs, mine))
@@ -226,20 +227,27 @@
     return jnp.dot(a, b, preferred_element_type=f32)
 
 
-def newton_body(got_ref, out_ref, a_ref):
+def newton_body(got_ref, out_ref, a_ref, *, tall, wide):
     order = out_ref.shape[1]
     chunk = got_ref.shape[2]
-    each = chunk // 8
-    for row in range(4):
-        rows = slice(row * chunk, (row + 1) * chunk)
-        for number, q in enumerate((row // 2 * 2, row // 2 * 2 + 1, SINGLE[row])):
-            tile = got_ref[row * each : (row + 1) * each, 8 * number : 8 * number + 8, :]
-            tile = tile.astype(f32).reshape(chunk, chunk)
-            a_ref[rows, q * chunk : (q + 1) * chunk] = tile
+
+    def column(number):
+        tiles = [
+            got_ref[pl.ds(z, wide, stride=tall), 8 * number : 8 * number + 8, :].astype(f32)
+            for z in range(tall)
+        ]
+        return jnp.concatenate([tile.reshape(8 * wide, chunk) for tile in tiles], axis=0)
+
+    for number in range(3):
+        tiles = column(number)
+        for row in range(4):
+            q = (row // 2 * 2, row // 2 * 2 + 1, SINGLE[row])[number]
+            rows = slice(row * chunk, (row + 1) * chunk)
+            a_ref[rows, q * chunk : (q + 1) * chunk] = tiles[rows]
             if MISSING[q] == row:
-                a_ref[q * chunk : (q + 1) * chunk, rows] = tile.T
+                a_ref[q * chunk : (q + 1) * chunk, rows] = tiles[rows].T
     for q in range(2):
-        tile = got_ref[:, 24 + 8 * q : 32 + 8 * q, :].astype(f32).reshape(order, chunk).astype(bf16)
+        tile = column(3 + q).astype(bf16)
         for v in range(2):
             place = slice((2 * v + q) * chunk, (2 * v + q + 1) * chunk)
             out_ref[order:, place] = tile[v * order // 2 : (v + 1) * order // 2]
@@ -355,6 +363,7 @@
     chunk = order // 4
     struct = jax.ShapeDtypeStruct
     swap = [(0, 1), (1, 0)]
+    sides = dict(tall=lax.axis_size("z"), wide=lax.axis_size("y"))
 
     stats = packed(stats_partial.reshape(2 * blocks, local_rows, order))
     out_shape = (2 * groups, each // 2, 24, chunk)
@@ -382,15 +391,18 @@
     )(order_info, grad)
     grad_theirs = lax.ppermute(grad_half, "c", swap)
     summed = call(
-        functools.partial(sum_stats_body, groups=groups, blocks=blocks),
+        functools.partial(sum_stats_body, groups=groups, blocks=blocks, **sides),
         pltpu.VMEM((columns, 40, chunk), bf16),
         [VMEM, VMEM, VMEM, VMEM],
         [pltpu.SMEM((1, blocks), i32), pltpu.SemaphoreType.DMA],
     )(order_info, held(arrived), grad, held(grad_theirs))
-    statistic = lax.all_to_all(summed, ("z", "y"), 0, 0, tiled=True)
+    statistic = lax.all_to_all(summed, ("y", "z"), 0, 0, tiled=True)
     bundle_shape = (order + order // 2, order)
     bundle = call(
-        newton_body, pltpu.VMEM(bundle_shape, bf16), [VMEM], [pltpu.VMEM((order, order), f32)]
+        functools.partial(newton_body, **sides),
+        pltpu.VMEM(bundle_shape, bf16),
+        [VMEM],
+        [pltpu.VMEM((order, order), f32)],
     )(held(statistic))
     other = lax.ppermute(bundle, "c", swap)
     *quarters, norms = call(
@@ -401,7 +413,7 @@
         [pltpu.VMEM((order, order), bf16), pltpu.SMEM(place.shape, i32), pltpu.SemaphoreType.DMA],
         (VMEM,) * (groups + 1),
     )(place, held(bundle), held(other))
-    norms = lax.all_to_all(norms, ("dp", "z", "y"), 0, 0, tiled=True)
+    norms = lax.all_to_all(norms, ("y", "z", "dp"), 0, 0, tiled=True)
     spread = [held(quarters[0])]
     for step in range(1, groups):
         pairs = [(i, (i + step) % groups) for i in range(groups)]

time: 95.4 us -> 94.8 us (level)
  no operation moved by 1% of the time
where the time goes in v7:
time: 94.8 us; the launch traced here: 94.2 us
  starting transfers between devices  37.1 us (39%)
  blocking collectives  30.1 us (32%)
  waiting for transfers between devices  15.5 us (16%)
  Pallas kernels  11.3 us (12%)
    all_to_all x1, blocking collectives, on_device(): statistic = lax.all_to_all(summed, ('y', 'z'), 0, 0, tiled=True)  30.1 us
    all_to_all x1, starting transfers between devices, on_device(): arrived = lax.all_to_all(outgoing, ('dp', 'c'), 0, 0, tiled=True)  10.3 us
    all_to_all x1, starting transfers between devices, on_device(): norms = lax.all_to_all(norms, ('y', 'z', 'dp'), 0, 0, tiled=True)  10.1 us
    ppermute x3, starting transfers between devices, on_device(): spread.append(held(lax.ppermute(quarters[step], 'dp', pairs)))  9 us
    all_to_all x1, waiting for transfers between devices, on_device(): arrived = lax.all_to_all(outgoing, ('dp', 'c'), 0, 0, tiled=True)  8.39 us
    ppermute x1, starting transfers between devices, on_device(): other = lax.ppermute(bundle, 'c', swap)  5.74 us
    ppermute x3, waiting for transfers between devices, on_device(): spread.append(held(lax.ppermute(quarters[step], 'dp', pairs)))  4.14 us
    pallas_call x1, Pallas kernels, on_device(): call(functools.partial(pack_stats_body, groups=groups, columns=columns),...  3.18 us
  transfers between devices with their start and end apart: 7, of which 5 were waited for; matrix products, arithmetic and copies ran while one was open for 0% of the time, Pallas kernels for 1%

profile of v7, /device:TPU:1, one launch (start us, length us, event | category | flops | bytes accessed | tf_op | source)
XLA Modules:
  0.0 94.2 jit_solution(7911952122356346318)
XLA Ops:
  0.0 0.0 copy-start
  0.0 3.2 %shard_map.46 = (bf16[8,16,24,128]{3,2,1,0:T(8,128)(2,1)}, s32[1,128]{1,0:T(1,128)S(1)}, s32[1,128]{1,0:T(1,128)S(1)}) custom-call(s32[1,128]{1,0:T(1,128)} %bitcast.15, s32[4]{0:T(128)} %count_ref.1, f32[256,16,128]{2,1,0:T(8,128)} %bitcast.14), custom_call_target="tpu_custom_call" | custom-call | tf_op jit(solution)/shard_map/pallas_call | solution.py:370
  3.2 10.3 %all-to-all-start = ((bf16[8,16,24,128]{3,2,1,0:T(8,128)(2,1)}), bf16[8,16,24,128]{3,2,1,0:T(8,128)(2,1)S(1)}, u32[]{:S(2)}, u32[]{:S(2)}) async-start(bf16[8,16,24,128]{3,2,1,0:T(8,128)(2,1)} %get-tuple-element.15), calls=%async_computation | async-start | bytes 1572864 | tf_op jit(solution)/shard_map/all_to_all | solution.py:385
  13.5 0.0 copy-done
  13.5 0.6 shard_map.47
  14.1 2.0 %collective-permute-start = (bf16[32,8,128]{2,1,0:T(8,128)(2,1)S(1)}, bf16[32,8,128]{2,1,0:T(8,128)(2,1)S(1)}, u32[]{:S(2)}, u32[]{:S(2)}) collective-permute-start(bf16[32,8,128]{2,1,0:T(8,128)(2,1)S(1)} %shard_map.47), channel_id=1, source_target_pairs={{0,1},{1,0},{2,3},{3,2},{4,5},{5,4},{6,7},{7,6},{8,9},{9,8},{10,11... | collective-permute-start | bytes 196616 | tf_op jit(solution)/shard_map/ppermute | solution.py:392
  16.2 1.1 %collective-permute-done.theirs_ref = bf16[32,8,128]{2,1,0:T(8,128)(2,1)S(1)} collective-permute-done((bf16[32,8,128]{2,1,0:T(8,128)(2,1)S(1)}, bf16[32,8,128]{2,1,0:T(8,128)(2,1)S(1)}, u32[]{:S(2)}, u32[]{:S(2)}) %collective-permute-start) | collective-permute-done | bytes 65568 | tf_op jit(solution)/shard_map/ppermute | solution.py:392
  17.3 8.4 %all-to-all-done.got_ref = bf16[8,16,24,128]{3,2,1,0:T(8,128)(2,1)S(1)} async-done(((bf16[8,16,24,128]{3,2,1,0:T(8,128)(2,1)}), bf16[8,16,24,128]{3,2,1,0:T(8,128)(2,1)S(1)}, u32[]{:S(2)}, u32[]{:S(2)}) %all-to-all-start) | async-done | bytes 786464 | tf_op jit(solution)/shard_map/all_to_all | solution.py:385
  25.7 0.8 shard_map.48
  26.5 30.1 %all_to_all.15.got_ref = bf16[64,40,128]{2,1,0:T(8,128)(2,1)S(1)} all-to-all(bf16[64,40,128]{2,1,0:T(8,128)(2,1)S(1)} %shard_map.48), channel_id=1, replica_groups=mesh['dp'=4,'z'=8,'y'=8,'c'=2] {'y','z'}, dimensions={0} | all-to-all | bytes 1310720 | tf_op jit(solution)/shard_map/all_to_all | solution.py:399
  56.5 3.0 %shard_map.49.mine_ref = bf16[768,512]{1,0:T(8,128)(2,1)S(1)} custom-call(bf16[64,40,128]{2,1,0:T(8,128)(2,1)S(1)} %all_to_all.15.got_ref), custom_call_target="tpu_custom_call" | custom-call | tf_op jit(solution)/shard_map/pallas_call | solution.py:401
  59.5 5.7 %collective-permute-start.1 = (bf16[768,512]{1,0:T(8,128)(2,1)S(1)}, bf16[768,512]{1,0:T(8,128)(2,1)S(1)}, u32[]{:S(2)}, u32[]{:S(2)}) collective-permute-start(bf16[768,512]{1,0:T(8,128)(2,1)S(1)} %shard_map.49.mine_ref), channel_id=1, source_target_pairs={{0,1},{1,0},{2,3},{3,2},{4,5},{5,4},{6,7},{7,6},{8,9},{9,8},{10,11... | collective-permute-start | bytes 2359304 | tf_op jit(solution)/shard_map/ppermute | solution.py:407
  65.3 1.9 %collective-permute-done.1.other_ref = bf16[768,512]{1,0:T(8,128)(2,1)S(1)} collective-permute-done((bf16[768,512]{1,0:T(8,128)(2,1)S(1)}, bf16[768,512]{1,0:T(8,128)(2,1)S(1)}, u32[]{:S(2)}, u32[]{:S(2)}) %collective-permute-start.1) | collective-permute-done | bytes 786464 | tf_op jit(solution)/shard_map/ppermute | solution.py:407
  67.2 2.2 %shard_map.50 = (bf16[128,512]{1,0:T(8,128)(2,1)S(1)}, bf16[128,512]{1,0:T(8,128)(2,1)S(1)}, bf16[128,512]{1,0:T(8,128)(2,1)S(1)}, bf16[128,512]{1,0:T(8,128)(2,1)S(1)}, f32[256,1,128]{2,1,0:T(1,128)}) custom-call(s32[1,128]{1,0:T(1,128)S(1)} %get-tuple-element.13.scalars_ref, bf16[768,512]{1,0:T(8,128)(2,1)S(1)} %shard_map.49.mine_ref, ...), custom_call_target="tpu_custom_call" | custom-call | tf_op jit(solution)/shard_map/pallas_call | solution.py:408
  69.4 10.1 %all-to-all-start.2 = ((f32[256,1,128]{2,1,0:T(1,128)}), f32[256,1,128]{2,1,0:T(1,128)S(1)}, u32[]{:S(2)}, u32[]{:S(2)}) async-start(f32[256,1,128]{2,1,0:T(1,128)} %get-tuple-element.16), calls=%async_computation.2 | async-start | bytes 262144 | tf_op jit(solution)/shard_map/all_to_all | solution.py:416
  79.4 1.9 %collective-permute-start.2 = (bf16[128,512]{1,0:T(8,128)(2,1)S(1)}, bf16[128,512]{1,0:T(8,128)(2,1)S(1)}, u32[]{:S(2)}, u32[]{:S(2)}) collective-permute-start(bf16[128,512]{1,0:T(8,128)(2,1)S(1)} %get-tuple-element.18), channel_id=1, source_target_pairs={{0,128},{128,256},{256,384},{384,0},{1,129},{129,257},{257,385},{3... | collective-permute-start | bytes 393224 | tf_op jit(solution)/shard_map/ppermute | solution.py:420
  81.4 4.0 %collective-permute-start.3 = (bf16[128,512]{1,0:T(8,128)(2,1)S(1)}, bf16[128,512]{1,0:T(8,128)(2,1)S(1)}, u32[]{:S(2)}, u32[]{:S(2)}) collective-permute-start(bf16[128,512]{1,0:T(8,128)(2,1)S(1)} %get-tuple-element.19), channel_id=1, source_target_pairs={{0,256},{128,384},{256,0},{384,128},{1,257},{129,385},{257,1},{385... | collective-permute-start | bytes 393224 | tf_op jit(solution)/shard_map/ppermute | solution.py:420
  85.4 3.1 %collective-permute-start.4 = (bf16[128,512]{1,0:T(8,128)(2,1)S(1)}, bf16[128,512]{1,0:T(8,128)(2,1)S(1)}, u32[]{:S(2)}, u32[]{:S(2)}) collective-permute-start(bf16[128,512]{1,0:T(8,128)(2,1)S(1)} %get-tuple-element.20), channel_id=1, source_target_pairs={{0,384},{128,0},{256,128},{384,256},{1,385},{129,1},{257,129},{385... | collective-permute-start | bytes 393224 | tf_op jit(solution)/shard_map/ppermute | solution.py:420
  88.5 0.0 collective-permute-done.2.refs_0_
  88.5 2.4 %collective-permute-done.3.refs_1_ = bf16[128,512]{1,0:T(8,128)(2,1)S(1)} collective-permute-done((bf16[128,512]{1,0:T(8,128)(2,1)S(1)}, bf16[128,512]{1,0:T(8,128)(2,1)S(1)}, u32[]{:S(2)}, u32[]{:S(2)}) %collective-permute-start.3) | collective-permute-done | bytes 131104 | tf_op jit(solution)/shard_map/ppermute | solution.py:420
  90.9 1.8 %collective-permute-done.4.refs_2_ = bf16[128,512]{1,0:T(8,128)(2,1)S(1)} collective-permute-done((bf16[128,512]{1,0:T(8,128)(2,1)S(1)}, bf16[128,512]{1,0:T(8,128)(2,1)S(1)}, u32[]{:S(2)}, u32[]{:S(2)}) %collective-permute-start.4) | collective-permute-done | bytes 131104 | tf_op jit(solution)/shard_map/ppermute | solution.py:420
  92.6 0.0 all-to-all-done.2.norm_ref
  92.6 1.5 %shard_map.51 = bf16[2,128,512]{2,1,0:T(8,128)(2,1)} custom-call(s32[1,128]{1,0:T(1,128)S(1)} %get-tuple-element.13.scalars_ref, f32[256,1,128]{2,1,0:T(1,128)S(1)} %all-to-all-done.2.norm_ref, bf16[128,512]{1,0:T(8,128)(2,1)S(1)} %get-tuple-element.17.raw_ref, bf16[128,512]{1,0:T(8,128)(2,1)S(1)} %collective-permute-done.2.refs_0_, ...), custom_call_target="tpu_custom_call" | custom-call | tf_op jit(solution)/shard_map/pallas_call | solution.py:422
Async XLA Ops:
  0.0 13.5 %copy-start = (bf16[128,4,512]{2,1,0:T(4,128)(2,1)S(1)}, bf16[128,4,512]{2,1,0:T(4,128)(2,1)}, u32[]{:S(2)}) copy-start(bf16[128,4,512]{2,1,0:T(4,128)(2,1)} %param.5) | copy-start | bytes 1572868
  3.2 22.5 %all-to-all-start = ((bf16[8,16,24,128]{3,2,1,0:T(8,128)(2,1)}), bf16[8,16,24,128]{3,2,1,0:T(8,128)(2,1)S(1)}, u32[]{:S(2)}, u32[]{:S(2)}) async-start(bf16[8,16,24,128]{3,2,1,0:T(8,128)(2,1)} %get-tuple-element.15), calls=%async_computation | async-start | bytes 1572864 | tf_op jit(solution)/shard_map/all_to_all | solution.py:385
  14.1 3.1 %collective-permute-start = (bf16[32,8,128]{2,1,0:T(8,128)(2,1)S(1)}, bf16[32,8,128]{2,1,0:T(8,128)(2,1)S(1)}, u32[]{:S(2)}, u32[]{:S(2)}) collective-permute-start(bf16[32,8,128]{2,1,0:T(8,128)(2,1)S(1)} %shard_map.47), channel_id=1, source_target_pairs={{0,1},{1,0},{2,3},{3,2},{4,5},{5,4},{6,7},{7,6},{8,9},{9,8},{10,11... | collective-permute-start | bytes 196616 | tf_op jit(solution)/shard_map/ppermute | solution.py:392
  59.5 7.6 %collective-permute-start.1 = (bf16[768,512]{1,0:T(8,128)(2,1)S(1)}, bf16[768,512]{1,0:T(8,128)(2,1)S(1)}, u32[]{:S(2)}, u32[]{:S(2)}) collective-permute-start(bf16[768,512]{1,0:T(8,128)(2,1)S(1)} %shard_map.49.mine_ref), channel_id=1, source_target_pairs={{0,1},{1,0},{2,3},{3,2},{4,5},{5,4},{6,7},{7,6},{8,9},{9,8},{10,11... | collective-permute-start | bytes 2359304 | tf_op jit(solution)/shard_map/ppermute | solution.py:407
  69.4 23.2 %all-to-all-start.2 = ((f32[256,1,128]{2,1,0:T(1,128)}), f32[256,1,128]{2,1,0:T(1,128)S(1)}, u32[]{:S(2)}, u32[]{:S(2)}) async-start(f32[256,1,128]{2,1,0:T(1,128)} %get-tuple-element.16), calls=%async_computation.2 | async-start | bytes 262144 | tf_op jit(solution)/shard_map/all_to_all | solution.py:416
  79.4 9.0 %collective-permute-start.2 = (bf16[128,512]{1,0:T(8,128)(2,1)S(1)}, bf16[128,512]{1,0:T(8,128)(2,1)S(1)}, u32[]{:S(2)}, u32[]{:S(2)}) collective-permute-start(bf16[128,512]{1,0:T(8,128)(2,1)S(1)} %get-tuple-element.18), channel_id=1, source_target_pairs={{0,128},{128,256},{256,384},{384,0},{1,129},{129,257},{257,385},{3... | collective-permute-start | bytes 393224 | tf_op jit(solution)/shard_map/ppermute | solution.py:420
  81.4 9.5 %collective-permute-start.3 = (bf16[128,512]{1,0:T(8,128)(2,1)S(1)}, bf16[128,512]{1,0:T(8,128)(2,1)S(1)}, u32[]{:S(2)}, u32[]{:S(2)}) collective-permute-start(bf16[128,512]{1,0:T(8,128)(2,1)S(1)} %get-tuple-element.19), channel_id=1, source_target_pairs={{0,256},{128,384},{256,0},{384,128},{1,257},{129,385},{257,1},{385... | collective-permute-start | bytes 393224 | tf_op jit(solution)/shard_map/ppermute | solution.py:420
  85.4 7.2 %collective-permute-start.4 = (bf16[128,512]{1,0:T(8,128)(2,1)S(1)}, bf16[128,512]{1,0:T(8,128)(2,1)S(1)}, u32[]{:S(2)}, u32[]{:S(2)}) collective-permute-start(bf16[128,512]{1,0:T(8,128)(2,1)S(1)} %get-tuple-element.20), channel_id=1, source_target_pairs={{0,384},{128,0},{256,128},{384,256},{1,385},{129,1},{257,129},{385... | collective-permute-start | bytes 393224 | tf_op jit(solution)/shard_map/ppermute | solution.py:420
